TPU v7x, 256 devices: a whole 4x4x8 slice. The times are simulated.
256 devices in a mesh: depth: 8 (over y, core), lat: 32 (over z, x).
Axes of the slice: x: 4, y: 4, z: 8, core: 2. Of those that a mesh axis runs over, the one named last changes fastest.
Arguments:
- field: float32 [8, 1, 2, 1024, 1024], P('depth', None, None, 'lat'), may hold values from -6 to 6
- fresh: float32 [1, 2, 1024, 1024], P(None, None, 'lat'), may hold values from -6 to 6
- freq_index: int32 [8, 1], P('depth'), may hold values from 0 to 219
- ref_slowness: float32 [8], P('depth'), may hold values from 0.22 to 0.67
- slowness: float32 [8, 1024, 1024], P('depth', 'lat'), may hold values from 0.22 to 0.67
- tile_classes: int32 [8, 32, 32], P('depth', 'lat'), may hold values from 0 to 15
- fd_blocks: float32 [16, 2, 32, 32], replicated, as said below
- fd_coupling: float32 [16, 2], replicated, may hold values from 0.1 to 0.6
- image: float32 [8, 1024, 1024], P('depth', 'lat'), may hold values from -6 to 6
Outputs:
- next_field: float32 [8, 1, 2, 1024, 1024], P('depth', None, None, 'lat')
- new_image: float32 [8, 1024, 1024], P('depth', 'lat')
Inputs may be any that keep to these rules, and one draw needn't show every extreme that they name: `fd_blocks`: real and imaginary parts of one complex matrix of order 32 for each of the 16 velocity classes.
All inputs are finite; a program needn't handle non-finite values.
Results may differ from a plain program's by a relative error of at most 0.0003.
Values sent between devices are 32-bit elements; how exact they have to be, the bound alone decides.
No kernel may reach another device: no remote copies, remote signals or barrier semaphores. Data moves between devices by JAX's collectives and lax.ppermute only.
A program may use at most 64 MiB of HBM per device.

v0:
```python
import math

import jax
import jax.numpy as jnp
import ml_dtypes
import numpy as np
from jax import lax
from jax.experimental import pallas as pl
from jax.experimental.pallas import tpu as pltpu
from jax.sharding import PartitionSpec as P

LOW_HZ = 5.0
STEP_HZ = 0.25
DEPTH_KM = 0.01
SPACING_KM = 0.025
N = 1024
LAT = 32
NORM = 1.0 / (N * N)
INTERPRET = False


def parts(values):
    high = values.astype(ml_dtypes.bfloat16)
    low = (values - high.astype(np.float64)).astype(ml_dtypes.bfloat16)
    return np.stack([high, low])


def rotation(angle):
    cos, sin = np.cos(angle), np.sin(angle)
    return np.stack([np.stack([cos, -sin]), np.stack([sin, cos])])


def tables():
    n2 = np.arange(128)
    small = np.arange(32)
    k2 = np.arange(128).reshape(32, 4)
    line = rotation(-2 * np.pi * (k2[:, :, None] * n2 % 128) / 128)
    w1 = line.transpose(2, 0, 3, 1, 4).reshape(256, 256)
    line = rotation(2 * np.pi * (k2[:, :, None] * n2 % 128) / 128)
    w3 = line.transpose(2, 1, 3, 0, 4).reshape(256, 256)
    grid = 2 * np.pi * (small[:, None] * small % 32) / 32
    eye4 = np.eye(4)
    a1 = np.einsum("dcqi,kl->dkqicl", rotation(-grid), eye4).reshape(256, 256)
    a2 = np.einsum("dciq,kl->idkclq", rotation(grid), eye4).reshape(256, 256)
    b1 = np.einsum("dcxp,kl->ckxdlp", rotation(-grid), eye4).reshape(256, 256)
    b2 = np.einsum("dcpx,kl->ckpdlx", rotation(grid), eye4).reshape(256, 256)
    ty = 2 * np.pi * np.arange(8)[:, None] * n2 / N
    tx = np.tile(2 * np.pi * small[:, None] * small / N, (1, 4))
    twist_y = np.stack([np.cos(ty), np.sin(ty)]).astype(np.float32)
    twist_x = np.stack([np.cos(tx), np.sin(tx)]).astype(np.float32)
    edge = np.zeros((8, 32, 16, 8))
    for k1 in range(8):
        edge[k1, 31, k1, 0] = 1
        edge[k1, 0, k1, 1] = 1
    edge = edge.reshape(256, 128).astype(ml_dtypes.bfloat16)
    own = (np.arange(128)[None, :] // 32 == np.arange(4)[:, None]).astype(np.float32)
    own = np.broadcast_to(own[:, None, :], (4, 32, 128)).astype(ml_dtypes.bfloat16)
    spread = np.tile(np.eye(32), (1, 4)).astype(ml_dtypes.bfloat16)
    return {
        "w1": parts(w1),
        "w3": parts(w3),
        "a1": parts(a1),
        "a2": parts(a2),
        "b1": parts(b1),
        "b2": parts(b2),
        "twist_y": twist_y,
        "twist_x": twist_x,
        "edge": edge,
        "own": own,
        "spread": spread,
    }


NN = (((1,), (0,)), ((), ()))
NT = (((1,), (1,)), ((), ()))


def split(values):
    high = values.astype(jnp.bfloat16)
    low = (values - high.astype(jnp.float32)).astype(jnp.bfloat16)
    return high, low


def product(left, right, dims=NN):
    dot = lambda a, b: lax.dot_general(a, b, dims, preferred_element_type=jnp.float32)
    return dot(left[0], right[0]) + (dot(left[1], right[0]) + dot(left[0], right[1]))


def cmul(a, b):
    return a[0] * b[0] - a[1] * b[1], a[0] * b[1] + a[1] * b[0]


def dft(values, sign):
    count = len(values)
    if count == 1:
        return values
    even, odd = dft(values[0::2], sign), dft(values[1::2], sign)
    first, second = [], []
    for k in range(count // 2):
        re, im = odd[k]
        if 4 * k == count:
            re, im = -sign * im, sign * re
        elif k:
            cos = math.cos(2 * math.pi * k / count)
            sin = sign * math.sin(2 * math.pi * k / count)
            if 8 * k == count:
                re, im = cos * (re - sign * im), cos * (im + sign * re)
            else:
                re, im = cmul(odd[k], (cos, sin))
        first.append((even[k][0] + re, even[k][1] + im))
        second.append((even[k][0] - re, even[k][1] - im))
    return first + second


def call(body, outs, scratch, args, spaces, flops=0):
    size = sum(math.prod(o.shape) * o.dtype.itemsize for o in outs)
    size += sum(math.prod(a.shape) * a.dtype.itemsize for a in args)
    in_specs = [
        pl.BlockSpec(memory_space=pltpu.SMEM if i in spaces else pltpu.VMEM) for i in range(len(args))
    ]
    return pl.pallas_call(
        body,
        out_shape=outs,
        in_specs=in_specs,
        out_specs=[pl.BlockSpec(memory_space=pltpu.VMEM) for _ in outs],
        scratch_shapes=scratch,
        compiler_params=pltpu.CompilerParams(vmem_limit_bytes=24 << 20),
        cost_estimate=pl.CostEstimate(flops=flops, bytes_accessed=size, transcendentals=0),
        interpret=INTERPRET,
    )(*args)


def shape(*dims, dtype=jnp.float32):
    return jax.ShapeDtypeStruct(dims, dtype)


def forward_y(field_ref, w1_ref, twist_ref, out_ref, high_ref, low_ref):
    for top in range(0, 32, 16):
        rows = slice(top, top + 16)
        lines = [
            tuple(field_ref[c, rows, n1 * 128 : n1 * 128 + 128] for c in range(2)) for n1 in range(8)
        ]
        for k1, value in enumerate(dft(lines, -1)):
            if k1:
                cos, sin = twist_ref[0, k1 : k1 + 1], twist_ref[1, k1 : k1 + 1]
                value = cmul(value, (cos, -sin))
            at = slice(k1 * 32 + top, k1 * 32 + top + 16)
            for c in range(2):
                high, low = split(value[c])
                high_ref[at, c * 128 : c * 128 + 128] = high
                low_ref[at, c * 128 : c * 128 + 128] = low
    out = product((w1_ref[0], w1_ref[1]), (high_ref[...], low_ref[...]), NT)
    out_ref[...] = out.reshape(32, 8, 256)


def sincos(angle):
    return jnp.cos(angle), jnp.sin(angle)


def phases(freq_ref, slow_ref, lat_ref, out_ref):
    omega = 2.0 * math.pi * (LOW_HZ + STEP_HZ * freq_ref[0].astype(jnp.float32))
    reach = omega * slow_ref[0]
    scale = 2.0 * math.pi / (N * SPACING_KM)
    for block in range(8):
        h, k2l = block // 4, block % 4
        q = lax.broadcasted_iota(jnp.int32, (32, 128), 0)
        lane = lax.broadcasted_iota(jnp.int32, (32, 128), 1)
        kx = q + 32 * (lane % 32)
        ky = h * 4 + lane // 32 + 8 * (4 * lat_ref[0] + k2l)
        kx = jnp.where(kx < N // 2, kx, kx - N).astype(jnp.float32) * scale
        ky = jnp.where(ky < N // 2, ky, ky - N).astype(jnp.float32) * scale
        square = reach * reach - kx * kx - ky * ky
        root = jnp.sqrt(jnp.abs(square))
        angle = jnp.where(square > 0, root * DEPTH_KM, 0.0)
        amplitude = jnp.where(square > 0, 1.0, jnp.exp(-root * DEPTH_KM))
        cos, sin = sincos(angle)
        out_ref[0, block * 32 : block * 32 + 32] = amplitude * cos
        out_ref[1, block * 32 : block * 32 + 32] = amplitude * sin


def along_x(in_ref, phase_ref, a1_ref, b1_ref, b2_ref, a2_ref, twist_ref, edge_ref, out_ref, high_ref, low_ref):
    lines = in_ref[...].reshape(256, 256)
    mixed = product((a1_ref[0], a1_ref[1]), split(lines))
    cos, sin = twist_ref[0], twist_ref[1]

    def put(at, value):
        for c in range(2):
            high, low = split(value[c])
            high_ref[at, c * 128 : c * 128 + 128] = high
            low_ref[at, c * 128 : c * 128 + 128] = low

    for h in range(2):
        lanes = slice(h * 128, h * 128 + 128)
        for k2l in range(4):
            value = (mixed[k2l * 32 : k2l * 32 + 32, lanes], mixed[128 + k2l * 32 : 160 + k2l * 32, lanes])
            top = (h * 4 + k2l) * 32
            put(slice(top, top + 32), cmul(value, (cos, -sin)))
    spectrum = product((high_ref[...], low_ref[...]), (b1_ref[0], b1_ref[1]))
    for block in range(8):
        rows = slice(block * 32, block * 32 + 32)
        value = (spectrum[rows, :128], spectrum[rows, 128:])
        put(rows, cmul(value, (phase_ref[0, rows], phase_ref[1, rows])))
    mixed = product((high_ref[...], low_ref[...]), (b2_ref[0], b2_ref[1]))
    for h in range(2):
        for k2l in range(4):
            rows = slice((h * 4 + k2l) * 32, (h * 4 + k2l) * 32 + 32)
            value = cmul((mixed[rows, :128], mixed[rows, 128:]), (cos, sin))
            for c in range(2):
                high, low = split(value[c])
                at = slice(c * 128 + k2l * 32, c * 128 + k2l * 32 + 32)
                high_ref[at, h * 128 : h * 128 + 128] = high
                low_ref[at, h * 128 : h * 128 + 128] = low
    out = product((a2_ref[0], a2_ref[1]), (high_ref[...], low_ref[...]))
    high, low = split(out)
    dot = lambda a: lax.dot_general(a, edge_ref[...], NN, preferred_element_type=jnp.float32)
    edge = (dot(high) + dot(low)).reshape(32, 8, 128)
    out_ref[:, :, :256] = out.reshape(32, 8, 256)
    side = lax.broadcasted_iota(jnp.int32, (32, 8, 128), 2) % 8
    zero = jnp.zeros((1, 8, 128), jnp.float32)
    before = jnp.concatenate([zero, edge[:-1]], axis=0)
    after = jnp.concatenate([edge[1:], zero], axis=0)
    out_ref[:, :, 256:] = jnp.where(side == 0, before, after)


def weights(
    freq_ref, refslow_ref, class_ref, coupling_ref, slow_ref, up_ref, down_ref, blocks_ref, own_ref, spread_ref,
    lens_ref, beta_ref, mx_ref, my_ref, wide_ref,
):
    omega = 2.0 * math.pi * (LOW_HZ + STEP_HZ * freq_ref[0].astype(jnp.float32))
    base = refslow_ref[0]

    def lens(values):
        cos, sin = sincos(omega * (values - base) * DEPTH_KM)
        return cos * NORM, sin * NORM

    for top in range(0, 32, 8):
        lens_ref[0, top : top + 8], lens_ref[1, top : top + 8] = lens(slow_ref[top : top + 8])
    row = lax.broadcasted_iota(jnp.int32, (8, N), 0)
    sides = jnp.where(row == 0, up_ref[...], down_ref[...])
    lens_ref[0, 32:40], lens_ref[1, 32:40] = lens(sides)
    high, low = split(blocks_ref[...])
    dot = lambda a: lax.dot_general(a, spread_ref[...], NN, preferred_element_type=jnp.float32)
    wide_ref[0] = dot(high).astype(jnp.bfloat16).reshape(16, 64, 128)
    wide_ref[1] = dot(low).astype(jnp.bfloat16).reshape(16, 64, 128)
    lane = lax.broadcasted_iota(jnp.int32, (8, 128), 1) // 32
    for g in range(8):
        classes = [class_ref[g * 4 + t] for t in range(4)]
        for c in range(2):
            beta = jnp.full((8, 128), coupling_ref[classes[0] * 2 + c])
            for t in range(1, 4):
                beta = jnp.where(lane == t, coupling_ref[classes[t] * 2 + c], beta)
            beta_ref[c, :, g * 128 : g * 128 + 128] = beta
        for part in range(2):
            total = [None, None]
            for t in range(4):
                for c in range(2):
                    tile = wide_ref[part, classes[t], c * 32 : c * 32 + 32] * own_ref[t]
                    total[c] = tile if t == 0 else total[c] + tile
                    if c == 0:
                        my_ref[part, g, t * 32 : t * 32 + 32, :128] = tile
                        my_ref[part, g, 128 + t * 32 : 160 + t * 32, 128:] = tile
                    else:
                        my_ref[part, g, 128 + t * 32 : 160 + t * 32, :128] = tile
                        my_ref[part, g, t * 32 : t * 32 + 32, 128:] = -tile
            mx_ref[part, g, :32, :128] = total[0]
            mx_ref[part, g, :32, 128:] = -total[1]
            mx_ref[part, g, 32:, :128] = total[1]
            mx_ref[part, g, 32:, 128:] = total[0]


def finish(
    in_ref, w3_ref, twist_ref, lens_ref, beta_ref, mx_ref, my_ref, own_ref, image_ref,
    out_ref, image_out_ref, mixed_ref, lensed_ref, rhs_ref, across_ref,
):
    turned = in_ref[...].reshape(256, 384)[:, :384].T
    mixed_ref[...] = product(split(turned[:320]), (w3_ref[0], w3_ref[1]))
    for block in range(5):
        values = []
        for k1 in range(8):
            top = k1 * 32 + block * 8 if block < 4 else 256 + k1 * 8
            value = (mixed_ref[top : top + 8, :128], mixed_ref[top : top + 8, 128:])
            if k1:
                value = cmul(value, (twist_ref[0, k1 : k1 + 1], twist_ref[1, k1 : k1 + 1]))
            values.append(value)
        for n1, value in enumerate(dft(values, 1)):
            lanes = slice(n1 * 128, n1 * 128 + 128)
            rows = slice(block * 8, block * 8 + 8)
            value = cmul(value, (lens_ref[0, rows, lanes], lens_ref[1, rows, lanes]))
            for c in range(2):
                if block < 4:
                    lensed_ref[c, 8 + block * 8 : 16 + block * 8, lanes] = value[c]
                else:
                    lensed_ref[c, 7:8, lanes] = value[c][0:1]
                    lensed_ref[c, 40:41, lanes] = value[c][1:2]
    for g in range(8):
        lanes = slice(g * 128, g * 128 + 128)
        beta = (beta_ref[0, 0:1, lanes], beta_ref[1, 0:1, lanes])
        mid = [lensed_ref[c, 8:40, lanes] for c in range(2)]
        diff = tuple(
            lensed_ref[c, 9:41, lanes] + lensed_ref[c, 7:39, lanes] - 2.0 * mid[c] for c in range(2)
        )
        more = cmul(diff, beta)
        pieces = [split(mid[c] + more[c]) for c in range(2)]
        rhs = [
            jnp.concatenate([pieces[c][part] * own_ref[t] for c in range(2) for t in range(4)], axis=0)
            for part in range(2)
        ]
        out = product((mx_ref[0, g], mx_ref[1, g]), rhs)
        across_ref[0, :, lanes] = out[:32]
        across_ref[1, :, lanes] = out[32:]
    lane = lax.broadcasted_iota(jnp.int32, (32, N), 1)
    diff = []
    for c in range(2):
        whole = across_ref[c]
        after = jnp.where(lane == N - 1, 0.0, pltpu.roll(whole, N - 1, 1))
        before = jnp.where(lane == 0, 0.0, pltpu.roll(whole, 1, 1))
        diff.append(after + before - 2.0 * whole)
    more = cmul(diff, (beta_ref[0, 0:1], beta_ref[1, 0:1]))
    for c in range(2):
        rhs_ref[c] = across_ref[c] + more[c]
    for g in range(8):
        lanes = slice(g * 128, g * 128 + 128)
        rhs = jnp.concatenate([rhs_ref[0, :, lanes], rhs_ref[1, :, lanes]], axis=1)
        out = product(split(rhs), (my_ref[0, g], my_ref[1, g]), NT)
        out_ref[0, :, lanes] = out[:, :128]
        out_ref[1, :, lanes] = out[:, 128:]
        image_out_ref[:, lanes] = image_ref[:, lanes] + out[:, :128]


def spread_y(field, t):
    scratch = [pltpu.VMEM((256, 256), jnp.bfloat16)] * 2
    return call(forward_y, [shape(32, 8, 256)], scratch, [field, t["w1"], t["twist_y"]], ())[0]


def phase_tables(freq, refslow, lat):
    return call(phases, [shape(2, 256, 128)], [], [freq, refslow, lat], (0, 1, 2))[0]


def continue_x(block, phase, t):
    scratch = [pltpu.VMEM((256, 256), jnp.bfloat16)] * 2
    args = [block, phase, t["a1"], t["b1"], t["b2"], t["a2"], t["twist_x"], t["edge"]]
    return call(along_x, [shape(32, 8, 384)], scratch, args, ())[0]


def correction_tables(freq, refslow, classes, coupling, slow, up, down, blocks, t):
    half = jnp.bfloat16
    outs = [shape(2, 40, N), shape(2, 8, N), shape(2, 8, 64, 256, dtype=half), shape(2, 8, 256, 256, dtype=half)]
    scratch = [pltpu.VMEM((2, 16, 64, 128), half)]
    args = [freq, refslow, classes, coupling, slow, up, down, blocks, t["own"], t["spread"]]
    return call(weights, outs, scratch, args, (0, 1, 2, 3))


def correct(block, tabs, image, t):
    lens, beta, mx, my = tabs
    scratch = [
        pltpu.VMEM((320, 256), jnp.float32),
        pltpu.VMEM((2, 48, N), jnp.float32),
        pltpu.VMEM((2, 32, N), jnp.float32),
        pltpu.VMEM((2, 32, N), jnp.float32),
    ]
    args = [block, t["w3"], t["twist_y"], lens, beta, mx, my, t["own"], image]
    return call(finish, [shape(2, 32, N), shape(32, N)], scratch, args, ())


def exchange(block):
    return lax.all_to_all(block, "lat", split_axis=0, concat_axis=0, tiled=True)


def after(value, *others):
    return lax.optimization_barrier((value, others))


def per_device(
    field, fresh, freq_index, ref_slowness, slowness, tile_classes, fd_blocks, fd_coupling, image
):
    t = tables()
    block = spread_y(field.reshape(2, 32, N), t)
    block, (freq, refslow, slow) = after(block, freq_index.reshape(1), ref_slowness, slowness[0])
    received = exchange(block)
    lat = lax.axis_index("lat").reshape(1).astype(jnp.int32)
    phase = phase_tables(freq, refslow, lat)
    down = lax.ppermute(slow[:1], "lat", [(i + 1, i) for i in range(LAT - 1)])
    up = lax.ppermute(slow[-1:], "lat", [(i, i + 1) for i in range(LAT - 1)])
    block = continue_x(received, phase, t)
    block, (freq, classes, up, down) = after(block, freq, tile_classes.reshape(32), up, down)
    received = exchange(block)
    tabs = correction_tables(
        freq, refslow, classes, fd_coupling.reshape(32), slow, up, down, fd_blocks.reshape(1024, 32), t
    )
    result, new_image = correct(received, tabs, image[0], t)
    count = lax.axis_size("depth")
    moved = lax.ppermute(result, "depth", [(i, i + 1) for i in range(count - 1)])
    first_section = lax.axis_index("depth") == 0
    next_field = jnp.where(first_section, fresh[0], moved)[None, None]
    return next_field, new_image[None]


def solution(mesh):
    return jax.shard_map(
        per_device,
        mesh=mesh,
        in_specs=(
            P("depth", None, None, "lat", None),
            P(None, None, "lat", None),
            P("depth", None),
            P("depth"),
            P("depth", "lat", None),
            P("depth", "lat", None),
            P(),
            P(),
            P("depth", "lat", None),
        ),
        out_specs=(P("depth", None, None, "lat", None), P("depth", "lat", None)),
        check_vma=False,
    )
```

profile of v0, /device:TPU:1, one launch (start us, length us, event | category | flops | bytes accessed | tf_op | source)
XLA Modules:
  0.0 72.9 jit_solution(16614830634013852888)
XLA Ops:
  0.6 0.0 copy-start
  0.6 0.9 %copy-done = bf16[2,256,256]{2,1,0:T(8,128)(2,1)S(1)} copy-done((bf16[2,256,256]{2,1,0:T(8,128)(2,1)S(1)}, bf16[2,256,256]{2,1,0:T(8,128)(2,1)}, u32[]{:S(2)}) %copy-start) | copy-done | bytes 262168
  1.6 0.9 %copy-done.7 = f32[1,1,2,32,1024]{4,3,2,1,0:T(8,128)S(1)} copy-done((f32[1,1,2,32,1024]{4,3,2,1,0:T(8,128)S(1)}, f32[1,1,2,32,1024]{4,3,2,1,0:T(8,128)}, u32[]{:S(2)}) %copy-start.7) | copy-done | bytes 262168
  2.5 0.7 copy-done.17
  3.3 1.1 %shard_map.203 = f32[32,8,256]{2,1,0:T(8,128)} custom-call(f32[2,32,1024]{2,1,0:T(8,128)S(1)} %bitcast.17, bf16[2,256,256]{2,1,0:T(8,128)(2,1)S(1)} %copy-done, f32[2,8,128]{2,1,0:T(8,128)S(1)} %copy-done.17), custom_call_target="tpu_custom_call" | custom-call | bytes 794624 | tf_op jit(solution)/shard_map/pallas_call | solution.py:121
  4.4 12.0 %all-to-all-start = ((f32[32,8,256]{2,1,0:T(8,128)}), f32[32,8,256]{2,1,0:T(8,128)S(1)}, u32[]{:S(2)}, u32[]{:S(2)}) async-start(f32[32,8,256]{2,1,0:T(8,128)} %shard_map.203), calls=%async_computation | async-start | bytes 524288 | tf_op jit(solution)/shard_map/all_to_all | solution.py:366
  16.4 0.8 %fusion.1 = (f32[1,1024]{1,0:T(1,128)S(1)}, f32[1,1024]{1,0:T(1,128)S(1)}) fusion(f32[32,1024]{1,0:T(8,128)} %bitcast.18), kind=kLoop, calls=%fused_computation.2 | loop fusion | bytes 16384 | tf_op jit(solution)/shard_map/slice | solution.py:382
  17.1 1.3 %collective-permute-start.1 = (f32[1,1024]{1,0:T(1,128)S(1)}, f32[1,1024]{1,0:T(1,128)S(1)}, u32[]{:S(2)}, u32[]{:S(2)}) collective-permute-start(f32[1,1024]{1,0:T(1,128)S(1)} %get-tuple-element.32), channel_id=1, source_target_pairs={{1,0},{2,1},{3,2},{4,3},{5,4},{6,5},{7,6},{8,7},{9,8},{10,9},{11,1... | collective-permute-start | bytes 12296 | tf_op jit(solution)/shard_map/ppermute | solution.py:382
  18.4 4.0 %collective-permute-start = (f32[1,1024]{1,0:T(1,128)S(1)}, f32[1,1024]{1,0:T(1,128)S(1)}, u32[]{:S(2)}, u32[]{:S(2)}) collective-permute-start(f32[1,1024]{1,0:T(1,128)S(1)} %get-tuple-element.33), channel_id=1, source_target_pairs={{0,1},{1,2},{2,3},{3,4},{4,5},{5,6},{6,7},{7,8},{8,9},{9,10},{10,1... | collective-permute-start | bytes 12296 | tf_op jit(solution)/shard_map/ppermute | solution.py:383
  23.7 0.6 shard_map.204.phase_ref
  24.3 3.2 %all-to-all-done.in_ref = f32[32,8,256]{2,1,0:T(8,128)S(1)} async-done(((f32[32,8,256]{2,1,0:T(8,128)}), f32[32,8,256]{2,1,0:T(8,128)S(1)}, u32[]{:S(2)}, u32[]{:S(2)}) %all-to-all-start) | async-done | bytes 262176 | tf_op jit(solution)/shard_map/all_to_all | solution.py:366
  27.5 0.9 %copy-done.8 = bf16[2,256,256]{2,1,0:T(8,128)(2,1)S(1)} copy-done((bf16[2,256,256]{2,1,0:T(8,128)(2,1)S(1)}, bf16[2,256,256]{2,1,0:T(8,128)(2,1)}, u32[]{:S(2)}) %copy-start.8) | copy-done | bytes 262168
  28.5 0.9 %copy-done.9 = bf16[2,256,256]{2,1,0:T(8,128)(2,1)S(1)} copy-done((bf16[2,256,256]{2,1,0:T(8,128)(2,1)S(1)}, bf16[2,256,256]{2,1,0:T(8,128)(2,1)}, u32[]{:S(2)}) %copy-start.9) | copy-done | bytes 262168
  29.4 0.9 %copy-done.10 = bf16[2,256,256]{2,1,0:T(8,128)(2,1)S(1)} copy-done((bf16[2,256,256]{2,1,0:T(8,128)(2,1)S(1)}, bf16[2,256,256]{2,1,0:T(8,128)(2,1)}, u32[]{:S(2)}) %copy-start.10) | copy-done | bytes 262168
  30.4 0.9 %copy-done.11 = bf16[2,256,256]{2,1,0:T(8,128)(2,1)S(1)} copy-done((bf16[2,256,256]{2,1,0:T(8,128)(2,1)S(1)}, bf16[2,256,256]{2,1,0:T(8,128)(2,1)}, u32[]{:S(2)}) %copy-start.11) | copy-done | bytes 262168
  31.4 0.8 %copy-done.15 = bf16[256,128]{1,0:T(8,128)(2,1)S(1)} copy-done((bf16[256,128]{1,0:T(8,128)(2,1)S(1)}, bf16[256,128]{1,0:T(8,128)(2,1)}, u32[]{:S(2)}) %copy-start.15) | copy-done | bytes 65560
  32.2 0.8 %copy-done.16 = f32[2,32,128]{2,1,0:T(8,128)S(1)} copy-done((f32[2,32,128]{2,1,0:T(8,128)S(1)}, f32[2,32,128]{2,1,0:T(8,128)}, u32[]{:S(2)}) %copy-start.16) | copy-done | bytes 32792
  32.9 2.2 %shard_map.205 = f32[32,8,384]{2,1,0:T(8,128)} custom-call(f32[32,8,256]{2,1,0:T(8,128)S(1)} %all-to-all-done.in_ref, f32[2,256,128]{2,1,0:T(8,128)S(1)} %shard_map.204.phase_ref, bf16[2,256,256]{2,1,0:T(8,128)(2,1)S(1)} %copy-done.11, bf16[2,256,256]{2,1,0:T(8,128)(2,1)S(1)} %copy-done.10, bf16[2,256,256]{2,1,0:T(8,128)(2,1)S(1)} %copy-done.9, ...), custom_call_target="tpu_custom_call" | custom-call | bytes 2064384 | tf_op jit(solution)/shard_map/pallas_call | solution.py:121
  35.2 7.8 %all-to-all-start.1 = ((f32[32,8,384]{2,1,0:T(8,128)}), f32[32,8,384]{2,1,0:T(8,128)S(1)}, u32[]{:S(2)}, u32[]{:S(2)}) async-start(f32[32,8,384]{2,1,0:T(8,128)} %shard_map.205), calls=%async_computation.1 | async-start | bytes 786432 | tf_op jit(solution)/shard_map/all_to_all | solution.py:366
  43.0 0.1 copy.23
  43.1 0.1 reshape.26.coupling_ref
  43.2 1.8 %shard_map.206 = (f32[2,40,1024]{2,1,0:T(8,128)S(1)}, f32[2,8,1024]{2,1,0:T(8,128)S(1)}, bf16[2,8,64,256]{3,2,1,0:T(8,128)(2,1)S(1)}, bf16[2,8,256,256]{3,2,1,0:T(8,128)(2,1)S(1)}) custom-call(s32[1]{0:T(128)} %bitcast.15.freq_ref, f32[1]{0:T(128)S(6)} %copy.25.slow_ref.refslow_ref, s32[32]{0:T(128)S(1)} %bitcast.21, f32[32]{0:T(128)S(1)} %reshape.26.coupling_ref, ...), custom_call_target="tpu_custom_call" | custom-call | bytes 3326216 | tf_op jit(solution)/shard_map/pallas_call | solution.py:121
  45.1 0.8 %copy-done.3 = bf16[2,8,64,256]{3,2,1,0:T(8,128)(2,1)} copy-done((bf16[2,8,64,256]{3,2,1,0:T(8,128)(2,1)}, bf16[2,8,64,256]{3,2,1,0:T(8,128)(2,1)S(1)}, u32[]{:S(2)}) %copy-start.3) | copy-done | bytes 524312
  45.9 0.7 copy-done.5
  46.6 8.9 %all-to-all-done.1.in_ref = f32[32,8,384]{2,1,0:T(8,128)S(1)} async-done(((f32[32,8,384]{2,1,0:T(8,128)}), f32[32,8,384]{2,1,0:T(8,128)S(1)}, u32[]{:S(2)}, u32[]{:S(2)}) %all-to-all-start.1) | async-done | bytes 393248 | tf_op jit(solution)/shard_map/all_to_all | solution.py:366
  55.5 1.0 %copy-done.4 = bf16[2,8,64,256]{3,2,1,0:T(8,128)(2,1)S(1)} copy-done((bf16[2,8,64,256]{3,2,1,0:T(8,128)(2,1)S(1)}, bf16[2,8,64,256]{3,2,1,0:T(8,128)(2,1)}, u32[]{:S(2)}) %copy-start.4) | copy-done | bytes 524312
  56.6 1.0 %copy-done.6 = f32[2,40,1024]{2,1,0:T(8,128)S(1)} copy-done((f32[2,40,1024]{2,1,0:T(8,128)S(1)}, f32[2,40,1024]{2,1,0:T(8,128)}, u32[]{:S(2)}) %copy-start.6) | copy-done | bytes 327704
  57.5 0.9 %copy-done.14 = f32[1,32,1024]{2,1,0:T(8,128)S(1)} copy-done((f32[1,32,1024]{2,1,0:T(8,128)S(1)}, f32[1,32,1024]{2,1,0:T(8,128)}, u32[]{:S(2)}) %copy-start.14) | copy-done | bytes 131096
  58.4 2.7 %shard_map.207 = (f32[2,32,1024]{2,1,0:T(8,128)S(1)}, f32[32,1024]{1,0:T(8,128)}) custom-call(f32[32,8,384]{2,1,0:T(8,128)S(1)} %all-to-all-done.1.in_ref, bf16[2,256,256]{2,1,0:T(8,128)(2,1)S(1)} %copy-done.1, f32[2,8,128]{2,1,0:T(8,128)S(1)} %copy-done.18, f32[2,40,1024]{2,1,0:T(8,128)S(1)} %copy-done.6, f32[2,8,1024]{2,1,0:T(8,128)S(1)} %get-tuple-element.27.beta_ref, ...), custom_call_target="tpu_custom_call" | custom-call | bytes 4235264 | tf_op jit(solution)/shard_map/pallas_call | solution.py:121
  61.2 6.8 %collective-permute-start.2 = (f32[2,32,1024]{2,1,0:T(8,128)S(1)}, f32[2,32,1024]{2,1,0:T(8,128)S(1)}, u32[]{:S(2)}, u32[]{:S(2)}) collective-permute-start(f32[2,32,1024]{2,1,0:T(8,128)S(1)} %get-tuple-element.30), channel_id=1, source_target_pairs={{0,32},{32,64},{64,96},{96,128},{128,160},{160,192},{192,224},{1,3... | collective-permute-start | bytes 786440 | tf_op jit(solution)/shard_map/ppermute | solution.py:392
  68.0 3.3 %collective-permute-done.2 = f32[2,32,1024]{2,1,0:T(8,128)S(1)} collective-permute-done((f32[2,32,1024]{2,1,0:T(8,128)S(1)}, f32[2,32,1024]{2,1,0:T(8,128)S(1)}, u32[]{:S(2)}, u32[]{:S(2)}) %collective-permute-start.2) | collective-permute-done | bytes 262176 | tf_op jit(solution)/shard_map/ppermute | solution.py:392
  71.3 1.7 %fusion = f32[1,1,2,32,1024]{4,3,2,1,0:T(8,128)} fusion(f32[2,32,1024]{2,1,0:T(8,128)S(1)} %collective-permute-done.2, f32[1,2,32,1024]{3,2,1,0:T(8,128)} %param.21, pred[]{:T(512)S(6)} %eq.3), kind=kLoop, calls=%fused_computation.1 | loop fusion | flops 65536 | bytes 786433 | tf_op jit(solution)/shard_map/broadcast_in_dim | solution.py:394
  (31 shorter events, 0.1 us)
Async XLA Ops:
  0.6 1.0 %copy-start = (bf16[2,256,256]{2,1,0:T(8,128)(2,1)S(1)}, bf16[2,256,256]{2,1,0:T(8,128)(2,1)}, u32[]{:S(2)}) copy-start(bf16[2,256,256]{2,1,0:T(8,128)(2,1)} %constant.31.clone.w1_ref.w3_ref) | copy-start | bytes 786436
  1.6 0.9 %copy-start.7 = (f32[1,1,2,32,1024]{4,3,2,1,0:T(8,128)S(1)}, f32[1,1,2,32,1024]{4,3,2,1,0:T(8,128)}, u32[]{:S(2)}) copy-start(f32[1,1,2,32,1024]{4,3,2,1,0:T(8,128)} %param.20) | copy-start | bytes 786436
  2.5 0.7 copy-start.17
  3.2 39.8 %copy-start.21 = (f32[16,2]{0,1:T(2,128)S(1)}, f32[16,2]{0,1:T(2,128)}, u32[]{:S(2)}) copy-start(f32[16,2]{0,1:T(2,128)} %param.27) | copy-start | bytes 388
  3.2 39.9 %copy-start.2 = (f32[16,2,32,32]{3,2,1,0:T(8,128)S(1)}, f32[16,2,32,32]{3,2,1,0:T(8,128)}, u32[]{:S(2)}) copy-start(f32[16,2,32,32]{3,2,1,0:T(8,128)} %param.26) | copy-start | bytes 393220
  3.2 40.0 %copy-start.12 = (f32[1,32,1024]{2,1,0:T(8,128)S(1)}, f32[1,32,1024]{2,1,0:T(8,128)}, u32[]{:S(2)}) copy-start(f32[1,32,1024]{2,1,0:T(8,128)} %param.24) | copy-start | bytes 393220
  3.2 40.0 %copy-start.13 = (bf16[4,32,128]{2,1,0:T(8,128)(2,1)S(1)}, bf16[4,32,128]{2,1,0:T(8,128)(2,1)}, u32[]{:S(2)}) copy-start(bf16[4,32,128]{2,1,0:T(8,128)(2,1)} %constant.39.clone.own_ref) | copy-start | bytes 98308
  3.2 40.0 %copy-start.19 = (bf16[32,128]{1,0:T(8,128)(2,1)S(1)}, bf16[32,128]{1,0:T(8,128)(2,1)}, u32[]{:S(2)}) copy-start(bf16[32,128]{1,0:T(8,128)(2,1)} %constant.40.clone.spread_ref) | copy-start | bytes 24580
  3.3 40.0 %copy-start.20 = (s32[1,1,32]{2,1,0:T(1,128)S(1)}, s32[1,1,32]{2,1,0:T(1,128)}, u32[]{:S(2)}) copy-start(s32[1,1,32]{2,1,0:T(1,128)} %param.25) | copy-start | bytes 388
  4.3 51.2 %copy-start.1 = (bf16[2,256,256]{2,1,0:T(8,128)(2,1)S(1)}, bf16[2,256,256]{2,1,0:T(8,128)(2,1)}, u32[]{:S(2)}) copy-start(bf16[2,256,256]{2,1,0:T(8,128)(2,1)} %constant.31.clone.w1_ref.w3_ref) | copy-start | bytes 786436
  4.4 51.2 %copy-start.18 = (f32[2,8,128]{2,1,0:T(8,128)S(1)}, f32[2,8,128]{2,1,0:T(8,128)}, u32[]{:S(2)}) copy-start(f32[2,8,128]{2,1,0:T(8,128)} %constant.32.clone.twist_ref) | copy-start | bytes 24580
  4.4 23.2 %all-to-all-start = ((f32[32,8,256]{2,1,0:T(8,128)}), f32[32,8,256]{2,1,0:T(8,128)S(1)}, u32[]{:S(2)}, u32[]{:S(2)}) async-start(f32[32,8,256]{2,1,0:T(8,128)} %shard_map.203), calls=%async_computation | async-start | bytes 524288 | tf_op jit(solution)/shard_map/all_to_all | solution.py:366
  17.1 18.0 %collective-permute-start.1 = (f32[1,1024]{1,0:T(1,128)S(1)}, f32[1,1024]{1,0:T(1,128)S(1)}, u32[]{:S(2)}, u32[]{:S(2)}) collective-permute-start(f32[1,1024]{1,0:T(1,128)S(1)} %get-tuple-element.32), channel_id=1, source_target_pairs={{1,0},{2,1},{3,2},{4,3},{5,4},{6,5},{7,6},{8,7},{9,8},{10,9},{11,1... | collective-permute-start | bytes 12296 | tf_op jit(solution)/shard_map/ppermute | solution.py:382
  18.4 16.7 %collective-permute-start = (f32[1,1024]{1,0:T(1,128)S(1)}, f32[1,1024]{1,0:T(1,128)S(1)}, u32[]{:S(2)}, u32[]{:S(2)}) collective-permute-start(f32[1,1024]{1,0:T(1,128)S(1)} %get-tuple-element.33), channel_id=1, source_target_pairs={{0,1},{1,2},{2,3},{3,4},{4,5},{5,6},{6,7},{7,8},{8,9},{9,10},{10,1... | collective-permute-start | bytes 12296 | tf_op jit(solution)/shard_map/ppermute | solution.py:383
  27.5 1.0 %copy-start.8 = (bf16[2,256,256]{2,1,0:T(8,128)(2,1)S(1)}, bf16[2,256,256]{2,1,0:T(8,128)(2,1)}, u32[]{:S(2)}) copy-start(bf16[2,256,256]{2,1,0:T(8,128)(2,1)} %constant.36.clone.a2_ref) | copy-start | bytes 786436
  28.5 0.9 %copy-start.9 = (bf16[2,256,256]{2,1,0:T(8,128)(2,1)S(1)}, bf16[2,256,256]{2,1,0:T(8,128)(2,1)}, u32[]{:S(2)}) copy-start(bf16[2,256,256]{2,1,0:T(8,128)(2,1)} %constant.35.clone.b2_ref) | copy-start | bytes 786436
  29.4 0.9 %copy-start.10 = (bf16[2,256,256]{2,1,0:T(8,128)(2,1)S(1)}, bf16[2,256,256]{2,1,0:T(8,128)(2,1)}, u32[]{:S(2)}) copy-start(bf16[2,256,256]{2,1,0:T(8,128)(2,1)} %constant.34.clone.b1_ref) | copy-start | bytes 786436
  30.4 0.9 %copy-start.11 = (bf16[2,256,256]{2,1,0:T(8,128)(2,1)S(1)}, bf16[2,256,256]{2,1,0:T(8,128)(2,1)}, u32[]{:S(2)}) copy-start(bf16[2,256,256]{2,1,0:T(8,128)(2,1)} %constant.33.clone.a1_ref) | copy-start | bytes 786436
  31.3 0.8 %copy-start.15 = (bf16[256,128]{1,0:T(8,128)(2,1)S(1)}, bf16[256,128]{1,0:T(8,128)(2,1)}, u32[]{:S(2)}) copy-start(bf16[256,128]{1,0:T(8,128)(2,1)} %constant.38.clone.edge_ref) | copy-start | bytes 196612
  32.2 0.8 %copy-start.16 = (f32[2,32,128]{2,1,0:T(8,128)S(1)}, f32[2,32,128]{2,1,0:T(8,128)}, u32[]{:S(2)}) copy-start(f32[2,32,128]{2,1,0:T(8,128)} %constant.37.clone.twist_ref) | copy-start | bytes 98308
  35.2 20.3 %all-to-all-start.1 = ((f32[32,8,384]{2,1,0:T(8,128)}), f32[32,8,384]{2,1,0:T(8,128)S(1)}, u32[]{:S(2)}, u32[]{:S(2)}) async-start(f32[32,8,384]{2,1,0:T(8,128)} %shard_map.205), calls=%async_computation.1 | async-start | bytes 786432 | tf_op jit(solution)/shard_map/all_to_all | solution.py:366
  45.1 0.8 %copy-start.3 = (bf16[2,8,64,256]{3,2,1,0:T(8,128)(2,1)}, bf16[2,8,64,256]{3,2,1,0:T(8,128)(2,1)S(1)}, u32[]{:S(2)}) copy-start(bf16[2,8,64,256]{3,2,1,0:T(8,128)(2,1)S(1)} %get-tuple-element.28.mx_ref) | copy-start | bytes 1572868
  45.9 0.7 copy-start.5
  55.5 1.0 %copy-start.4 = (bf16[2,8,64,256]{3,2,1,0:T(8,128)(2,1)S(1)}, bf16[2,8,64,256]{3,2,1,0:T(8,128)(2,1)}, u32[]{:S(2)}) copy-start(bf16[2,8,64,256]{3,2,1,0:T(8,128)(2,1)} %copy-done.3) | copy-start | bytes 1572868
  56.5 1.0 %copy-start.6 = (f32[2,40,1024]{2,1,0:T(8,128)S(1)}, f32[2,40,1024]{2,1,0:T(8,128)}, u32[]{:S(2)}) copy-start(f32[2,40,1024]{2,1,0:T(8,128)} %copy-done.5) | copy-start | bytes 983044
  57.5 0.9 %copy-start.14 = (f32[1,32,1024]{2,1,0:T(8,128)S(1)}, f32[1,32,1024]{2,1,0:T(8,128)}, u32[]{:S(2)}) copy-start(f32[1,32,1024]{2,1,0:T(8,128)} %param.28) | copy-start | bytes 393220
  61.2 10.1 %collective-permute-start.2 = (f32[2,32,1024]{2,1,0:T(8,128)S(1)}, f32[2,32,1024]{2,1,0:T(8,128)S(1)}, u32[]{:S(2)}, u32[]{:S(2)}) collective-permute-start(f32[2,32,1024]{2,1,0:T(8,128)S(1)} %get-tuple-element.30), channel_id=1, source_target_pairs={{0,32},{32,64},{64,96},{96,128},{128,160},{160,192},{192,224},{1,3... | collective-permute-start | bytes 786440 | tf_op jit(solution)/shard_map/ppermute | solution.py:392
where the time goes:
time: 73.8 us; the launch traced here: 72.9 us
  starting transfers between devices  31.9 us (43%)
  waiting for transfers between devices  15.4 us (21%)
  local copies, waits for them, and re-layouts  13.4 us (18%)
  Pallas kernels  8.44 us (11%)
  between operations  2.09 us (3%)
  other arithmetic  1.68 us (2%)
    all_to_all x2, starting transfers between devices, exchange(): return lax.all_to_all(block, 'lat', split_axis=0, concat_axis=0, tiled=True)  19.8 us
    unnamed x45, local copies, waits for them, and re-layouts  12.6 us
    all_to_all x2, waiting for transfers between devices, exchange(): return lax.all_to_all(block, 'lat', split_axis=0, concat_axis=0, tiled=True)  12.1 us
    pallas_call x5, Pallas kernels, call(): pl.pallas_call(body, out_shape=outs, in_specs=in_specs, out_specs=[pl.Blo...  8.44 us
    ppermute x1, starting transfers between devices, per_device(): lax.ppermute(result, 'depth', [(i, i + 1) for i in range(count - 1)])  6.8 us
    ppermute x1, starting transfers between devices, per_device(): up = lax.ppermute(slow[-1:], 'lat', [(i, i + 1) for i in range(LAT - 1)])  3.99 us
    ppermute x1, waiting for transfers between devices, per_device(): lax.ppermute(result, 'depth', [(i, i + 1) for i in range(count - 1)])  3.29 us
    broadcast_in_dim x1, other arithmetic, per_device(): next_field = jnp.where(first_section, fresh[0], moved)[None, None]  1.68 us
  transfers between devices with their start and end apart: 5, of which 3 were waited for; matrix products, arithmetic and copies ran while one was open for 1% of the time, Pallas kernels for 6%

commit v1 on v0

--- a/solution.py
+++ b/solution.py
@@ -54,15 +54,12 @@
         edge[k1, 0, k1, 1] = 1
     edge = edge.reshape(256, 128).astype(ml_dtypes.bfloat16)
     own = (np.arange(128)[None, :] // 32 == np.arange(4)[:, None]).astype(np.float32)
-    own = np.broadcast_to(own[:, None, :], (4, 32, 128)).astype(ml_dtypes.bfloat16)
+    own = np.broadcast_to(np.tile(own, (1, 2))[:, None, :], (4, 32, 256)).astype(ml_dtypes.bfloat16)
     spread = np.tile(np.eye(32), (1, 4)).astype(ml_dtypes.bfloat16)
     return {
         "w1": parts(w1),
         "w3": parts(w3),
-        "a1": parts(a1),
-        "a2": parts(a2),
-        "b1": parts(b1),
-        "b2": parts(b2),
+        "x": np.stack([parts(a1), parts(b1), parts(b2), parts(a2)]),
         "twist_y": twist_y,
         "twist_x": twist_x,
         "edge": edge,
@@ -112,29 +109,38 @@
     return first + second
 
 
-def call(body, outs, scratch, args, spaces, flops=0):
+def call(body, outs, scratch, args, scalars=(), large=()):
     size = sum(math.prod(o.shape) * o.dtype.itemsize for o in outs)
     size += sum(math.prod(a.shape) * a.dtype.itemsize for a in args)
-    in_specs = [
-        pl.BlockSpec(memory_space=pltpu.SMEM if i in spaces else pltpu.VMEM) for i in range(len(args))
-    ]
+    args = [pltpu.with_memory_space_constraint(a, pltpu.HBM) if i in large else a for i, a in enumerate(args)]
+    space = lambda i: pltpu.SMEM if i in scalars else pltpu.HBM if i in large else pltpu.VMEM
     return pl.pallas_call(
         body,
         out_shape=outs,
-        in_specs=in_specs,
+        in_specs=[pl.BlockSpec(memory_space=space(i)) for i in range(len(args))],
         out_specs=[pl.BlockSpec(memory_space=pltpu.VMEM) for _ in outs],
         scratch_shapes=scratch,
         compiler_params=pltpu.CompilerParams(vmem_limit_bytes=24 << 20),
-        cost_estimate=pl.CostEstimate(flops=flops, bytes_accessed=size, transcendentals=0),
+        cost_estimate=pl.CostEstimate(flops=0, bytes_accessed=size, transcendentals=0),
         interpret=INTERPRET,
     )(*args)
 
 
+def fetch(sources, targets, sems):
+    copies = [pltpu.make_async_copy(a, b, sems.at[i]) for i, (a, b) in enumerate(zip(sources, targets, strict=True))]
+    for copy in copies:
+        copy.start()
+    return copies
+
+
 def shape(*dims, dtype=jnp.float32):
     return jax.ShapeDtypeStruct(dims, dtype)
 
 
-def forward_y(field_ref, w1_ref, twist_ref, out_ref, high_ref, low_ref):
+def forward_y(field_any, twist_any, w1_any, out_ref, field_ref, twist_ref, w1_ref, high_ref, low_ref, sems):
+    copies = fetch([field_any, twist_any, w1_any], [field_ref, twist_ref, w1_ref], sems)
+    copies[0].wait()
+    copies[1].wait()
     for top in range(0, 32, 16):
         rows = slice(top, top + 16)
         lines = [
@@ -149,6 +155,7 @@
                 high, low = split(value[c])
                 high_ref[at, c * 128 : c * 128 + 128] = high
                 low_ref[at, c * 128 : c * 128 + 128] = low
+    copies[2].wait()
     out = product((w1_ref[0], w1_ref[1]), (high_ref[...], low_ref[...]), NT)
     out_ref[...] = out.reshape(32, 8, 256)
 
@@ -157,7 +164,8 @@
     return jnp.cos(angle), jnp.sin(angle)
 
 
-def phases(freq_ref, slow_ref, lat_ref, out_ref):
+def phases(freq_ref, slow_ref, lat_ref, x_any, twist_any, edge_any, out_ref, x_ref, twist_ref, edge_ref, sems):
+    copies = fetch([x_any, twist_any, edge_any], [x_ref, twist_ref, edge_ref], sems)
     omega = 2.0 * math.pi * (LOW_HZ + STEP_HZ * freq_ref[0].astype(jnp.float32))
     reach = omega * slow_ref[0]
     scale = 2.0 * math.pi / (N * SPACING_KM)
@@ -176,11 +184,13 @@
         cos, sin = sincos(angle)
         out_ref[0, block * 32 : block * 32 + 32] = amplitude * cos
         out_ref[1, block * 32 : block * 32 + 32] = amplitude * sin
-
-
-def along_x(in_ref, phase_ref, a1_ref, b1_ref, b2_ref, a2_ref, twist_ref, edge_ref, out_ref, high_ref, low_ref):
+    for copy in copies:
+        copy.wait()
+
+
+def along_x(in_ref, phase_ref, x_ref, twist_ref, edge_ref, out_ref, high_ref, low_ref):
     lines = in_ref[...].reshape(256, 256)
-    mixed = product((a1_ref[0], a1_ref[1]), split(lines))
+    mixed = product((x_ref[0, 0], x_ref[0, 1]), split(lines))
     cos, sin = twist_ref[0], twist_ref[1]
 
     def put(at, value):
@@ -195,12 +205,12 @@
             value = (mixed[k2l * 32 : k2l * 32 + 32, lanes], mixed[128 + k2l * 32 : 160 + k2l * 32, lanes])
             top = (h * 4 + k2l) * 32
             put(slice(top, top + 32), cmul(value, (cos, -sin)))
-    spectrum = product((high_ref[...], low_ref[...]), (b1_ref[0], b1_ref[1]))
+    spectrum = product((high_ref[...], low_ref[...]), (x_ref[1, 0], x_ref[1, 1]))
     for block in range(8):
         rows = slice(block * 32, block * 32 + 32)
         value = (spectrum[rows, :128], spectrum[rows, 128:])
         put(rows, cmul(value, (phase_ref[0, rows], phase_ref[1, rows])))
-    mixed = product((high_ref[...], low_ref[...]), (b2_ref[0], b2_ref[1]))
+    mixed = product((high_ref[...], low_ref[...]), (x_ref[2, 0], x_ref[2, 1]))
     for h in range(2):
         for k2l in range(4):
             rows = slice((h * 4 + k2l) * 32, (h * 4 + k2l) * 32 + 32)
@@ -210,7 +220,7 @@
                 at = slice(c * 128 + k2l * 32, c * 128 + k2l * 32 + 32)
                 high_ref[at, h * 128 : h * 128 + 128] = high
                 low_ref[at, h * 128 : h * 128 + 128] = low
-    out = product((a2_ref[0], a2_ref[1]), (high_ref[...], low_ref[...]))
+    out = product((x_ref[3, 0], x_ref[3, 1]), (high_ref[...], low_ref[...]))
     high, low = split(out)
     dot = lambda a: lax.dot_general(a, edge_ref[...], NN, preferred_element_type=jnp.float32)
     edge = (dot(high) + dot(low)).reshape(32, 8, 128)
@@ -223,45 +233,35 @@
 
 
 def weights(
-    freq_ref, refslow_ref, class_ref, coupling_ref, slow_ref, up_ref, down_ref, blocks_ref, own_ref, spread_ref,
-    lens_ref, beta_ref, mx_ref, my_ref, wide_ref,
+    freq_ref, refslow_ref, class_ref, coupling_ref, last_ref, slow_ref, blocks_ref, own_ref, spread_ref,
+    lens_ref, row_ref, mx_ref, wide_ref,
 ):
     omega = 2.0 * math.pi * (LOW_HZ + STEP_HZ * freq_ref[0].astype(jnp.float32))
     base = refslow_ref[0]
-
-    def lens(values):
-        cos, sin = sincos(omega * (values - base) * DEPTH_KM)
-        return cos * NORM, sin * NORM
-
     for top in range(0, 32, 8):
-        lens_ref[0, top : top + 8], lens_ref[1, top : top + 8] = lens(slow_ref[top : top + 8])
-    row = lax.broadcasted_iota(jnp.int32, (8, N), 0)
-    sides = jnp.where(row == 0, up_ref[...], down_ref[...])
-    lens_ref[0, 32:40], lens_ref[1, 32:40] = lens(sides)
+        rows = slice(top, top + 8)
+        cos, sin = sincos(omega * (slow_ref[rows] - base) * DEPTH_KM)
+        lens_ref[0, rows], lens_ref[1, rows] = cos * NORM, sin * NORM
     high, low = split(blocks_ref[...])
     dot = lambda a: lax.dot_general(a, spread_ref[...], NN, preferred_element_type=jnp.float32)
     wide_ref[0] = dot(high).astype(jnp.bfloat16).reshape(16, 64, 128)
     wide_ref[1] = dot(low).astype(jnp.bfloat16).reshape(16, 64, 128)
-    lane = lax.broadcasted_iota(jnp.int32, (8, 128), 1) // 32
+    row_ref[2:3] = jnp.full((1, N), omega)
+    row_ref[3:4] = jnp.full((1, N), base)
+    row_ref[4:5] = jnp.full((1, N), last_ref[0].astype(jnp.float32))
+    lane = lax.broadcasted_iota(jnp.int32, (1, 128), 1) // 32
     for g in range(8):
         classes = [class_ref[g * 4 + t] for t in range(4)]
         for c in range(2):
-            beta = jnp.full((8, 128), coupling_ref[classes[0] * 2 + c])
+            beta = jnp.full((1, 128), coupling_ref[classes[0] * 2 + c])
             for t in range(1, 4):
                 beta = jnp.where(lane == t, coupling_ref[classes[t] * 2 + c], beta)
-            beta_ref[c, :, g * 128 : g * 128 + 128] = beta
+            row_ref[c : c + 1, g * 128 : g * 128 + 128] = beta
         for part in range(2):
-            total = [None, None]
-            for t in range(4):
-                for c in range(2):
-                    tile = wide_ref[part, classes[t], c * 32 : c * 32 + 32] * own_ref[t]
-                    total[c] = tile if t == 0 else total[c] + tile
-                    if c == 0:
-                        my_ref[part, g, t * 32 : t * 32 + 32, :128] = tile
-                        my_ref[part, g, 128 + t * 32 : 160 + t * 32, 128:] = tile
-                    else:
-                        my_ref[part, g, 128 + t * 32 : 160 + t * 32, :128] = tile
-                        my_ref[part, g, t * 32 : t * 32 + 32, 128:] = -tile
+            total = []
+            for c in range(2):
+                tiles = [wide_ref[part, classes[t], c * 32 : c * 32 + 32] * own_ref[t, :, :128] for t in range(4)]
+                total.append((tiles[0] + tiles[1]) + (tiles[2] + tiles[3]))
             mx_ref[part, g, :32, :128] = total[0]
             mx_ref[part, g, :32, 128:] = -total[1]
             mx_ref[part, g, 32:, :128] = total[1]
@@ -269,9 +269,15 @@
 
 
 def finish(
-    in_ref, w3_ref, twist_ref, lens_ref, beta_ref, mx_ref, my_ref, own_ref, image_ref,
-    out_ref, image_out_ref, mixed_ref, lensed_ref, rhs_ref, across_ref,
+    in_ref, w3_ref, twist_ref, lens_ref, row_ref, mx_ref, own_ref, up_ref, down_ref, fresh_any,
+    out_ref, real_ref, mixed_ref, lensed_ref, rhs_ref, across_ref, fresh_ref, sem,
 ):
+    copy = pltpu.make_async_copy(fresh_any, fresh_ref, sem)
+    copy.start()
+    side = lax.broadcasted_iota(jnp.int32, (8, N), 0)
+    sides = jnp.where(side == 0, up_ref[...], down_ref[...])
+    cos, sin = sincos(row_ref[2:3] * (sides - row_ref[3:4]) * DEPTH_KM)
+    side_lens = cos * NORM, sin * NORM
     turned = in_ref[...].reshape(256, 384)[:, :384].T
     mixed_ref[...] = product(split(turned[:320]), (w3_ref[0], w3_ref[1]))
     for block in range(5):
@@ -285,7 +291,10 @@
         for n1, value in enumerate(dft(values, 1)):
             lanes = slice(n1 * 128, n1 * 128 + 128)
             rows = slice(block * 8, block * 8 + 8)
-            value = cmul(value, (lens_ref[0, rows, lanes], lens_ref[1, rows, lanes]))
+            if block < 4:
+                value = cmul(value, (lens_ref[0, rows, lanes], lens_ref[1, rows, lanes]))
+            else:
+                value = cmul(value, (side_lens[0][:, lanes], side_lens[1][:, lanes]))
             for c in range(2):
                 if block < 4:
                     lensed_ref[c, 8 + block * 8 : 16 + block * 8, lanes] = value[c]
@@ -294,7 +303,7 @@
                     lensed_ref[c, 40:41, lanes] = value[c][1:2]
     for g in range(8):
         lanes = slice(g * 128, g * 128 + 128)
-        beta = (beta_ref[0, 0:1, lanes], beta_ref[1, 0:1, lanes])
+        beta = (row_ref[0:1, lanes], row_ref[1:2, lanes])
         mid = [lensed_ref[c, 8:40, lanes] for c in range(2)]
         diff = tuple(
             lensed_ref[c, 9:41, lanes] + lensed_ref[c, 7:39, lanes] - 2.0 * mid[c] for c in range(2)
@@ -302,7 +311,7 @@
         more = cmul(diff, beta)
         pieces = [split(mid[c] + more[c]) for c in range(2)]
         rhs = [
-            jnp.concatenate([pieces[c][part] * own_ref[t] for c in range(2) for t in range(4)], axis=0)
+            jnp.concatenate([pieces[c][part] * own_ref[t, :, :128] for c in range(2) for t in range(4)], axis=0)
             for part in range(2)
         ]
         out = product((mx_ref[0, g], mx_ref[1, g]), rhs)
@@ -315,51 +324,59 @@
         after = jnp.where(lane == N - 1, 0.0, pltpu.roll(whole, N - 1, 1))
         before = jnp.where(lane == 0, 0.0, pltpu.roll(whole, 1, 1))
         diff.append(after + before - 2.0 * whole)
-    more = cmul(diff, (beta_ref[0, 0:1], beta_ref[1, 0:1]))
+    more = cmul(diff, (row_ref[0:1], row_ref[1:2]))
     for c in range(2):
         rhs_ref[c] = across_ref[c] + more[c]
+    copy.wait()
     for g in range(8):
         lanes = slice(g * 128, g * 128 + 128)
         rhs = jnp.concatenate([rhs_ref[0, :, lanes], rhs_ref[1, :, lanes]], axis=1)
-        out = product(split(rhs), (my_ref[0, g], my_ref[1, g]), NT)
-        out_ref[0, :, lanes] = out[:, :128]
-        out_ref[1, :, lanes] = out[:, 128:]
-        image_out_ref[:, lanes] = image_ref[:, lanes] + out[:, :128]
+        tiles = [
+            jnp.concatenate(
+                [mx_ref[part, g, c * 32 : c * 32 + 32] * own_ref[t] for c in range(2) for t in range(4)], axis=0
+            )
+            for part in range(2)
+        ]
+        out = product(split(rhs), tiles, NT)
+        real_ref[:, lanes] = out[:, :128]
+        last = row_ref[4:5, lanes] > 0.5
+        for c in range(2):
+            out_ref[c, :, lanes] = jnp.where(last, fresh_ref[c, :, lanes], out[:, c * 128 : c * 128 + 128])
 
 
 def spread_y(field, t):
+    half = pltpu.VMEM((256, 256), jnp.bfloat16)
+    scratch = [pltpu.VMEM((2, 32, N), jnp.float32), pltpu.VMEM((2, 8, 128), jnp.float32)]
+    scratch += [pltpu.VMEM((2, 256, 256), jnp.bfloat16), half, half, pltpu.SemaphoreType.DMA((3,))]
+    args = [field, t["twist_y"], t["w1"]]
+    return call(forward_y, [shape(32, 8, 256)], scratch, args, large=(0, 1, 2))[0]
+
+
+def phase_tables(freq, refslow, lat, t):
+    args = [freq, refslow, lat, t["x"], t["twist_x"], t["edge"]]
+    outs = [shape(2, 256, 128)] + [jax.ShapeDtypeStruct(a.shape, a.dtype) for a in args[3:]]
+    return call(phases, outs, [pltpu.SemaphoreType.DMA((3,))], args, scalars=(0, 1, 2), large=(3, 4, 5))
+
+
+def continue_x(block, tabs):
     scratch = [pltpu.VMEM((256, 256), jnp.bfloat16)] * 2
-    return call(forward_y, [shape(32, 8, 256)], scratch, [field, t["w1"], t["twist_y"]], ())[0]
-
-
-def phase_tables(freq, refslow, lat):
-    return call(phases, [shape(2, 256, 128)], [], [freq, refslow, lat], (0, 1, 2))[0]
-
-
-def continue_x(block, phase, t):
-    scratch = [pltpu.VMEM((256, 256), jnp.bfloat16)] * 2
-    args = [block, phase, t["a1"], t["b1"], t["b2"], t["a2"], t["twist_x"], t["edge"]]
-    return call(along_x, [shape(32, 8, 384)], scratch, args, ())[0]
-
-
-def correction_tables(freq, refslow, classes, coupling, slow, up, down, blocks, t):
+    return call(along_x, [shape(32, 8, 384)], scratch, [block, *tabs])[0]
+
+
+def correction_tables(freq, refslow, classes, coupling, last, slow, blocks, t):
     half = jnp.bfloat16
-    outs = [shape(2, 40, N), shape(2, 8, N), shape(2, 8, 64, 256, dtype=half), shape(2, 8, 256, 256, dtype=half)]
+    outs = [shape(2, 32, N), shape(8, N), shape(2, 8, 64, 256, dtype=half)]
     scratch = [pltpu.VMEM((2, 16, 64, 128), half)]
-    args = [freq, refslow, classes, coupling, slow, up, down, blocks, t["own"], t["spread"]]
-    return call(weights, outs, scratch, args, (0, 1, 2, 3))
-
-
-def correct(block, tabs, image, t):
-    lens, beta, mx, my = tabs
-    scratch = [
-        pltpu.VMEM((320, 256), jnp.float32),
-        pltpu.VMEM((2, 48, N), jnp.float32),
-        pltpu.VMEM((2, 32, N), jnp.float32),
-        pltpu.VMEM((2, 32, N), jnp.float32),
-    ]
-    args = [block, t["w3"], t["twist_y"], lens, beta, mx, my, t["own"], image]
-    return call(finish, [shape(2, 32, N), shape(32, N)], scratch, args, ())
+    args = [freq, refslow, classes, coupling, last, slow, blocks, t["own"], t["spread"]]
+    return call(weights, outs, scratch, args, scalars=(0, 1, 2, 3, 4))
+
+
+def correct(block, tabs, up, down, fresh, t):
+    plane = pltpu.VMEM((2, 32, N), jnp.float32)
+    scratch = [pltpu.VMEM((320, 256), jnp.float32), pltpu.VMEM((2, 48, N), jnp.float32)]
+    scratch += [plane, plane, plane, pltpu.SemaphoreType.DMA]
+    args = [block, t["w3"], t["twist_y"], *tabs, t["own"], up, down, fresh]
+    return call(finish, [shape(2, 32, N), shape(32, N)], scratch, args, large=(9,))
 
 
 def exchange(block):
@@ -375,24 +392,23 @@
 ):
     t = tables()
     block = spread_y(field.reshape(2, 32, N), t)
-    block, (freq, refslow, slow) = after(block, freq_index.reshape(1), ref_slowness, slowness[0])
+    block, (freq, refslow) = after(block, freq_index.reshape(1), ref_slowness)
     received = exchange(block)
     lat = lax.axis_index("lat").reshape(1).astype(jnp.int32)
-    phase = phase_tables(freq, refslow, lat)
+    block = continue_x(received, phase_tables(freq, refslow, lat, t))
+    block, (freq, classes, slow) = after(block, freq, tile_classes.reshape(32), slowness[0])
+    received = exchange(block)
+    count = lax.axis_size("depth")
+    last = (lax.axis_index("depth") == count - 1).reshape(1).astype(jnp.int32)
+    tabs = correction_tables(
+        freq, refslow, classes, fd_coupling.reshape(32), last, slow, fd_blocks.reshape(1024, 32), t
+    )
+    tabs, (slow,) = after(tabs, slow)
     down = lax.ppermute(slow[:1], "lat", [(i + 1, i) for i in range(LAT - 1)])
     up = lax.ppermute(slow[-1:], "lat", [(i, i + 1) for i in range(LAT - 1)])
-    block = continue_x(received, phase, t)
-    block, (freq, classes, up, down) = after(block, freq, tile_classes.reshape(32), up, down)
-    received = exchange(block)
-    tabs = correction_tables(
-        freq, refslow, classes, fd_coupling.reshape(32), slow, up, down, fd_blocks.reshape(1024, 32), t
-    )
-    result, new_image = correct(received, tabs, image[0], t)
-    count = lax.axis_size("depth")
-    moved = lax.ppermute(result, "depth", [(i, i + 1) for i in range(count - 1)])
-    first_section = lax.axis_index("depth") == 0
-    next_field = jnp.where(first_section, fresh[0], moved)[None, None]
-    return next_field, new_image[None]
+    result, real = correct(received, tabs, up, down, fresh[0], t)
+    next_field = lax.ppermute(result, "depth", [(i, (i + 1) % count) for i in range(count)])
+    return next_field[None, None], image + real[None]
 
 
 def solution(mesh):

time: 73.8 us -> 60 us (0.81)
  the two profiles are of different devices: /device:TPU:1 before, /device:TPU:102 now
where the time goes in v1:
time: 60 us; the launch traced here: 59.5 us
  starting transfers between devices  24.4 us (41%)
  waiting for transfers between devices  19.9 us (33%)
  Pallas kernels  10.2 us (17%)
  local copies, waits for them, and re-layouts  2.2 us (4%)
  between operations  2.1 us (4%)
  other arithmetic  0.67 us (1%)
    all_to_all x2, starting transfers between devices, exchange(): return lax.all_to_all(block, 'lat', split_axis=0, concat_axis=0, tiled=True)  17.9 us
    pallas_call x5, Pallas kernels, call(): pl.pallas_call(body, out_shape=outs, in_specs=[pl.BlockSpec(memory_space=...  10.2 us
    ppermute x1, waiting for transfers between devices, per_device(): down = lax.ppermute(slow[:1], 'lat', [(i + 1, i) for i in range(LAT - 1)])  6.88 us
    all_to_all x2, waiting for transfers between devices, exchange(): return lax.all_to_all(block, 'lat', split_axis=0, concat_axis=0, tiled=True)  6.66 us
    ppermute x1, waiting for transfers between devices, per_device(): lax.ppermute(result, 'depth', [(i, (i + 1) % count) for i in range(count)])  6.31 us
    ppermute x1, starting transfers between devices, per_device(): up = lax.ppermute(slow[-1:], 'lat', [(i, i + 1) for i in range(LAT - 1)])  4.58 us
    unnamed x20, local copies, waits for them, and re-layouts  2.11 us
    ppermute x1, starting transfers between devices, per_device(): down = lax.ppermute(slow[:1], 'lat', [(i + 1, i) for i in range(LAT - 1)])  1.92 us
  transfers between devices with their start and end apart: 5, of which 3 were waited for; matrix products, arithmetic and copies ran while one was open for 1% of the time, Pallas kernels for 5%

profile of v1, /device:TPU:102, one launch (start us, length us, event | category | flops | bytes accessed | tf_op | source)
XLA Modules:
  0.0 59.5 jit_solution(11357660990681361828)
XLA Ops:
  0.6 2.1 %shard_map.176 = f32[32,8,256]{2,1,0:T(8,128)} custom-call(f32[2,32,1024]{2,1,0:T(8,128)} %bitcast.17, f32[2,8,128]{2,1,0:T(8,128)} %constant.25.clone.twist_any.twist_ref, bf16[2,256,256]{2,1,0:T(8,128)(2,1)} %constant.26.clone.w1_any.w3_ref), custom_call_target="tpu_custom_call" | custom-call | bytes 794624 | tf_op jit(solution)/shard_map/pallas_call | solution.py:117
  2.7 10.2 %all-to-all-start = ((f32[32,8,256]{2,1,0:T(8,128)}), f32[32,8,256]{2,1,0:T(8,128)S(1)}, u32[]{:S(2)}, u32[]{:S(2)}) async-start(f32[32,8,256]{2,1,0:T(8,128)} %shard_map.176), calls=%async_computation | async-start | bytes 524288 | tf_op jit(solution)/shard_map/all_to_all | solution.py:383
  14.2 1.3 %shard_map.177 = (f32[2,256,128]{2,1,0:T(8,128)S(1)}, bf16[4,2,256,256]{3,2,1,0:T(8,128)(2,1)S(1)}, f32[2,32,128]{2,1,0:T(8,128)S(1)}, bf16[256,128]{1,0:T(8,128)(2,1)S(1)}) custom-call(s32[1]{0:T(128)} %bitcast.11.freq_ref, f32[1]{0:T(128)S(6)} %copy.23.slow_ref.refslow_ref, s32[1]{0:T(128)} %bitcast.2.lat_ref, ...), custom_call_target="tpu_custom_call" | custom-call | bytes 2555916 | tf_op jit(solution)/shard_map/pallas_call | solution.py:117
  15.5 6.7 %all-to-all-done.in_ref = f32[32,8,256]{2,1,0:T(8,128)S(1)} async-done(((f32[32,8,256]{2,1,0:T(8,128)}), f32[32,8,256]{2,1,0:T(8,128)S(1)}, u32[]{:S(2)}, u32[]{:S(2)}) %all-to-all-start) | async-done | bytes 262176 | tf_op jit(solution)/shard_map/all_to_all | solution.py:383
  22.2 2.2 %shard_map.178 = f32[32,8,384]{2,1,0:T(8,128)} custom-call(f32[32,8,256]{2,1,0:T(8,128)S(1)} %all-to-all-done.in_ref, f32[2,256,128]{2,1,0:T(8,128)S(1)} %get-tuple-element.25.phase_ref, bf16[4,2,256,256]{3,2,1,0:T(8,128)(2,1)S(1)} %get-tuple-element.26.x_ref, f32[2,32,128]{2,1,0:T(8,128)S(1)} %get-tuple-element.27.twist_ref, ...), custom_call_target="tpu_custom_call" | custom-call | bytes 2064384 | tf_op jit(solution)/shard_map/pallas_call | solution.py:117
  24.4 7.7 %all-to-all-start.1 = ((f32[32,8,384]{2,1,0:T(8,128)}), f32[32,8,384]{2,1,0:T(8,128)S(1)}, u32[]{:S(2)}, u32[]{:S(2)}) async-start(f32[32,8,384]{2,1,0:T(8,128)} %shard_map.178), calls=%async_computation.1 | async-start | bytes 786432 | tf_op jit(solution)/shard_map/all_to_all | solution.py:383
  32.1 0.0 copy-start.8
  32.1 0.7 %copy-done.8 = f32[16,2]{0,1:T(2,128)S(1)} copy-done((f32[16,2]{0,1:T(2,128)S(1)}, f32[16,2]{0,1:T(2,128)}, u32[]{:S(2)}) %copy-start.8) | copy-done | bytes 152
  32.8 0.1 copy.20
  32.9 0.1 reshape.29.coupling_ref
  33.0 0.0 copy-start.6
  33.0 0.0 copy-done.1
  33.0 0.0 copy-done.2
  33.0 0.0 copy-done.3
  33.0 0.6 copy-done.5
  33.6 0.1 copy-done.6
  33.6 1.5 %shard_map.179 = (f32[2,32,1024]{2,1,0:T(8,128)S(1)}, f32[8,1024]{1,0:T(8,128)S(1)}, bf16[2,8,64,256]{3,2,1,0:T(8,128)(2,1)S(1)}) custom-call(s32[1]{0:T(128)} %bitcast.12.freq_ref, f32[1]{0:T(128)S(6)} %copy.23.slow_ref.refslow_ref, s32[32]{0:T(128)S(1)} %bitcast.16, f32[32]{0:T(128)S(1)} %reshape.29.coupling_ref, s32[1]{0:T(128)} %bitcast.5.last_ref, ...), custom_call_target="tpu_custom_call" | custom-call | bytes 1155340 | tf_op jit(solution)/shard_map/pallas_call | solution.py:117
  35.1 0.0 copy-start.4
  35.2 4.6 %collective-permute-start = (f32[1,1024]{1,0:T(1,128)S(1)}, f32[1,1024]{1,0:T(1,128)S(1)}, u32[]{:S(2)}, u32[]{:S(2)}) collective-permute-start(f32[1,1024]{1,0:T(1,128)S(1)} %get-tuple-element.43), channel_id=1, source_target_pairs={{0,1},{1,2},{2,3},{3,4},{4,5},{5,6},{6,7},{7,8},{8,9},{9,10},{10,1... | collective-permute-start | bytes 12296 | tf_op jit(solution)/shard_map/ppermute | solution.py:408
  39.7 1.9 %collective-permute-start.1 = (f32[1,1024]{1,0:T(1,128)S(1)}, f32[1,1024]{1,0:T(1,128)S(1)}, u32[]{:S(2)}, u32[]{:S(2)}) collective-permute-start(f32[1,1024]{1,0:T(1,128)S(1)} %get-tuple-element.42), channel_id=1, source_target_pairs={{1,0},{2,1},{3,2},{4,3},{5,4},{6,5},{7,6},{8,7},{9,8},{10,9},{11,1... | collective-permute-start | bytes 12296 | tf_op jit(solution)/shard_map/ppermute | solution.py:407
  41.7 0.0 collective-permute-done.up_ref
  41.7 6.9 %collective-permute-done.1.down_ref = f32[1,1024]{1,0:T(1,128)S(1)} collective-permute-done((f32[1,1024]{1,0:T(1,128)S(1)}, f32[1,1024]{1,0:T(1,128)S(1)}, u32[]{:S(2)}, u32[]{:S(2)}) %collective-permute-start.1) | collective-permute-done | bytes 4128 | tf_op jit(solution)/shard_map/ppermute | solution.py:407
  48.6 0.0 all-to-all-done.1.in_ref
  48.6 0.0 copy-done
  48.6 0.0 copy-done.4
  48.6 0.0 copy-start.7
  48.6 3.2 %shard_map.180 = (f32[2,32,1024]{2,1,0:T(8,128)S(1)}, f32[32,1024]{1,0:T(8,128)S(1)}) custom-call(f32[32,8,384]{2,1,0:T(8,128)S(1)} %all-to-all-done.1.in_ref, bf16[2,256,256]{2,1,0:T(8,128)(2,1)S(1)} %copy-done, f32[2,8,128]{2,1,0:T(8,128)S(1)} %copy-done.4, f32[2,32,1024]{2,1,0:T(8,128)S(1)} %get-tuple-element.36.lens_ref, ...), custom_call_target="tpu_custom_call" | custom-call | bytes 2211840 | tf_op jit(solution)/shard_map/pallas_call | solution.py:117
  51.8 0.0 collective-permute-start.2
  51.8 0.0 copy-done.7
  51.8 0.7 %bitcast_add_fusion = f32[1,32,1024]{2,1,0:T(8,128)} fusion(f32[1,32,1024]{2,1,0:T(8,128)S(1)} %copy-done.7, f32[32,1024]{1,0:T(8,128)S(1)} %get-tuple-element.41), kind=kLoop, calls=%fused_computation | loop fusion | flops 32768 | bytes 393216 | tf_op jit(solution)/shard_map/add | solution.py:411
  52.5 6.3 %collective-permute-done.2 = f32[2,32,1024]{2,1,0:T(8,128)S(1)} collective-permute-done((f32[2,32,1024]{2,1,0:T(8,128)S(1)}, f32[2,32,1024]{2,1,0:T(8,128)S(1)}, u32[]{:S(2)}, u32[]{:S(2)}) %collective-permute-start.2) | collective-permute-done | bytes 262176 | tf_op jit(solution)/shard_map/ppermute | solution.py:410
  58.8 0.7 %copy.24 = f32[1,1,2,32,1024]{4,3,2,1,0:T(8,128)} copy(f32[1,1,2,32,1024]{4,3,2,1,0:T(8,128)S(1)} %bitcast.19) | data formatting | bytes 524288
  (6 shorter events, 0.0 us)
Async XLA Ops:
  2.7 19.4 %all-to-all-start = ((f32[32,8,256]{2,1,0:T(8,128)}), f32[32,8,256]{2,1,0:T(8,128)S(1)}, u32[]{:S(2)}, u32[]{:S(2)}) async-start(f32[32,8,256]{2,1,0:T(8,128)} %shard_map.176), calls=%async_computation | async-start | bytes 524288 | tf_op jit(solution)/shard_map/all_to_all | solution.py:383
  24.4 8.6 %copy-start.1 = (f32[16,2,32,32]{3,2,1,0:T(8,128)S(1)}, f32[16,2,32,32]{3,2,1,0:T(8,128)}, u32[]{:S(2)}) copy-start(f32[16,2,32,32]{3,2,1,0:T(8,128)} %param.23) | copy-start | bytes 393220
  24.4 8.6 %copy-start.2 = (bf16[4,32,256]{2,1,0:T(8,128)(2,1)S(1)}, bf16[4,32,256]{2,1,0:T(8,128)(2,1)}, u32[]{:S(2)}) copy-start(bf16[4,32,256]{2,1,0:T(8,128)(2,1)} %constant.30.clone.own_ref) | copy-start | bytes 196612
  24.4 8.6 %copy-start.3 = (f32[1,32,1024]{2,1,0:T(8,128)S(1)}, f32[1,32,1024]{2,1,0:T(8,128)}, u32[]{:S(2)}) copy-start(f32[1,32,1024]{2,1,0:T(8,128)} %param.21) | copy-start | bytes 393220
  24.4 24.2 %all-to-all-start.1 = ((f32[32,8,384]{2,1,0:T(8,128)}), f32[32,8,384]{2,1,0:T(8,128)S(1)}, u32[]{:S(2)}, u32[]{:S(2)}) async-start(f32[32,8,384]{2,1,0:T(8,128)} %shard_map.178), calls=%async_computation.1 | async-start | bytes 786432 | tf_op jit(solution)/shard_map/all_to_all | solution.py:383
  32.1 0.7 %copy-start.8 = (f32[16,2]{0,1:T(2,128)S(1)}, f32[16,2]{0,1:T(2,128)}, u32[]{:S(2)}) copy-start(f32[16,2]{0,1:T(2,128)} %param.24) | copy-start | bytes 388
  32.9 0.7 %copy-start.5 = (bf16[32,128]{1,0:T(8,128)(2,1)S(1)}, bf16[32,128]{1,0:T(8,128)(2,1)}, u32[]{:S(2)}) copy-start(bf16[32,128]{1,0:T(8,128)(2,1)} %constant.31.clone.spread_ref) | copy-start | bytes 24580
  33.0 0.7 %copy-start.6 = (s32[1,1,32]{2,1,0:T(1,128)S(1)}, s32[1,1,32]{2,1,0:T(1,128)}, u32[]{:S(2)}) copy-start(s32[1,1,32]{2,1,0:T(1,128)} %param.22) | copy-start | bytes 388
  33.6 15.0 %copy-start = (bf16[2,256,256]{2,1,0:T(8,128)(2,1)S(1)}, bf16[2,256,256]{2,1,0:T(8,128)(2,1)}, u32[]{:S(2)}) copy-start(bf16[2,256,256]{2,1,0:T(8,128)(2,1)} %constant.26.clone.w1_any.w3_ref) | copy-start | bytes 786436
  35.1 13.4 %copy-start.4 = (f32[2,8,128]{2,1,0:T(8,128)S(1)}, f32[2,8,128]{2,1,0:T(8,128)}, u32[]{:S(2)}) copy-start(f32[2,8,128]{2,1,0:T(8,128)} %constant.25.clone.twist_any.twist_ref) | copy-start | bytes 24580
  35.2 6.5 %collective-permute-start = (f32[1,1024]{1,0:T(1,128)S(1)}, f32[1,1024]{1,0:T(1,128)S(1)}, u32[]{:S(2)}, u32[]{:S(2)}) collective-permute-start(f32[1,1024]{1,0:T(1,128)S(1)} %get-tuple-element.43), channel_id=1, source_target_pairs={{0,1},{1,2},{2,3},{3,4},{4,5},{5,6},{6,7},{7,8},{8,9},{9,10},{10,1... | collective-permute-start | bytes 12296 | tf_op jit(solution)/shard_map/ppermute | solution.py:408
  39.7 8.8 %collective-permute-start.1 = (f32[1,1024]{1,0:T(1,128)S(1)}, f32[1,1024]{1,0:T(1,128)S(1)}, u32[]{:S(2)}, u32[]{:S(2)}) collective-permute-start(f32[1,1024]{1,0:T(1,128)S(1)} %get-tuple-element.42), channel_id=1, source_target_pairs={{1,0},{2,1},{3,2},{4,3},{5,4},{6,5},{7,6},{8,7},{9,8},{10,9},{11,1... | collective-permute-start | bytes 12296 | tf_op jit(solution)/shard_map/ppermute | solution.py:407
  48.6 3.2 %copy-start.7 = (f32[1,32,1024]{2,1,0:T(8,128)S(1)}, f32[1,32,1024]{2,1,0:T(8,128)}, u32[]{:S(2)}) copy-start(f32[1,32,1024]{2,1,0:T(8,128)} %param.25) | copy-start | bytes 393220
  51.8 7.0 %collective-permute-start.2 = (f32[2,32,1024]{2,1,0:T(8,128)S(1)}, f32[2,32,1024]{2,1,0:T(8,128)S(1)}, u32[]{:S(2)}, u32[]{:S(2)}) collective-permute-start(f32[2,32,1024]{2,1,0:T(8,128)S(1)} %get-tuple-element.40), channel_id=1, source_target_pairs={{0,32},{32,64},{64,96},{96,128},{128,160},{160,192},{192,224},{224... | collective-permute-start | bytes 786440 | tf_op jit(solution)/shard_map/ppermute | solution.py:410

commit v2 on v1

--- a/solution.py
+++ b/solution.py
@@ -48,11 +48,16 @@
     tx = np.tile(2 * np.pi * small[:, None] * small / N, (1, 4))
     twist_y = np.stack([np.cos(ty), np.sin(ty)]).astype(np.float32)
     twist_x = np.stack([np.cos(tx), np.sin(tx)]).astype(np.float32)
-    edge = np.zeros((8, 32, 16, 8))
+    edge = np.zeros((8, 32, 8, 8, 2))
+    fold = np.zeros((8, 8, 2, 16, 8))
     for k1 in range(8):
-        edge[k1, 31, k1, 0] = 1
-        edge[k1, 0, k1, 1] = 1
+        edge[k1, 31, :, k1, 0] = 1
+        edge[k1, 0, :, k1, 1] = 1
+        for side in range(2):
+            fold[:, k1, side, k1, side] = 1
     edge = edge.reshape(256, 128).astype(ml_dtypes.bfloat16)
+    fold = fold.reshape(128, 128).astype(ml_dtypes.bfloat16)
+    gather = np.repeat(np.eye(32), 8, axis=1).astype(ml_dtypes.bfloat16)
     own = (np.arange(128)[None, :] // 32 == np.arange(4)[:, None]).astype(np.float32)
     own = np.broadcast_to(np.tile(own, (1, 2))[:, None, :], (4, 32, 256)).astype(ml_dtypes.bfloat16)
     spread = np.tile(np.eye(32), (1, 4)).astype(ml_dtypes.bfloat16)
@@ -63,6 +68,8 @@
         "twist_y": twist_y,
         "twist_x": twist_x,
         "edge": edge,
+        "fold": fold,
+        "gather": gather,
         "own": own,
         "spread": spread,
     }
@@ -137,8 +144,20 @@
     return jax.ShapeDtypeStruct(dims, dtype)
 
 
-def forward_y(field_any, twist_any, w1_any, out_ref, field_ref, twist_ref, w1_ref, high_ref, low_ref, sems):
-    copies = fetch([field_any, twist_any, w1_any], [field_ref, twist_ref, w1_ref], sems)
+FIRST = 17
+SECOND = 18
+
+
+def lane_of(dims):
+    return lax.broadcasted_iota(jnp.int32, dims, len(dims) - 1)
+
+
+def forward_y(
+    field_any, twist_any, w1_any, slow_any, out_ref,
+    field_ref, twist_ref, w1_ref, slow_ref, high_ref, low_ref, ends_ref, sems,
+):
+    sources = [field_any, twist_any, slow_any.at[0:8], slow_any.at[24:32], w1_any]
+    copies = fetch(sources, [field_ref, twist_ref, slow_ref.at[0:8], slow_ref.at[8:16], w1_ref], sems)
     copies[0].wait()
     copies[1].wait()
     for top in range(0, 32, 16):
@@ -156,16 +175,32 @@
                 high_ref[at, c * 128 : c * 128 + 128] = high
                 low_ref[at, c * 128 : c * 128 + 128] = low
     copies[2].wait()
+    copies[3].wait()
+    for n1 in range(8):
+        ends_ref[0, n1 : n1 + 1] = slow_ref[0:1, n1 * 128 : n1 * 128 + 128]
+        ends_ref[1, n1 : n1 + 1] = slow_ref[15:16, n1 * 128 : n1 * 128 + 128]
+    lane = lane_of((8, 128))
+    for m in range(4):
+        first = pltpu.roll(ends_ref[0], (-32 * m) % 128, 1)
+        last = pltpu.roll(ends_ref[1], (32 - 32 * m) % 128, 1)
+        out_ref[pl.ds(FIRST * m + 16, 8, stride=4 * FIRST), :] = jnp.where(lane < 32, first, last)
+    copies[4].wait()
     out = product((w1_ref[0], w1_ref[1]), (high_ref[...], low_ref[...]), NT)
-    out_ref[...] = out.reshape(32, 8, 256)
+    for j in range(LAT):
+        for half in range(2):
+            top = FIRST * j + half * 8
+            out_ref[top : top + 8] = out[j * 8 : j * 8 + 8, half * 128 : half * 128 + 128]
 
 
 def sincos(angle):
     return jnp.cos(angle), jnp.sin(angle)
 
 
-def phases(freq_ref, slow_ref, lat_ref, x_any, twist_any, edge_any, out_ref, x_ref, twist_ref, edge_ref, sems):
-    copies = fetch([x_any, twist_any, edge_any], [x_ref, twist_ref, edge_ref], sems)
+def phases(
+    freq_ref, slow_ref, lat_ref, x_any, twist_any, edge_any, gather_any,
+    out_ref, x_ref, twist_ref, edge_ref, gather_ref, sems,
+):
+    copies = fetch([x_any, twist_any, edge_any, gather_any], [x_ref, twist_ref, edge_ref, gather_ref], sems)
     omega = 2.0 * math.pi * (LOW_HZ + STEP_HZ * freq_ref[0].astype(jnp.float32))
     reach = omega * slow_ref[0]
     scale = 2.0 * math.pi / (N * SPACING_KM)
@@ -188,8 +223,14 @@
         copy.wait()
 
 
-def along_x(in_ref, phase_ref, x_ref, twist_ref, edge_ref, out_ref, high_ref, low_ref):
-    lines = in_ref[...].reshape(256, 256)
+def both_tiles(ref, rows):
+    return [
+        jnp.concatenate([ref[rows * i + half * 8 : rows * i + half * 8 + 8] for i in range(LAT)], axis=0) for half in range(2)
+    ]
+
+
+def along_x(in_ref, phase_ref, x_ref, twist_ref, edge_ref, gather_ref, out_ref, high_ref, low_ref):
+    lines = jnp.concatenate(both_tiles(in_ref, FIRST), axis=1)
     mixed = product((x_ref[0, 0], x_ref[0, 1]), split(lines))
     cos, sin = twist_ref[0], twist_ref[1]
 
@@ -221,15 +262,24 @@
                 high_ref[at, h * 128 : h * 128 + 128] = high
                 low_ref[at, h * 128 : h * 128 + 128] = low
     out = product((x_ref[3, 0], x_ref[3, 1]), (high_ref[...], low_ref[...]))
+    for i in range(LAT):
+        for half in range(2):
+            top = SECOND * i + half * 8
+            out_ref[top : top + 8] = out[i * 8 : i * 8 + 8, half * 128 : half * 128 + 128]
+    dot = lambda a, b: lax.dot_general(a, b, NN, preferred_element_type=jnp.float32)
     high, low = split(out)
-    dot = lambda a: lax.dot_general(a, edge_ref[...], NN, preferred_element_type=jnp.float32)
-    edge = (dot(high) + dot(low)).reshape(32, 8, 128)
-    out_ref[:, :, :256] = out.reshape(32, 8, 256)
-    side = lax.broadcasted_iota(jnp.int32, (32, 8, 128), 2) % 8
-    zero = jnp.zeros((1, 8, 128), jnp.float32)
-    before = jnp.concatenate([zero, edge[:-1]], axis=0)
-    after = jnp.concatenate([edge[1:], zero], axis=0)
-    out_ref[:, :, 256:] = jnp.where(side == 0, before, after)
+    edge = dot(high, edge_ref[...]) + dot(low, edge_ref[...])
+    own = lane_of((256, 128)) // 16 == lax.broadcasted_iota(jnp.int32, (256, 128), 0) % 8
+    high, low = split(jnp.where(own, edge, 0.0))
+    edge = dot(gather_ref[...], high) + dot(gather_ref[...], low)
+    lane, row = lane_of((LAT, 128)), lax.broadcasted_iota(jnp.int32, (LAT, 128), 0)
+    before = jnp.where(row == 0, 0.0, pltpu.roll(edge, 1, 0))
+    after = jnp.where(row == LAT - 1, 0.0, pltpu.roll(edge, LAT - 1, 0))
+    out_ref[pl.ds(16, LAT, stride=SECOND), :] = jnp.where(lane % 2 == 0, before, after)
+    slow = in_ref[pl.ds(16, LAT, stride=FIRST), :]
+    before = pltpu.roll(pltpu.roll(slow, 96, 1), 1, 0)
+    after = pltpu.roll(pltpu.roll(slow, 32, 1), LAT - 1, 0)
+    out_ref[pl.ds(17, LAT, stride=SECOND), :] = jnp.where(lane < 32, before, after)
 
 
 def weights(
@@ -269,17 +319,31 @@
 
 
 def finish(
-    in_ref, w3_ref, twist_ref, lens_ref, row_ref, mx_ref, own_ref, up_ref, down_ref, fresh_any,
+    in_ref, w3_ref, twist_ref, lens_ref, row_ref, mx_ref, own_ref, fold_ref, fresh_any,
     out_ref, real_ref, mixed_ref, lensed_ref, rhs_ref, across_ref, fresh_ref, sem,
 ):
     copy = pltpu.make_async_copy(fresh_any, fresh_ref, sem)
     copy.start()
-    side = lax.broadcasted_iota(jnp.int32, (8, N), 0)
-    sides = jnp.where(side == 0, up_ref[...], down_ref[...])
-    cos, sin = sincos(row_ref[2:3] * (sides - row_ref[3:4]) * DEPTH_KM)
-    side_lens = cos * NORM, sin * NORM
-    turned = in_ref[...].reshape(256, 384)[:, :384].T
-    mixed_ref[...] = product(split(turned[:320]), (w3_ref[0], w3_ref[1]))
+    lane = lane_of((8, 128))
+    sides = [None, None]
+    for m in range(4):
+        pieces = in_ref[pl.ds(17 + SECOND * m, 8, stride=4 * SECOND), :]
+        for side in range(2):
+            piece = pltpu.roll(pieces, (32 * m - 32 * side) % 128, 1)
+            sides[side] = piece if m == 0 else jnp.where(lane // 32 == m, piece, sides[side])
+    side_lens = []
+    for side in range(2):
+        cos, sin = sincos(row_ref[2:3, :128] * (sides[side] - row_ref[3:4, :128]) * DEPTH_KM)
+        side_lens.append((cos * NORM, sin * NORM))
+    beside = jnp.concatenate(
+        [jnp.broadcast_to(in_ref[SECOND * j + 16 : SECOND * j + 17], (8, 128)) for j in range(LAT)], axis=0
+    )
+    own = lane_of((256, 128)) // 16 == lax.broadcasted_iota(jnp.int32, (256, 128), 0) % 8
+    high, low = split(jnp.where(own, beside, 0.0))
+    dot = lambda a: lax.dot_general(a, fold_ref[...], NN, preferred_element_type=jnp.float32)
+    lines = [*both_tiles(in_ref, SECOND), dot(high) + dot(low)]
+    turned = jnp.concatenate([line.T for line in lines], axis=0)[:320]
+    mixed_ref[...] = product(split(turned), (w3_ref[0], w3_ref[1]))
     for block in range(5):
         values = []
         for k1 in range(8):
@@ -293,14 +357,14 @@
             rows = slice(block * 8, block * 8 + 8)
             if block < 4:
                 value = cmul(value, (lens_ref[0, rows, lanes], lens_ref[1, rows, lanes]))
-            else:
-                value = cmul(value, (side_lens[0][:, lanes], side_lens[1][:, lanes]))
-            for c in range(2):
-                if block < 4:
+                for c in range(2):
                     lensed_ref[c, 8 + block * 8 : 16 + block * 8, lanes] = value[c]
-                else:
-                    lensed_ref[c, 7:8, lanes] = value[c][0:1]
-                    lensed_ref[c, 40:41, lanes] = value[c][1:2]
+                continue
+            for side, at in enumerate((7, 40)):
+                pair = [value[c][side : side + 1] for c in range(2)]
+                pair = cmul(pair, [side_lens[side][c][n1 : n1 + 1] for c in range(2)])
+                for c in range(2):
+                    lensed_ref[c, at : at + 1, lanes] = pair[c]
     for g in range(8):
         lanes = slice(g * 128, g * 128 + 128)
         beta = (row_ref[0:1, lanes], row_ref[1:2, lanes])
@@ -344,23 +408,24 @@
             out_ref[c, :, lanes] = jnp.where(last, fresh_ref[c, :, lanes], out[:, c * 128 : c * 128 + 128])
 
 
-def spread_y(field, t):
+def spread_y(field, slow, t):
     half = pltpu.VMEM((256, 256), jnp.bfloat16)
     scratch = [pltpu.VMEM((2, 32, N), jnp.float32), pltpu.VMEM((2, 8, 128), jnp.float32)]
-    scratch += [pltpu.VMEM((2, 256, 256), jnp.bfloat16), half, half, pltpu.SemaphoreType.DMA((3,))]
-    args = [field, t["twist_y"], t["w1"]]
-    return call(forward_y, [shape(32, 8, 256)], scratch, args, large=(0, 1, 2))[0]
+    scratch += [pltpu.VMEM((2, 256, 256), jnp.bfloat16), pltpu.VMEM((16, N), jnp.float32), half, half]
+    scratch += [pltpu.VMEM((2, 8, 128), jnp.float32), pltpu.SemaphoreType.DMA((5,))]
+    args = [field, t["twist_y"], t["w1"], slow]
+    return call(forward_y, [shape(LAT * FIRST, 128)], scratch, args, large=(0, 1, 2, 3))[0]
 
 
 def phase_tables(freq, refslow, lat, t):
-    args = [freq, refslow, lat, t["x"], t["twist_x"], t["edge"]]
+    args = [freq, refslow, lat, t["x"], t["twist_x"], t["edge"], t["gather"]]
     outs = [shape(2, 256, 128)] + [jax.ShapeDtypeStruct(a.shape, a.dtype) for a in args[3:]]
-    return call(phases, outs, [pltpu.SemaphoreType.DMA((3,))], args, scalars=(0, 1, 2), large=(3, 4, 5))
+    return call(phases, outs, [pltpu.SemaphoreType.DMA((4,))], args, scalars=(0, 1, 2), large=(3, 4, 5, 6))
 
 
 def continue_x(block, tabs):
     scratch = [pltpu.VMEM((256, 256), jnp.bfloat16)] * 2
-    return call(along_x, [shape(32, 8, 384)], scratch, [block, *tabs])[0]
+    return call(along_x, [shape(LAT * SECOND, 128)], scratch, [block, *tabs])[0]
 
 
 def correction_tables(freq, refslow, classes, coupling, last, slow, blocks, t):
@@ -371,16 +436,17 @@
     return call(weights, outs, scratch, args, scalars=(0, 1, 2, 3, 4))
 
 
-def correct(block, tabs, up, down, fresh, t):
+def correct(block, tabs, fresh, t):
     plane = pltpu.VMEM((2, 32, N), jnp.float32)
     scratch = [pltpu.VMEM((320, 256), jnp.float32), pltpu.VMEM((2, 48, N), jnp.float32)]
     scratch += [plane, plane, plane, pltpu.SemaphoreType.DMA]
-    args = [block, t["w3"], t["twist_y"], *tabs, t["own"], up, down, fresh]
-    return call(finish, [shape(2, 32, N), shape(32, N)], scratch, args, large=(9,))
+    args = [block, t["w3"], t["twist_y"], *tabs, t["own"], t["fold"], fresh]
+    return call(finish, [shape(2, 32, N), shape(32, N)], scratch, args, large=(8,))
 
 
 def exchange(block):
-    return lax.all_to_all(block, "lat", split_axis=0, concat_axis=0, tiled=True)
+    blocks = block.reshape(LAT, 1, -1)
+    return lax.all_to_all(blocks, "lat", split_axis=0, concat_axis=0, tiled=True).reshape(block.shape)
 
 
 def after(value, *others):
@@ -391,22 +457,20 @@
     field, fresh, freq_index, ref_slowness, slowness, tile_classes, fd_blocks, fd_coupling, image
 ):
     t = tables()
-    block = spread_y(field.reshape(2, 32, N), t)
+    slow = slowness[0]
+    block = spread_y(field.reshape(2, 32, N), slow, t)
     block, (freq, refslow) = after(block, freq_index.reshape(1), ref_slowness)
     received = exchange(block)
     lat = lax.axis_index("lat").reshape(1).astype(jnp.int32)
     block = continue_x(received, phase_tables(freq, refslow, lat, t))
-    block, (freq, classes, slow) = after(block, freq, tile_classes.reshape(32), slowness[0])
+    block, (freq, classes, slow) = after(block, freq, tile_classes.reshape(32), slow)
     received = exchange(block)
     count = lax.axis_size("depth")
     last = (lax.axis_index("depth") == count - 1).reshape(1).astype(jnp.int32)
     tabs = correction_tables(
         freq, refslow, classes, fd_coupling.reshape(32), last, slow, fd_blocks.reshape(1024, 32), t
     )
-    tabs, (slow,) = after(tabs, slow)
-    down = lax.ppermute(slow[:1], "lat", [(i + 1, i) for i in range(LAT - 1)])
-    up = lax.ppermute(slow[-1:], "lat", [(i, i + 1) for i in range(LAT - 1)])
-    result, real = correct(received, tabs, up, down, fresh[0], t)
+    result, real = correct(received, tabs, fresh[0], t)
     next_field = lax.ppermute(result, "depth", [(i, (i + 1) % count) for i in range(count)])
     return next_field[None, None], image + real[None]
 

time: 60 us -> 57 us (0.950)
  the two profiles are of different devices: /device:TPU:102 before, /device:TPU:1 now
where the time goes in v2:
time: 57 us; the launch traced here: 56.6 us
  starting transfers between devices  21.5 us (38%)
  waiting for transfers between devices  19.8 us (35%)
  Pallas kernels  10.4 us (18%)
  local copies, waits for them, and re-layouts  2.2 us (4%)
  between operations  2.05 us (4%)
  other arithmetic  0.67 us (1%)
    all_to_all x2, waiting for transfers between devices, exchange(): lax.all_to_all(blocks, 'lat', split_axis=0, concat_axis=0, tiled=True)  17.2 us
    all_to_all x2, starting transfers between devices, exchange(): lax.all_to_all(blocks, 'lat', split_axis=0, concat_axis=0, tiled=True)  16.5 us
    pallas_call x5, Pallas kernels, call(): pl.pallas_call(body, out_shape=outs, in_specs=[pl.BlockSpec(memory_space=...  10.4 us
    ppermute x1, starting transfers between devices, per_device(): lax.ppermute(result, 'depth', [(i, (i + 1) % count) for i in range(count)])  5.04 us
    ppermute x1, waiting for transfers between devices, per_device(): lax.ppermute(result, 'depth', [(i, (i + 1) % count) for i in range(count)])  2.64 us
    unnamed x22, local copies, waits for them, and re-layouts  2.11 us
  transfers between devices with their start and end apart: 3, of which 3 were waited for; matrix products, arithmetic and copies ran while one was open for 1% of the time, Pallas kernels for 5%

profile of v2, /device:TPU:1, one launch (start us, length us, event | category | flops | bytes accessed | tf_op | source)
XLA Modules:
  0.0 56.6 jit_solution(10782139269428034501)
XLA Ops:
  0.6 2.2 %shard_map.194 = f32[544,128]{1,0:T(8,128)} custom-call(f32[2,32,1024]{2,1,0:T(8,128)} %bitcast.23, f32[2,8,128]{2,1,0:T(8,128)} %constant.29.clone.twist_any.twist_ref, bf16[2,256,256]{2,1,0:T(8,128)(2,1)} %constant.30.clone.w1_any.w3_ref, f32[32,1024]{1,0:T(8,128)} %bitcast.19), custom_call_target="tpu_custom_call" | custom-call | bytes 942080 | tf_op jit(solution)/shard_map/pallas_call | solution.py:124
  2.8 11.9 %all-to-all-start = ((f32[32,1,2176]{2,1,0:T(1,128)}), f32[32,1,2176]{2,1,0:T(1,128)S(1)}, u32[]{:S(2)}, u32[]{:S(2)}) async-start(f32[32,1,2176]{2,1,0:T(1,128)} %bitcast.3), calls=%async_computation | async-start | bytes 557056 | tf_op jit(solution)/shard_map/all_to_all | solution.py:449
  16.0 1.3 %shard_map.195 = (f32[2,256,128]{2,1,0:T(8,128)S(1)}, bf16[4,2,256,256]{3,2,1,0:T(8,128)(2,1)S(1)}, f32[2,32,128]{2,1,0:T(8,128)S(1)}, bf16[256,128]{1,0:T(8,128)(2,1)S(1)}, bf16[32,256]{1,0:T(8,128)(2,1)S(1)}) custom-call(s32[1]{0:T(128)} %bitcast.15.freq_ref, f32[1]{0:T(128)S(6)} %copy.28.slow_ref.refslow_ref, s32[1]{0:T(128)} %bitcast.5.lat_ref, ...), custom_call_target="tpu_custom_call" | custom-call | bytes 2588684 | tf_op jit(solution)/shard_map/pallas_call | solution.py:124
  17.3 9.2 %all-to-all-done = f32[32,1,2176]{2,1,0:T(1,128)S(1)} async-done(((f32[32,1,2176]{2,1,0:T(1,128)}), f32[32,1,2176]{2,1,0:T(1,128)S(1)}, u32[]{:S(2)}, u32[]{:S(2)}) %all-to-all-start) | async-done | bytes 278560 | tf_op jit(solution)/shard_map/all_to_all | solution.py:449
  26.5 0.0 copy-start.2
  26.5 2.3 %shard_map.196 = f32[576,128]{1,0:T(8,128)} custom-call(f32[544,128]{1,0:T(8,128)S(1)} %bitcast.18, f32[2,256,128]{2,1,0:T(8,128)S(1)} %get-tuple-element.22.phase_ref, bf16[4,2,256,256]{3,2,1,0:T(8,128)(2,1)S(1)} %get-tuple-element.23.x_ref, f32[2,32,128]{2,1,0:T(8,128)S(1)} %get-tuple-element.24.twist_ref, ...), custom_call_target="tpu_custom_call" | custom-call | bytes 1998848 | tf_op jit(solution)/shard_map/pallas_call | solution.py:124
  28.9 0.0 copy-start.1
  28.9 0.0 copy-start.3
  28.9 4.6 %all-to-all-start.1 = ((f32[32,1,2304]{2,1,0:T(1,128)}), f32[32,1,2304]{2,1,0:T(1,128)S(1)}, u32[]{:S(2)}, u32[]{:S(2)}) async-start(f32[32,1,2304]{2,1,0:T(1,128)} %bitcast.7), calls=%async_computation.1 | async-start | bytes 589824 | tf_op jit(solution)/shard_map/all_to_all | solution.py:449
  33.5 0.0 copy-start.9
  33.5 0.7 %copy-done.9 = f32[16,2]{0,1:T(2,128)S(1)} copy-done((f32[16,2]{0,1:T(2,128)S(1)}, f32[16,2]{0,1:T(2,128)}, u32[]{:S(2)}) %copy-start.9) | copy-done | bytes 152
  34.1 0.1 copy.25
  34.2 0.1 reshape.45.coupling_ref
  34.3 0.0 copy-start.7
  34.3 0.0 copy-done.2
  34.3 0.0 copy-done.1
  34.3 0.0 copy-done.3
  34.4 0.6 copy-done.6
  34.9 0.1 copy-done.7
  35.0 1.5 %shard_map.197 = (f32[2,32,1024]{2,1,0:T(8,128)S(1)}, f32[8,1024]{1,0:T(8,128)S(1)}, bf16[2,8,64,256]{3,2,1,0:T(8,128)(2,1)S(1)}) custom-call(s32[1]{0:T(128)} %bitcast.16.freq_ref, f32[1]{0:T(128)S(6)} %copy.28.slow_ref.refslow_ref, s32[32]{0:T(128)S(1)} %bitcast.22, f32[32]{0:T(128)S(1)} %reshape.45.coupling_ref, s32[1]{0:T(128)} %bitcast.9.last_ref, ...), custom_call_target="tpu_custom_call" | custom-call | bytes 1155340 | tf_op jit(solution)/shard_map/pallas_call | solution.py:124
  36.5 0.0 copy-start.4
  36.5 7.9 %all-to-all-done.1 = f32[32,1,2304]{2,1,0:T(1,128)S(1)} async-done(((f32[32,1,2304]{2,1,0:T(1,128)}), f32[32,1,2304]{2,1,0:T(1,128)S(1)}, u32[]{:S(2)}, u32[]{:S(2)}) %all-to-all-start.1) | async-done | bytes 294944 | tf_op jit(solution)/shard_map/all_to_all | solution.py:449
  44.4 0.0 copy-done
  44.4 0.0 copy-done.5
  44.4 0.0 copy-done.4
  44.4 0.0 copy-start.8
  44.4 3.1 %shard_map.198 = (f32[2,32,1024]{2,1,0:T(8,128)S(1)}, f32[32,1024]{1,0:T(8,128)S(1)}) custom-call(f32[576,128]{1,0:T(8,128)S(1)} %bitcast.17, bf16[2,256,256]{2,1,0:T(8,128)(2,1)S(1)} %copy-done, f32[2,8,128]{2,1,0:T(8,128)S(1)} %copy-done.4, f32[2,32,1024]{2,1,0:T(8,128)S(1)} %get-tuple-element.31.lens_ref, f32[8,1024]{1,0:T(8,128)S(1)} %get-tuple-element.32.row_ref, ...), custom_call_target="tpu_custom_call" | custom-call | bytes 2138112 | tf_op jit(solution)/shard_map/pallas_call | solution.py:124
  47.6 5.0 %collective-permute-start = (f32[2,32,1024]{2,1,0:T(8,128)S(1)}, f32[2,32,1024]{2,1,0:T(8,128)S(1)}, u32[]{:S(2)}, u32[]{:S(2)}) collective-permute-start(f32[2,32,1024]{2,1,0:T(8,128)S(1)} %get-tuple-element.34), channel_id=1, source_target_pairs={{0,32},{32,64},{64,96},{96,128},{128,160},{160,192},{192,224},{224... | collective-permute-start | bytes 786440 | tf_op jit(solution)/shard_map/ppermute | solution.py:474
  52.6 0.0 copy-done.8
  52.6 0.7 %bitcast_add_fusion = f32[1,32,1024]{2,1,0:T(8,128)} fusion(f32[1,32,1024]{2,1,0:T(8,128)S(1)} %copy-done.8, f32[32,1024]{1,0:T(8,128)S(1)} %get-tuple-element.35), kind=kLoop, calls=%fused_computation | loop fusion | flops 32768 | bytes 393216 | tf_op jit(solution)/shard_map/add | solution.py:475
  53.3 2.6 %collective-permute-done = f32[2,32,1024]{2,1,0:T(8,128)S(1)} collective-permute-done((f32[2,32,1024]{2,1,0:T(8,128)S(1)}, f32[2,32,1024]{2,1,0:T(8,128)S(1)}, u32[]{:S(2)}, u32[]{:S(2)}) %collective-permute-start) | collective-permute-done | bytes 262176 | tf_op jit(solution)/shard_map/ppermute | solution.py:474
  55.9 0.7 %copy.29 = f32[1,1,2,32,1024]{4,3,2,1,0:T(8,128)} copy(f32[1,1,2,32,1024]{4,3,2,1,0:T(8,128)S(1)} %bitcast.24) | data formatting | bytes 524288
  (3 shorter events, 0.0 us)
Async XLA Ops:
  2.8 23.7 %all-to-all-start = ((f32[32,1,2176]{2,1,0:T(1,128)}), f32[32,1,2176]{2,1,0:T(1,128)S(1)}, u32[]{:S(2)}, u32[]{:S(2)}) async-start(f32[32,1,2176]{2,1,0:T(1,128)} %bitcast.3), calls=%async_computation | async-start | bytes 557056 | tf_op jit(solution)/shard_map/all_to_all | solution.py:449
  26.5 7.8 %copy-start.2 = (f32[16,2,32,32]{3,2,1,0:T(8,128)S(1)}, f32[16,2,32,32]{3,2,1,0:T(8,128)}, u32[]{:S(2)}) copy-start(f32[16,2,32,32]{3,2,1,0:T(8,128)} %param.25) | copy-start | bytes 393220
  28.9 5.5 %copy-start.1 = (f32[1,32,1024]{2,1,0:T(8,128)S(1)}, f32[1,32,1024]{2,1,0:T(8,128)}, u32[]{:S(2)}) copy-start(f32[1,32,1024]{2,1,0:T(8,128)} %param.23) | copy-start | bytes 393220
  28.9 5.5 %copy-start.3 = (bf16[4,32,256]{2,1,0:T(8,128)(2,1)S(1)}, bf16[4,32,256]{2,1,0:T(8,128)(2,1)}, u32[]{:S(2)}) copy-start(bf16[4,32,256]{2,1,0:T(8,128)(2,1)} %constant.35.clone.own_ref) | copy-start | bytes 196612
  28.9 15.6 %all-to-all-start.1 = ((f32[32,1,2304]{2,1,0:T(1,128)}), f32[32,1,2304]{2,1,0:T(1,128)S(1)}, u32[]{:S(2)}, u32[]{:S(2)}) async-start(f32[32,1,2304]{2,1,0:T(1,128)} %bitcast.7), calls=%async_computation.1 | async-start | bytes 589824 | tf_op jit(solution)/shard_map/all_to_all | solution.py:449
  33.5 0.7 %copy-start.9 = (f32[16,2]{0,1:T(2,128)S(1)}, f32[16,2]{0,1:T(2,128)}, u32[]{:S(2)}) copy-start(f32[16,2]{0,1:T(2,128)} %param.26) | copy-start | bytes 388
  34.2 0.7 %copy-start.6 = (bf16[32,128]{1,0:T(8,128)(2,1)S(1)}, bf16[32,128]{1,0:T(8,128)(2,1)}, u32[]{:S(2)}) copy-start(bf16[32,128]{1,0:T(8,128)(2,1)} %constant.36.clone.spread_ref) | copy-start | bytes 24580
  34.3 0.7 %copy-start.7 = (s32[1,1,32]{2,1,0:T(1,128)S(1)}, s32[1,1,32]{2,1,0:T(1,128)}, u32[]{:S(2)}) copy-start(s32[1,1,32]{2,1,0:T(1,128)} %param.24) | copy-start | bytes 388
  35.0 9.4 %copy-start = (bf16[2,256,256]{2,1,0:T(8,128)(2,1)S(1)}, bf16[2,256,256]{2,1,0:T(8,128)(2,1)}, u32[]{:S(2)}) copy-start(bf16[2,256,256]{2,1,0:T(8,128)(2,1)} %constant.30.clone.w1_any.w3_ref) | copy-start | bytes 786436
  35.0 9.4 %copy-start.5 = (bf16[128,128]{1,0:T(8,128)(2,1)S(1)}, bf16[128,128]{1,0:T(8,128)(2,1)}, u32[]{:S(2)}) copy-start(bf16[128,128]{1,0:T(8,128)(2,1)} %constant.37.clone.fold_ref) | copy-start | bytes 98308
  36.5 7.9 %copy-start.4 = (f32[2,8,128]{2,1,0:T(8,128)S(1)}, f32[2,8,128]{2,1,0:T(8,128)}, u32[]{:S(2)}) copy-start(f32[2,8,128]{2,1,0:T(8,128)} %constant.29.clone.twist_any.twist_ref) | copy-start | bytes 24580
  44.4 8.2 %copy-start.8 = (f32[1,32,1024]{2,1,0:T(8,128)S(1)}, f32[1,32,1024]{2,1,0:T(8,128)}, u32[]{:S(2)}) copy-start(f32[1,32,1024]{2,1,0:T(8,128)} %param.27) | copy-start | bytes 393220
  47.6 8.4 %collective-permute-start = (f32[2,32,1024]{2,1,0:T(8,128)S(1)}, f32[2,32,1024]{2,1,0:T(8,128)S(1)}, u32[]{:S(2)}, u32[]{:S(2)}) collective-permute-start(f32[2,32,1024]{2,1,0:T(8,128)S(1)} %get-tuple-element.34), channel_id=1, source_target_pairs={{0,32},{32,64},{64,96},{96,128},{128,160},{160,192},{192,224},{224... | collective-permute-start | bytes 786440 | tf_op jit(solution)/shard_map/ppermute | solution.py:474

commit v3 on v2

--- a/solution.py
+++ b/solution.py
@@ -87,7 +87,9 @@
 
 def product(left, right, dims=NN):
     dot = lambda a, b: lax.dot_general(a, b, dims, preferred_element_type=jnp.float32)
-    return dot(left[0], right[0]) + (dot(left[1], right[0]) + dot(left[0], right[1]))
+    rows = left[0].shape[0]
+    both = dot(jnp.concatenate(left, axis=0), right[0])
+    return both[:rows] + (both[rows:] + dot(left[0], right[1]))
 
 
 def cmul(a, b):
@@ -284,7 +286,7 @@
 
 def weights(
     freq_ref, refslow_ref, class_ref, coupling_ref, last_ref, slow_ref, blocks_ref, own_ref, spread_ref,
-    lens_ref, row_ref, mx_ref, wide_ref,
+    lens_ref, row_ref, mx_ref, my_ref, wide_ref,
 ):
     omega = 2.0 * math.pi * (LOW_HZ + STEP_HZ * freq_ref[0].astype(jnp.float32))
     base = refslow_ref[0]
@@ -294,8 +296,8 @@
         lens_ref[0, rows], lens_ref[1, rows] = cos * NORM, sin * NORM
     high, low = split(blocks_ref[...])
     dot = lambda a: lax.dot_general(a, spread_ref[...], NN, preferred_element_type=jnp.float32)
-    wide_ref[0] = dot(high).astype(jnp.bfloat16).reshape(16, 64, 128)
-    wide_ref[1] = dot(low).astype(jnp.bfloat16).reshape(16, 64, 128)
+    wide_ref[0] = dot(high).astype(jnp.bfloat16).reshape(2, 16, 64, 128)
+    wide_ref[1] = dot(low).astype(jnp.bfloat16).reshape(2, 16, 64, 128)
     row_ref[2:3] = jnp.full((1, N), omega)
     row_ref[3:4] = jnp.full((1, N), base)
     row_ref[4:5] = jnp.full((1, N), last_ref[0].astype(jnp.float32))
@@ -309,17 +311,24 @@
             row_ref[c : c + 1, g * 128 : g * 128 + 128] = beta
         for part in range(2):
             total = []
-            for c in range(2):
-                tiles = [wide_ref[part, classes[t], c * 32 : c * 32 + 32] * own_ref[t, :, :128] for t in range(4)]
-                total.append((tiles[0] + tiles[1]) + (tiles[2] + tiles[3]))
+            for turned in range(2):
+                for c in range(2):
+                    own = [
+                        wide_ref[part, turned, classes[t], c * 32 : c * 32 + 32] * own_ref[t, :, :128] for t in range(4)
+                    ]
+                    total.append((own[0] + own[1]) + (own[2] + own[3]))
             mx_ref[part, g, :32, :128] = total[0]
             mx_ref[part, g, :32, 128:] = -total[1]
             mx_ref[part, g, 32:, :128] = total[1]
             mx_ref[part, g, 32:, 128:] = total[0]
+            my_ref[part, g, :32, :128] = total[2]
+            my_ref[part, g, :32, 128:] = total[3]
+            my_ref[part, g, 32:, :128] = -total[3]
+            my_ref[part, g, 32:, 128:] = total[2]
 
 
 def finish(
-    in_ref, w3_ref, twist_ref, lens_ref, row_ref, mx_ref, own_ref, fold_ref, fresh_any,
+    in_ref, w3_ref, twist_ref, lens_ref, row_ref, mx_ref, my_ref, own_ref, fold_ref, fresh_any,
     out_ref, real_ref, mixed_ref, lensed_ref, rhs_ref, across_ref, fresh_ref, sem,
 ):
     copy = pltpu.make_async_copy(fresh_any, fresh_ref, sem)
@@ -365,22 +374,32 @@
                 pair = cmul(pair, [side_lens[side][c][n1 : n1 + 1] for c in range(2)])
                 for c in range(2):
                     lensed_ref[c, at : at + 1, lanes] = pair[c]
-    for g in range(8):
-        lanes = slice(g * 128, g * 128 + 128)
-        beta = (row_ref[0:1, lanes], row_ref[1:2, lanes])
-        mid = [lensed_ref[c, 8:40, lanes] for c in range(2)]
-        diff = tuple(
-            lensed_ref[c, 9:41, lanes] + lensed_ref[c, 7:39, lanes] - 2.0 * mid[c] for c in range(2)
-        )
-        more = cmul(diff, beta)
-        pieces = [split(mid[c] + more[c]) for c in range(2)]
+    for g in range(0, 8, 2):
+        pair = []
+        for lanes in (slice(g * 128, g * 128 + 128), slice(g * 128 + 128, g * 128 + 256)):
+            beta = (row_ref[0:1, lanes], row_ref[1:2, lanes])
+            mid = [lensed_ref[c, 8:40, lanes] for c in range(2)]
+            diff = tuple(
+                lensed_ref[c, 9:41, lanes] + lensed_ref[c, 7:39, lanes] - 2.0 * mid[c] for c in range(2)
+            )
+            more = cmul(diff, beta)
+            pair.append([split(mid[c] + more[c]) for c in range(2)])
         rhs = [
-            jnp.concatenate([pieces[c][part] * own_ref[t, :, :128] for c in range(2) for t in range(4)], axis=0)
+            jnp.concatenate(
+                [
+                    jnp.concatenate([pieces[c][part] * own_ref[t, :, :128] for pieces in pair], axis=1)
+                    for c in range(2)
+                    for t in range(4)
+                ],
+                axis=0,
+            )
             for part in range(2)
         ]
-        out = product((mx_ref[0, g], mx_ref[1, g]), rhs)
-        across_ref[0, :, lanes] = out[:32]
-        across_ref[1, :, lanes] = out[32:]
+        left = [jnp.concatenate([mx_ref[part, g], mx_ref[part, g + 1]], axis=0) for part in range(2)]
+        out = product(left, rhs)
+        for c in range(2):
+            across_ref[c, :, g * 128 : g * 128 + 128] = out[c * 32 : c * 32 + 32, :128]
+            across_ref[c, :, g * 128 + 128 : g * 128 + 256] = out[64 + c * 32 : 96 + c * 32, 128:]
     lane = lax.broadcasted_iota(jnp.int32, (32, N), 1)
     diff = []
     for c in range(2):
@@ -397,11 +416,11 @@
         rhs = jnp.concatenate([rhs_ref[0, :, lanes], rhs_ref[1, :, lanes]], axis=1)
         tiles = [
             jnp.concatenate(
-                [mx_ref[part, g, c * 32 : c * 32 + 32] * own_ref[t] for c in range(2) for t in range(4)], axis=0
+                [my_ref[part, g, c * 32 : c * 32 + 32] * own_ref[t] for c in range(2) for t in range(4)], axis=0
             )
             for part in range(2)
         ]
-        out = product(split(rhs), tiles, NT)
+        out = product(split(rhs), tiles, NN)
         real_ref[:, lanes] = out[:, :128]
         last = row_ref[4:5, lanes] > 0.5
         for c in range(2):
@@ -430,8 +449,8 @@
 
 def correction_tables(freq, refslow, classes, coupling, last, slow, blocks, t):
     half = jnp.bfloat16
-    outs = [shape(2, 32, N), shape(8, N), shape(2, 8, 64, 256, dtype=half)]
-    scratch = [pltpu.VMEM((2, 16, 64, 128), half)]
+    outs = [shape(2, 32, N), shape(8, N), shape(2, 8, 64, 256, dtype=half), shape(2, 8, 64, 256, dtype=half)]
+    scratch = [pltpu.VMEM((2, 2, 16, 64, 128), half)]
     args = [freq, refslow, classes, coupling, last, slow, blocks, t["own"], t["spread"]]
     return call(weights, outs, scratch, args, scalars=(0, 1, 2, 3, 4))
 
@@ -441,7 +460,7 @@
     scratch = [pltpu.VMEM((320, 256), jnp.float32), pltpu.VMEM((2, 48, N), jnp.float32)]
     scratch += [plane, plane, plane, pltpu.SemaphoreType.DMA]
     args = [block, t["w3"], t["twist_y"], *tabs, t["own"], t["fold"], fresh]
-    return call(finish, [shape(2, 32, N), shape(32, N)], scratch, args, large=(8,))
+    return call(finish, [shape(2, 32, N), shape(32, N)], scratch, args, large=(9,))
 
 
 def exchange(block):
@@ -459,7 +478,7 @@
     t = tables()
     slow = slowness[0]
     block = spread_y(field.reshape(2, 32, N), slow, t)
-    block, (freq, refslow) = after(block, freq_index.reshape(1), ref_slowness)
+    block, (freq, refslow, blocks) = after(block, freq_index.reshape(1), ref_slowness, fd_blocks)
     received = exchange(block)
     lat = lax.axis_index("lat").reshape(1).astype(jnp.int32)
     block = continue_x(received, phase_tables(freq, refslow, lat, t))
@@ -467,9 +486,8 @@
     received = exchange(block)
     count = lax.axis_size("depth")
     last = (lax.axis_index("depth") == count - 1).reshape(1).astype(jnp.int32)
-    tabs = correction_tables(
-        freq, refslow, classes, fd_coupling.reshape(32), last, slow, fd_blocks.reshape(1024, 32), t
-    )
+    blocks = jnp.stack([blocks, jnp.swapaxes(blocks, 2, 3)]).reshape(2048, 32)
+    tabs = correction_tables(freq, refslow, classes, fd_coupling.reshape(32), last, slow, blocks, t)
     result, real = correct(received, tabs, fresh[0], t)
     next_field = lax.ppermute(result, "depth", [(i, (i + 1) % count) for i in range(count)])
     return next_field[None, None], image + real[None]

time: 57 us -> 55.6 us (0.975)
  Pallas kernels: 10.4 us -> 9.31 us
    pallas_call x5, Pallas kernels: 10.4 us -> 9.31 us  [call(): pl.pallas_call(body, out_shape=outs, in_specs=[pl.BlockSpec(memory_space=...]
  transfers between devices with their start and end apart: 3 -> 3, of which waited for: 3 -> 3; matrix products, arithmetic and copies ran while one was open for 1% -> 2% of each run, Pallas kernels for 5% -> 6%
where the time goes in v3:
time: 55.6 us; the launch traced here: 55.2 us
  starting transfers between devices  21.5 us (39%)
  waiting for transfers between devices  19.7 us (35%)
  Pallas kernels  9.31 us (17%)
  between operations  2.09 us (4%)
  local copies, waits for them, and re-layouts  1.89 us (3%)
  other arithmetic  0.76 us (1%)
    all_to_all x2, waiting for transfers between devices, exchange(): lax.all_to_all(blocks, 'lat', split_axis=0, concat_axis=0, tiled=True)  17 us
    all_to_all x2, starting transfers between devices, exchange(): lax.all_to_all(blocks, 'lat', split_axis=0, concat_axis=0, tiled=True)  16.5 us
    pallas_call x5, Pallas kernels, call(): pl.pallas_call(body, out_shape=outs, in_specs=[pl.BlockSpec(memory_space=...  9.31 us
    ppermute x1, starting transfers between devices, per_device(): lax.ppermute(result, 'depth', [(i, (i + 1) % count) for i in range(count)])  5.05 us
    ppermute x1, waiting for transfers between devices, per_device(): lax.ppermute(result, 'depth', [(i, (i + 1) % count) for i in range(count)])  2.64 us
    unnamed x22, local copies, waits for them, and re-layouts  1.6 us
  transfers between devices with their start and end apart: 3, of which 3 were waited for; matrix products, arithmetic and copies ran while one was open for 2% of the time, Pallas kernels for 6%

profile of v3, /device:TPU:1, one launch (start us, length us, event | category | flops | bytes accessed | tf_op | source)
XLA Modules:
  0.0 55.2 jit_solution(6814341995720390623)
XLA Ops:
  0.6 2.2 %shard_map.194 = f32[544,128]{1,0:T(8,128)} custom-call(f32[2,32,1024]{2,1,0:T(8,128)} %bitcast.29, f32[2,8,128]{2,1,0:T(8,128)} %constant.29.clone.twist_any.twist_ref, bf16[2,256,256]{2,1,0:T(8,128)(2,1)} %constant.30.clone.w1_any.w3_ref, f32[32,1024]{1,0:T(8,128)} %bitcast.24), custom_call_target="tpu_custom_call" | custom-call | bytes 942080 | tf_op jit(solution)/shard_map/pallas_call | solution.py:126
  2.9 11.9 %all-to-all-start = ((f32[32,1,2176]{2,1,0:T(1,128)}), f32[32,1,2176]{2,1,0:T(1,128)S(1)}, u32[]{:S(2)}, u32[]{:S(2)}) async-start(f32[32,1,2176]{2,1,0:T(1,128)} %bitcast.3), calls=%async_computation | async-start | bytes 557056 | tf_op jit(solution)/shard_map/all_to_all | solution.py:468
  16.0 1.3 %shard_map.195 = (f32[2,256,128]{2,1,0:T(8,128)S(1)}, bf16[4,2,256,256]{3,2,1,0:T(8,128)(2,1)S(1)}, f32[2,32,128]{2,1,0:T(8,128)S(1)}, bf16[256,128]{1,0:T(8,128)(2,1)S(1)}, bf16[32,256]{1,0:T(8,128)(2,1)S(1)}) custom-call(s32[1]{0:T(128)} %bitcast.19.freq_ref, f32[1]{0:T(128)S(6)} %copy.31.slow_ref.refslow_ref, s32[1]{0:T(128)} %bitcast.5.lat_ref, ...), custom_call_target="tpu_custom_call" | custom-call | bytes 2588684 | tf_op jit(solution)/shard_map/pallas_call | solution.py:126
  17.3 9.2 %all-to-all-done = f32[32,1,2176]{2,1,0:T(1,128)S(1)} async-done(((f32[32,1,2176]{2,1,0:T(1,128)}), f32[32,1,2176]{2,1,0:T(1,128)S(1)}, u32[]{:S(2)}, u32[]{:S(2)}) %all-to-all-start) | async-done | bytes 278560 | tf_op jit(solution)/shard_map/all_to_all | solution.py:468
  26.6 2.3 %shard_map.196 = f32[576,128]{1,0:T(8,128)} custom-call(f32[544,128]{1,0:T(8,128)S(1)} %bitcast.23, f32[2,256,128]{2,1,0:T(8,128)S(1)} %get-tuple-element.24.phase_ref, bf16[4,2,256,256]{3,2,1,0:T(8,128)(2,1)S(1)} %get-tuple-element.25.x_ref, f32[2,32,128]{2,1,0:T(8,128)S(1)} %get-tuple-element.26.twist_ref, ...), custom_call_target="tpu_custom_call" | custom-call | bytes 1998848 | tf_op jit(solution)/shard_map/pallas_call | solution.py:126
  28.9 4.6 %all-to-all-start.1 = ((f32[32,1,2304]{2,1,0:T(1,128)}), f32[32,1,2304]{2,1,0:T(1,128)S(1)}, u32[]{:S(2)}, u32[]{:S(2)}) async-start(f32[32,1,2304]{2,1,0:T(1,128)} %bitcast.7), calls=%async_computation.1 | async-start | bytes 589824 | tf_op jit(solution)/shard_map/all_to_all | solution.py:468
  33.5 0.0 copy-done.9
  33.5 0.1 copy.27
  33.6 0.1 reshape.45.coupling_ref
  33.7 0.0 copy-done.7
  33.7 0.2 copy.28
  33.9 0.0 copy-start.1
  33.9 0.0 copy-start.2
  33.9 0.0 copy-start.5
  33.9 0.1 pad_maximum_fusion
  34.0 0.0 copy-start.6
  34.0 0.8 %copy-done.1 = f32[1,32,1024]{2,1,0:T(8,128)S(1)} copy-done((f32[1,32,1024]{2,1,0:T(8,128)S(1)}, f32[1,32,1024]{2,1,0:T(8,128)}, u32[]{:S(2)}) %copy-start.1) | copy-done | bytes 131096
  34.8 0.0 copy-done.2
  34.8 0.0 copy-done.5
  34.8 0.0 copy-done.6
  34.8 0.0 copy-start.3
  34.8 1.8 %shard_map.197 = (f32[2,32,1024]{2,1,0:T(8,128)S(1)}, f32[8,1024]{1,0:T(8,128)S(1)}, bf16[2,8,64,256]{3,2,1,0:T(8,128)(2,1)S(1)}, bf16[2,8,64,256]{3,2,1,0:T(8,128)(2,1)S(1)}) custom-call(s32[1]{0:T(128)} %bitcast.20.freq_ref, f32[1]{0:T(128)S(6)} %copy.31.slow_ref.refslow_ref, s32[32]{0:T(128)S(1)} %bitcast.26, f32[32]{0:T(128)S(1)} %reshape.45.coupling_ref, ...), custom_call_target="tpu_custom_call" | custom-call | bytes 1810700 | tf_op jit(solution)/shard_map/pallas_call | solution.py:126
  36.6 0.0 copy-start.4
  36.6 7.8 %all-to-all-done.1 = f32[32,1,2304]{2,1,0:T(1,128)S(1)} async-done(((f32[32,1,2304]{2,1,0:T(1,128)}), f32[32,1,2304]{2,1,0:T(1,128)S(1)}, u32[]{:S(2)}, u32[]{:S(2)}) %all-to-all-start.1) | async-done | bytes 294944 | tf_op jit(solution)/shard_map/all_to_all | solution.py:468
  44.4 0.0 copy-done.3
  44.4 0.0 copy-start.8
  44.5 1.7 %shard_map.198 = (f32[2,32,1024]{2,1,0:T(8,128)S(1)}, f32[32,1024]{1,0:T(8,128)S(1)}) custom-call(f32[576,128]{1,0:T(8,128)S(1)} %bitcast.22, bf16[2,256,256]{2,1,0:T(8,128)(2,1)S(1)} %copy-done, f32[2,8,128]{2,1,0:T(8,128)S(1)} %copy-done.4, f32[2,32,1024]{2,1,0:T(8,128)S(1)} %get-tuple-element.34.lens_ref, f32[8,1024]{1,0:T(8,128)S(1)} %get-tuple-element.35.row_ref, ...), custom_call_target="tpu_custom_call" | custom-call | bytes 2662400 | tf_op jit(solution)/shard_map/pallas_call | solution.py:126
  46.2 5.1 %collective-permute-start = (f32[2,32,1024]{2,1,0:T(8,128)S(1)}, f32[2,32,1024]{2,1,0:T(8,128)S(1)}, u32[]{:S(2)}, u32[]{:S(2)}) collective-permute-start(f32[2,32,1024]{2,1,0:T(8,128)S(1)} %get-tuple-element.38), channel_id=1, source_target_pairs={{0,32},{32,64},{64,96},{96,128},{128,160},{160,192},{192,224},{224... | collective-permute-start | bytes 786440 | tf_op jit(solution)/shard_map/ppermute | solution.py:492
  51.2 0.0 copy-done.8
  51.2 0.7 %bitcast_add_fusion = f32[1,32,1024]{2,1,0:T(8,128)} fusion(f32[1,32,1024]{2,1,0:T(8,128)S(1)} %copy-done.8, f32[32,1024]{1,0:T(8,128)S(1)} %get-tuple-element.39), kind=kLoop, calls=%fused_computation.1 | loop fusion | flops 32768 | bytes 393216 | tf_op jit(solution)/shard_map/add | solution.py:493
  51.9 2.6 %collective-permute-done = f32[2,32,1024]{2,1,0:T(8,128)S(1)} collective-permute-done((f32[2,32,1024]{2,1,0:T(8,128)S(1)}, f32[2,32,1024]{2,1,0:T(8,128)S(1)}, u32[]{:S(2)}, u32[]{:S(2)}) %collective-permute-start) | collective-permute-done | bytes 262176 | tf_op jit(solution)/shard_map/ppermute | solution.py:492
  54.5 0.7 %copy.32 = f32[1,1,2,32,1024]{4,3,2,1,0:T(8,128)} copy(f32[1,1,2,32,1024]{4,3,2,1,0:T(8,128)S(1)} %bitcast.31) | data formatting | bytes 524288
  (5 shorter events, 0.0 us)
Async XLA Ops:
  2.9 23.7 %all-to-all-start = ((f32[32,1,2176]{2,1,0:T(1,128)}), f32[32,1,2176]{2,1,0:T(1,128)S(1)}, u32[]{:S(2)}, u32[]{:S(2)}) async-start(f32[32,1,2176]{2,1,0:T(1,128)} %bitcast.3), calls=%async_computation | async-start | bytes 557056 | tf_op jit(solution)/shard_map/all_to_all | solution.py:468
  28.9 4.8 %copy-start.7 = (f32[16,2,32,32]{3,2,1,0:T(8,128)S(1)}, f32[16,2,32,32]{3,2,1,0:T(8,128)}, u32[]{:S(2)}) copy-start(f32[16,2,32,32]{3,2,1,0:T(8,128)} %param.25) | copy-start | bytes 393220
  28.9 4.6 %copy-start.9 = (f32[16,2]{0,1:T(2,128)S(1)}, f32[16,2]{0,1:T(2,128)}, u32[]{:S(2)}) copy-start(f32[16,2]{0,1:T(2,128)} %param.26) | copy-start | bytes 388
  28.9 15.5 %all-to-all-start.1 = ((f32[32,1,2304]{2,1,0:T(1,128)}), f32[32,1,2304]{2,1,0:T(1,128)S(1)}, u32[]{:S(2)}, u32[]{:S(2)}) async-start(f32[32,1,2304]{2,1,0:T(1,128)} %bitcast.7), calls=%async_computation.1 | async-start | bytes 589824 | tf_op jit(solution)/shard_map/all_to_all | solution.py:468
  33.9 0.9 %copy-start.1 = (f32[1,32,1024]{2,1,0:T(8,128)S(1)}, f32[1,32,1024]{2,1,0:T(8,128)}, u32[]{:S(2)}) copy-start(f32[1,32,1024]{2,1,0:T(8,128)} %param.23) | copy-start | bytes 393220
  33.9 0.9 %copy-start.2 = (bf16[4,32,256]{2,1,0:T(8,128)(2,1)S(1)}, bf16[4,32,256]{2,1,0:T(8,128)(2,1)}, u32[]{:S(2)}) copy-start(bf16[4,32,256]{2,1,0:T(8,128)(2,1)} %constant.35.clone.own_ref) | copy-start | bytes 196612
  33.9 0.9 %copy-start.5 = (bf16[32,128]{1,0:T(8,128)(2,1)S(1)}, bf16[32,128]{1,0:T(8,128)(2,1)}, u32[]{:S(2)}) copy-start(bf16[32,128]{1,0:T(8,128)(2,1)} %constant.36.clone.spread_ref) | copy-start | bytes 24580
  34.0 0.8 %copy-start.6 = (s32[1,1,32]{2,1,0:T(1,128)S(1)}, s32[1,1,32]{2,1,0:T(1,128)}, u32[]{:S(2)}) copy-start(s32[1,1,32]{2,1,0:T(1,128)} %param.24) | copy-start | bytes 388
  34.8 9.6 %copy-start = (bf16[2,256,256]{2,1,0:T(8,128)(2,1)S(1)}, bf16[2,256,256]{2,1,0:T(8,128)(2,1)}, u32[]{:S(2)}) copy-start(bf16[2,256,256]{2,1,0:T(8,128)(2,1)} %constant.30.clone.w1_any.w3_ref) | copy-start | bytes 786436
  34.8 9.6 %copy-start.3 = (bf16[128,128]{1,0:T(8,128)(2,1)S(1)}, bf16[128,128]{1,0:T(8,128)(2,1)}, u32[]{:S(2)}) copy-start(bf16[128,128]{1,0:T(8,128)(2,1)} %constant.37.clone.fold_ref) | copy-start | bytes 98308
  36.6 7.8 %copy-start.4 = (f32[2,8,128]{2,1,0:T(8,128)S(1)}, f32[2,8,128]{2,1,0:T(8,128)}, u32[]{:S(2)}) copy-start(f32[2,8,128]{2,1,0:T(8,128)} %constant.29.clone.twist_any.twist_ref) | copy-start | bytes 24580
  44.4 6.8 %copy-start.8 = (f32[1,32,1024]{2,1,0:T(8,128)S(1)}, f32[1,32,1024]{2,1,0:T(8,128)}, u32[]{:S(2)}) copy-start(f32[1,32,1024]{2,1,0:T(8,128)} %param.27) | copy-start | bytes 393220
  46.2 8.4 %collective-permute-start = (f32[2,32,1024]{2,1,0:T(8,128)S(1)}, f32[2,32,1024]{2,1,0:T(8,128)S(1)}, u32[]{:S(2)}, u32[]{:S(2)}) collective-permute-start(f32[2,32,1024]{2,1,0:T(8,128)S(1)} %get-tuple-element.38), channel_id=1, source_target_pairs={{0,32},{32,64},{64,96},{96,128},{128,160},{160,192},{192,224},{224... | collective-permute-start | bytes 786440 | tf_op jit(solution)/shard_map/ppermute | solution.py:492

commit v4 on v3

--- a/solution.py
+++ b/solution.py
@@ -40,36 +40,32 @@
     w3 = line.transpose(2, 1, 3, 0, 4).reshape(256, 256)
     grid = 2 * np.pi * (small[:, None] * small % 32) / 32
     eye4 = np.eye(4)
-    a1 = np.einsum("dcqi,kl->dkqicl", rotation(-grid), eye4).reshape(256, 256)
-    a2 = np.einsum("dciq,kl->idkclq", rotation(grid), eye4).reshape(256, 256)
+    peers = []
+    for sign in (-1, 1):
+        high, low = parts(rotation(sign * grid).transpose(0, 2, 1, 3).reshape(64, 64))
+        peers.append(np.concatenate([high, high, low], axis=1))
     b1 = np.einsum("dcxp,kl->ckxdlp", rotation(-grid), eye4).reshape(256, 256)
     b2 = np.einsum("dcpx,kl->ckpdlx", rotation(grid), eye4).reshape(256, 256)
     ty = 2 * np.pi * np.arange(8)[:, None] * n2 / N
     tx = np.tile(2 * np.pi * small[:, None] * small / N, (1, 4))
     twist_y = np.stack([np.cos(ty), np.sin(ty)]).astype(np.float32)
     twist_x = np.stack([np.cos(tx), np.sin(tx)]).astype(np.float32)
-    edge = np.zeros((8, 32, 8, 8, 2))
-    fold = np.zeros((8, 8, 2, 16, 8))
+    fold = np.zeros((4, 8, 2, 2, 16, 8))
     for k1 in range(8):
-        edge[k1, 31, :, k1, 0] = 1
-        edge[k1, 0, :, k1, 1] = 1
         for side in range(2):
-            fold[:, k1, side, k1, side] = 1
-    edge = edge.reshape(256, 128).astype(ml_dtypes.bfloat16)
+            fold[k1 % 4, :, k1 // 4, side, k1, side] = 1
     fold = fold.reshape(128, 128).astype(ml_dtypes.bfloat16)
-    gather = np.repeat(np.eye(32), 8, axis=1).astype(ml_dtypes.bfloat16)
     own = (np.arange(128)[None, :] // 32 == np.arange(4)[:, None]).astype(np.float32)
     own = np.broadcast_to(np.tile(own, (1, 2))[:, None, :], (4, 32, 256)).astype(ml_dtypes.bfloat16)
     spread = np.tile(np.eye(32), (1, 4)).astype(ml_dtypes.bfloat16)
     return {
         "w1": parts(w1),
         "w3": parts(w3),
-        "x": np.stack([parts(a1), parts(b1), parts(b2), parts(a2)]),
+        "x": np.stack([parts(b1), parts(b2)]),
+        "peers": np.stack(peers),
         "twist_y": twist_y,
         "twist_x": twist_x,
-        "edge": edge,
         "fold": fold,
-        "gather": gather,
         "own": own,
         "spread": spread,
     }
@@ -198,11 +194,8 @@
     return jnp.cos(angle), jnp.sin(angle)
 
 
-def phases(
-    freq_ref, slow_ref, lat_ref, x_any, twist_any, edge_any, gather_any,
-    out_ref, x_ref, twist_ref, edge_ref, gather_ref, sems,
-):
-    copies = fetch([x_any, twist_any, edge_any, gather_any], [x_ref, twist_ref, edge_ref, gather_ref], sems)
+def phases(freq_ref, slow_ref, lat_ref, x_any, peers_any, twist_any, out_ref, x_ref, peers_ref, twist_ref, sems):
+    copies = fetch([x_any, peers_any, twist_any], [x_ref, peers_ref, twist_ref], sems)
     omega = 2.0 * math.pi * (LOW_HZ + STEP_HZ * freq_ref[0].astype(jnp.float32))
     reach = omega * slow_ref[0]
     scale = 2.0 * math.pi / (N * SPACING_KM)
@@ -231,9 +224,18 @@
     ]
 
 
-def along_x(in_ref, phase_ref, x_ref, twist_ref, edge_ref, gather_ref, out_ref, high_ref, low_ref):
-    lines = jnp.concatenate(both_tiles(in_ref, FIRST), axis=1)
-    mixed = product((x_ref[0, 0], x_ref[0, 1]), split(lines))
+def along_x(in_ref, phase_ref, x_ref, peers_ref, twist_ref, out_ref, high_ref, low_ref, back_ref):
+    dot = lambda a, b: lax.dot_general(a, b, NN, preferred_element_type=jnp.float32)
+    blocks = [(h, k2l) for h in range(2) for k2l in range(4)]
+    lines = jnp.concatenate(
+        [
+            jnp.concatenate([in_ref[pl.ds(h * 8 + c * 4 + k2l, LAT, stride=FIRST), :] for h, k2l in blocks], axis=1)
+            for c in range(2)
+        ],
+        axis=0,
+    )
+    high, low = split(lines)
+    mixed = dot(peers_ref[0], jnp.concatenate([high, low, high], axis=0))
     cos, sin = twist_ref[0], twist_ref[1]
 
     def put(at, value):
@@ -242,39 +244,32 @@
             high_ref[at, c * 128 : c * 128 + 128] = high
             low_ref[at, c * 128 : c * 128 + 128] = low
 
-    for h in range(2):
-        lanes = slice(h * 128, h * 128 + 128)
-        for k2l in range(4):
-            value = (mixed[k2l * 32 : k2l * 32 + 32, lanes], mixed[128 + k2l * 32 : 160 + k2l * 32, lanes])
-            top = (h * 4 + k2l) * 32
-            put(slice(top, top + 32), cmul(value, (cos, -sin)))
-    spectrum = product((high_ref[...], low_ref[...]), (x_ref[1, 0], x_ref[1, 1]))
+    for block in range(8):
+        lanes = slice(block * 128, block * 128 + 128)
+        put(slice(block * 32, block * 32 + 32), cmul((mixed[:32, lanes], mixed[32:, lanes]), (cos, -sin)))
+    spectrum = product((high_ref[...], low_ref[...]), (x_ref[0, 0], x_ref[0, 1]))
     for block in range(8):
         rows = slice(block * 32, block * 32 + 32)
         value = (spectrum[rows, :128], spectrum[rows, 128:])
         put(rows, cmul(value, (phase_ref[0, rows], phase_ref[1, rows])))
-    mixed = product((high_ref[...], low_ref[...]), (x_ref[2, 0], x_ref[2, 1]))
-    for h in range(2):
-        for k2l in range(4):
-            rows = slice((h * 4 + k2l) * 32, (h * 4 + k2l) * 32 + 32)
-            value = cmul((mixed[rows, :128], mixed[rows, 128:]), (cos, sin))
-            for c in range(2):
-                high, low = split(value[c])
-                at = slice(c * 128 + k2l * 32, c * 128 + k2l * 32 + 32)
-                high_ref[at, h * 128 : h * 128 + 128] = high
-                low_ref[at, h * 128 : h * 128 + 128] = low
-    out = product((x_ref[3, 0], x_ref[3, 1]), (high_ref[...], low_ref[...]))
-    for i in range(LAT):
-        for half in range(2):
-            top = SECOND * i + half * 8
-            out_ref[top : top + 8] = out[i * 8 : i * 8 + 8, half * 128 : half * 128 + 128]
-    dot = lambda a, b: lax.dot_general(a, b, NN, preferred_element_type=jnp.float32)
-    high, low = split(out)
-    edge = dot(high, edge_ref[...]) + dot(low, edge_ref[...])
-    own = lane_of((256, 128)) // 16 == lax.broadcasted_iota(jnp.int32, (256, 128), 0) % 8
-    high, low = split(jnp.where(own, edge, 0.0))
-    edge = dot(gather_ref[...], high) + dot(gather_ref[...], low)
+    mixed = product((high_ref[...], low_ref[...]), (x_ref[1, 0], x_ref[1, 1]))
+    for block in range(8):
+        rows, lanes = slice(block * 32, block * 32 + 32), slice(block * 128, block * 128 + 128)
+        value = cmul((mixed[rows, :128], mixed[rows, 128:]), (cos, sin))
+        for c in range(2):
+            high, low = split(value[c])
+            for at, piece in enumerate((high, low, high)):
+                back_ref[at * 64 + c * 32 : at * 64 + c * 32 + 32, lanes] = piece
+    out = dot(peers_ref[1], back_ref[...])
     lane, row = lane_of((LAT, 128)), lax.broadcasted_iota(jnp.int32, (LAT, 128), 0)
+    edge = jnp.zeros((LAT, 128), jnp.float32)
+    for block, (h, k2l) in enumerate(blocks):
+        for c in range(2):
+            piece = out[c * 32 : c * 32 + 32, block * 128 : block * 128 + 128]
+            out_ref[pl.ds(h * 8 + c * 4 + k2l, LAT, stride=SECOND), :] = piece
+            at = (c * 4 + k2l) * 4 + h * 2
+            edge = jnp.where(lane % 32 == at, pltpu.roll(piece, (at - 31) % 128, 1), edge)
+            edge = jnp.where(lane % 32 == at + 1, pltpu.roll(piece, at + 1, 1), edge)
     before = jnp.where(row == 0, 0.0, pltpu.roll(edge, 1, 0))
     after = jnp.where(row == LAT - 1, 0.0, pltpu.roll(edge, LAT - 1, 0))
     out_ref[pl.ds(16, LAT, stride=SECOND), :] = jnp.where(lane % 2 == 0, before, after)
@@ -347,7 +342,7 @@
     beside = jnp.concatenate(
         [jnp.broadcast_to(in_ref[SECOND * j + 16 : SECOND * j + 17], (8, 128)) for j in range(LAT)], axis=0
     )
-    own = lane_of((256, 128)) // 16 == lax.broadcasted_iota(jnp.int32, (256, 128), 0) % 8
+    own = lane_of((256, 128)) % 32 // 4 == lax.broadcasted_iota(jnp.int32, (256, 128), 0) % 8
     high, low = split(jnp.where(own, beside, 0.0))
     dot = lambda a: lax.dot_general(a, fold_ref[...], NN, preferred_element_type=jnp.float32)
     lines = [*both_tiles(in_ref, SECOND), dot(high) + dot(low)]
@@ -437,13 +432,13 @@
 
 
 def phase_tables(freq, refslow, lat, t):
-    args = [freq, refslow, lat, t["x"], t["twist_x"], t["edge"], t["gather"]]
+    args = [freq, refslow, lat, t["x"], t["peers"], t["twist_x"]]
     outs = [shape(2, 256, 128)] + [jax.ShapeDtypeStruct(a.shape, a.dtype) for a in args[3:]]
-    return call(phases, outs, [pltpu.SemaphoreType.DMA((4,))], args, scalars=(0, 1, 2), large=(3, 4, 5, 6))
+    return call(phases, outs, [pltpu.SemaphoreType.DMA((3,))], args, scalars=(0, 1, 2), large=(3, 4, 5))
 
 
 def continue_x(block, tabs):
-    scratch = [pltpu.VMEM((256, 256), jnp.bfloat16)] * 2
+    scratch = [pltpu.VMEM((256, 256), jnp.bfloat16)] * 2 + [pltpu.VMEM((192, N), jnp.bfloat16)]
     return call(along_x, [shape(LAT * SECOND, 128)], scratch, [block, *tabs])[0]
 
 

time: 55.6 us -> 55.1 us (level)
  Pallas kernels: 9.31 us -> 8.65 us
  local copies, waits for them, and re-layouts: 1.89 us -> 2.55 us
    unnamed x22, local copies, waits for them, and re-layouts: 1.6 us -> 2.27 us
    pallas_call x5, Pallas kernels: 9.31 us -> 8.65 us  [call(): pl.pallas_call(body, out_shape=outs, in_specs=[pl.BlockSpec(memory_space=...]
  transfers between devices with their start and end apart: 3 -> 3, of which waited for: 3 -> 3; matrix products, arithmetic and copies ran while one was open for 2% -> 2% of each run, Pallas kernels for 6% -> 5%
where the time goes in v4:
time: 55.1 us; the launch traced here: 54.8 us
  starting transfers between devices  21.5 us (39%)
  waiting for transfers between devices  19.2 us (35%)
  Pallas kernels  8.65 us (16%)
  local copies, waits for them, and re-layouts  2.55 us (5%)
  between operations  2.09 us (4%)
  other arithmetic  0.76 us (1%)
    all_to_all x2, waiting for transfers between devices, exchange(): lax.all_to_all(blocks, 'lat', split_axis=0, concat_axis=0, tiled=True)  16.6 us
    all_to_all x2, starting transfers between devices, exchange(): lax.all_to_all(blocks, 'lat', split_axis=0, concat_axis=0, tiled=True)  16.5 us
    pallas_call x5, Pallas kernels, call(): pl.pallas_call(body, out_shape=outs, in_specs=[pl.BlockSpec(memory_space=...  8.65 us
    ppermute x1, starting transfers between devices, per_device(): lax.ppermute(result, 'depth', [(i, (i + 1) % count) for i in range(count)])  5.05 us
    ppermute x1, waiting for transfers between devices, per_device(): lax.ppermute(result, 'depth', [(i, (i + 1) % count) for i in range(count)])  2.64 us
    unnamed x22, local copies, waits for them, and re-layouts  2.27 us
  transfers between devices with their start and end apart: 3, of which 3 were waited for; matrix products, arithmetic and copies ran while one was open for 2% of the time, Pallas kernels for 5%

profile of v4, /device:TPU:1, one launch (start us, length us, event | category | flops | bytes accessed | tf_op | source)
XLA Modules:
  0.0 54.8 jit_solution(6566425071933734301)
XLA Ops:
  0.6 2.2 %shard_map.185 = f32[544,128]{1,0:T(8,128)} custom-call(f32[2,32,1024]{2,1,0:T(8,128)} %bitcast.29, f32[2,8,128]{2,1,0:T(8,128)} %constant.27.clone.twist_any.twist_ref, bf16[2,256,256]{2,1,0:T(8,128)(2,1)} %constant.28.clone.w1_any.w3_ref, f32[32,1024]{1,0:T(8,128)} %bitcast.24), custom_call_target="tpu_custom_call" | custom-call | bytes 942080 | tf_op jit(solution)/shard_map/pallas_call | solution.py:122
  2.9 11.9 %all-to-all-start = ((f32[32,1,2176]{2,1,0:T(1,128)}), f32[32,1,2176]{2,1,0:T(1,128)S(1)}, u32[]{:S(2)}, u32[]{:S(2)}) async-start(f32[32,1,2176]{2,1,0:T(1,128)} %bitcast.3), calls=%async_computation | async-start | bytes 557056 | tf_op jit(solution)/shard_map/all_to_all | solution.py:463
  16.0 1.1 %shard_map.186 = (f32[2,256,128]{2,1,0:T(8,128)S(1)}, bf16[2,2,256,256]{3,2,1,0:T(8,128)(2,1)S(1)}, bf16[2,64,192]{2,1,0:T(8,128)(2,1)S(1)}, f32[2,32,128]{2,1,0:T(8,128)S(1)}) custom-call(s32[1]{0:T(128)} %bitcast.19.freq_ref, f32[1]{0:T(128)S(6)} %copy.30.slow_ref.refslow_ref, s32[1]{0:T(128)} %bitcast.5.lat_ref, ...), custom_call_target="tpu_custom_call" | custom-call | bytes 1474572 | tf_op jit(solution)/shard_map/pallas_call | solution.py:122
  17.1 9.4 %all-to-all-done = f32[32,1,2176]{2,1,0:T(1,128)S(1)} async-done(((f32[32,1,2176]{2,1,0:T(1,128)}), f32[32,1,2176]{2,1,0:T(1,128)S(1)}, u32[]{:S(2)}, u32[]{:S(2)}) %all-to-all-start) | async-done | bytes 278560 | tf_op jit(solution)/shard_map/all_to_all | solution.py:463
  26.6 1.8 %shard_map.187 = f32[576,128]{1,0:T(8,128)} custom-call(f32[544,128]{1,0:T(8,128)S(1)} %bitcast.23, f32[2,256,128]{2,1,0:T(8,128)S(1)} %get-tuple-element.23.phase_ref, bf16[2,2,256,256]{3,2,1,0:T(8,128)(2,1)S(1)} %get-tuple-element.24.x_ref, bf16[2,64,192]{2,1,0:T(8,128)(2,1)S(1)} %get-tuple-element.25.peers_ref, f32[2,32,128]{2,1,0:T(8,128)S(1)} %get-tuple-element.26.twist_ref), custom_call_target="tpu_custom_call" | custom-call | bytes 1441792 | tf_op jit(solution)/shard_map/pallas_call | solution.py:122
  28.4 4.6 %all-to-all-start.1 = ((f32[32,1,2304]{2,1,0:T(1,128)}), f32[32,1,2304]{2,1,0:T(1,128)S(1)}, u32[]{:S(2)}, u32[]{:S(2)}) async-start(f32[32,1,2304]{2,1,0:T(1,128)} %bitcast.7), calls=%async_computation.1 | async-start | bytes 589824 | tf_op jit(solution)/shard_map/all_to_all | solution.py:463
  33.0 0.0 copy-start.9
  33.0 0.7 %copy-done.9 = f32[16,2]{0,1:T(2,128)S(1)} copy-done((f32[16,2]{0,1:T(2,128)S(1)}, f32[16,2]{0,1:T(2,128)}, u32[]{:S(2)}) %copy-start.9) | copy-done | bytes 152
  33.7 0.1 copy.26
  33.8 0.1 reshape.45.coupling_ref
  33.9 0.0 copy-done.7
  33.9 0.2 copy.27
  34.1 0.0 copy-start.1
  34.1 0.0 copy-start.2
  34.1 0.0 copy-start.5
  34.1 0.1 pad_maximum_fusion
  34.2 0.0 copy-start.6
  34.2 0.8 %copy-done.1 = f32[1,32,1024]{2,1,0:T(8,128)S(1)} copy-done((f32[1,32,1024]{2,1,0:T(8,128)S(1)}, f32[1,32,1024]{2,1,0:T(8,128)}, u32[]{:S(2)}) %copy-start.1) | copy-done | bytes 131096
  35.0 0.0 copy-done.2
  35.0 0.0 copy-done.5
  35.0 0.0 copy-done.6
  35.0 0.0 copy-start.3
  35.0 1.8 %shard_map.188 = (f32[2,32,1024]{2,1,0:T(8,128)S(1)}, f32[8,1024]{1,0:T(8,128)S(1)}, bf16[2,8,64,256]{3,2,1,0:T(8,128)(2,1)S(1)}, bf16[2,8,64,256]{3,2,1,0:T(8,128)(2,1)S(1)}) custom-call(s32[1]{0:T(128)} %bitcast.20.freq_ref, f32[1]{0:T(128)S(6)} %copy.30.slow_ref.refslow_ref, s32[32]{0:T(128)S(1)} %bitcast.26, f32[32]{0:T(128)S(1)} %reshape.45.coupling_ref, ...), custom_call_target="tpu_custom_call" | custom-call | bytes 1810700 | tf_op jit(solution)/shard_map/pallas_call | solution.py:122
  36.8 0.0 copy-start.4
  36.8 7.1 %all-to-all-done.1 = f32[32,1,2304]{2,1,0:T(1,128)S(1)} async-done(((f32[32,1,2304]{2,1,0:T(1,128)}), f32[32,1,2304]{2,1,0:T(1,128)S(1)}, u32[]{:S(2)}, u32[]{:S(2)}) %all-to-all-start.1) | async-done | bytes 294944 | tf_op jit(solution)/shard_map/all_to_all | solution.py:463
  44.0 0.0 copy-done
  44.0 0.0 copy-start.8
  44.0 1.7 %shard_map.189 = (f32[2,32,1024]{2,1,0:T(8,128)S(1)}, f32[32,1024]{1,0:T(8,128)S(1)}) custom-call(f32[576,128]{1,0:T(8,128)S(1)} %bitcast.22, bf16[2,256,256]{2,1,0:T(8,128)(2,1)S(1)} %copy-done, f32[2,8,128]{2,1,0:T(8,128)S(1)} %copy-done.4, f32[2,32,1024]{2,1,0:T(8,128)S(1)} %get-tuple-element.32.lens_ref, f32[8,1024]{1,0:T(8,128)S(1)} %get-tuple-element.33.row_ref, ...), custom_call_target="tpu_custom_call" | custom-call | bytes 2662400 | tf_op jit(solution)/shard_map/pallas_call | solution.py:122
  45.7 5.0 %collective-permute-start = (f32[2,32,1024]{2,1,0:T(8,128)S(1)}, f32[2,32,1024]{2,1,0:T(8,128)S(1)}, u32[]{:S(2)}, u32[]{:S(2)}) collective-permute-start(f32[2,32,1024]{2,1,0:T(8,128)S(1)} %get-tuple-element.36), channel_id=1, source_target_pairs={{0,32},{32,64},{64,96},{96,128},{128,160},{160,192},{192,224},{224... | collective-permute-start | bytes 786440 | tf_op jit(solution)/shard_map/ppermute | solution.py:487
  50.8 0.7 %bitcast_add_fusion = f32[1,32,1024]{2,1,0:T(8,128)} fusion(f32[1,32,1024]{2,1,0:T(8,128)S(1)} %copy-done.8, f32[32,1024]{1,0:T(8,128)S(1)} %get-tuple-element.37), kind=kLoop, calls=%fused_computation.1 | loop fusion | flops 32768 | bytes 393216 | tf_op jit(solution)/shard_map/add | solution.py:488
  51.4 2.6 %collective-permute-done = f32[2,32,1024]{2,1,0:T(8,128)S(1)} collective-permute-done((f32[2,32,1024]{2,1,0:T(8,128)S(1)}, f32[2,32,1024]{2,1,0:T(8,128)S(1)}, u32[]{:S(2)}, u32[]{:S(2)}) %collective-permute-start) | collective-permute-done | bytes 262176 | tf_op jit(solution)/shard_map/ppermute | solution.py:487
  54.1 0.7 %copy.31 = f32[1,1,2,32,1024]{4,3,2,1,0:T(8,128)} copy(f32[1,1,2,32,1024]{4,3,2,1,0:T(8,128)S(1)} %bitcast.31) | data formatting | bytes 524288
  (5 shorter events, 0.0 us)
Async XLA Ops:
  2.9 23.7 %all-to-all-start = ((f32[32,1,2176]{2,1,0:T(1,128)}), f32[32,1,2176]{2,1,0:T(1,128)S(1)}, u32[]{:S(2)}, u32[]{:S(2)}) async-start(f32[32,1,2176]{2,1,0:T(1,128)} %bitcast.3), calls=%async_computation | async-start | bytes 557056 | tf_op jit(solution)/shard_map/all_to_all | solution.py:463
  28.4 5.5 %copy-start.7 = (f32[16,2,32,32]{3,2,1,0:T(8,128)S(1)}, f32[16,2,32,32]{3,2,1,0:T(8,128)}, u32[]{:S(2)}) copy-start(f32[16,2,32,32]{3,2,1,0:T(8,128)} %param.24) | copy-start | bytes 393220
  28.4 15.6 %all-to-all-start.1 = ((f32[32,1,2304]{2,1,0:T(1,128)}), f32[32,1,2304]{2,1,0:T(1,128)S(1)}, u32[]{:S(2)}, u32[]{:S(2)}) async-start(f32[32,1,2304]{2,1,0:T(1,128)} %bitcast.7), calls=%async_computation.1 | async-start | bytes 589824 | tf_op jit(solution)/shard_map/all_to_all | solution.py:463
  33.0 0.7 %copy-start.9 = (f32[16,2]{0,1:T(2,128)S(1)}, f32[16,2]{0,1:T(2,128)}, u32[]{:S(2)}) copy-start(f32[16,2]{0,1:T(2,128)} %param.25) | copy-start | bytes 388
  34.1 0.9 %copy-start.1 = (f32[1,32,1024]{2,1,0:T(8,128)S(1)}, f32[1,32,1024]{2,1,0:T(8,128)}, u32[]{:S(2)}) copy-start(f32[1,32,1024]{2,1,0:T(8,128)} %param.22) | copy-start | bytes 393220
  34.1 0.9 %copy-start.2 = (bf16[4,32,256]{2,1,0:T(8,128)(2,1)S(1)}, bf16[4,32,256]{2,1,0:T(8,128)(2,1)}, u32[]{:S(2)}) copy-start(bf16[4,32,256]{2,1,0:T(8,128)(2,1)} %constant.32.clone.own_ref) | copy-start | bytes 196612
  34.1 0.9 %copy-start.5 = (bf16[32,128]{1,0:T(8,128)(2,1)S(1)}, bf16[32,128]{1,0:T(8,128)(2,1)}, u32[]{:S(2)}) copy-start(bf16[32,128]{1,0:T(8,128)(2,1)} %constant.33.clone.spread_ref) | copy-start | bytes 24580
  34.2 0.8 %copy-start.6 = (s32[1,1,32]{2,1,0:T(1,128)S(1)}, s32[1,1,32]{2,1,0:T(1,128)}, u32[]{:S(2)}) copy-start(s32[1,1,32]{2,1,0:T(1,128)} %param.23) | copy-start | bytes 388
  35.0 9.0 %copy-start = (bf16[2,256,256]{2,1,0:T(8,128)(2,1)S(1)}, bf16[2,256,256]{2,1,0:T(8,128)(2,1)}, u32[]{:S(2)}) copy-start(bf16[2,256,256]{2,1,0:T(8,128)(2,1)} %constant.28.clone.w1_any.w3_ref) | copy-start | bytes 786436
  35.0 9.0 %copy-start.3 = (bf16[128,128]{1,0:T(8,128)(2,1)S(1)}, bf16[128,128]{1,0:T(8,128)(2,1)}, u32[]{:S(2)}) copy-start(bf16[128,128]{1,0:T(8,128)(2,1)} %constant.34.clone.fold_ref) | copy-start | bytes 98308
  36.8 7.1 %copy-start.4 = (f32[2,8,128]{2,1,0:T(8,128)S(1)}, f32[2,8,128]{2,1,0:T(8,128)}, u32[]{:S(2)}) copy-start(f32[2,8,128]{2,1,0:T(8,128)} %constant.27.clone.twist_any.twist_ref) | copy-start | bytes 24580
  44.0 6.8 %copy-start.8 = (f32[1,32,1024]{2,1,0:T(8,128)S(1)}, f32[1,32,1024]{2,1,0:T(8,128)}, u32[]{:S(2)}) copy-start(f32[1,32,1024]{2,1,0:T(8,128)} %param.26) | copy-start | bytes 393220
  45.7 8.4 %collective-permute-start = (f32[2,32,1024]{2,1,0:T(8,128)S(1)}, f32[2,32,1024]{2,1,0:T(8,128)S(1)}, u32[]{:S(2)}, u32[]{:S(2)}) collective-permute-start(f32[2,32,1024]{2,1,0:T(8,128)S(1)} %get-tuple-element.36), channel_id=1, source_target_pairs={{0,32},{32,64},{64,96},{96,128},{128,160},{160,192},{192,224},{224... | collective-permute-start | bytes 786440 | tf_op jit(solution)/shard_map/ppermute | solution.py:487

commit v5 on v4

--- a/solution.py
+++ b/solution.py
@@ -58,6 +58,7 @@
     own = (np.arange(128)[None, :] // 32 == np.arange(4)[:, None]).astype(np.float32)
     own = np.broadcast_to(np.tile(own, (1, 2))[:, None, :], (4, 32, 256)).astype(ml_dtypes.bfloat16)
     spread = np.tile(np.eye(32), (1, 4)).astype(ml_dtypes.bfloat16)
+    pick = np.einsum("gh,ab,t->gahtb", np.eye(4), np.eye(32), np.ones(4)).reshape(128, 512)
     return {
         "w1": parts(w1),
         "w3": parts(w3),
@@ -68,6 +69,7 @@
         "fold": fold,
         "own": own,
         "spread": spread,
+        "pick": pick.astype(ml_dtypes.bfloat16),
     }
 
 
@@ -194,17 +196,40 @@
     return jnp.cos(angle), jnp.sin(angle)
 
 
-def phases(freq_ref, slow_ref, lat_ref, x_any, peers_any, twist_any, out_ref, x_ref, peers_ref, twist_ref, sems):
-    copies = fetch([x_any, peers_any, twist_any], [x_ref, peers_ref, twist_ref], sems)
-    omega = 2.0 * math.pi * (LOW_HZ + STEP_HZ * freq_ref[0].astype(jnp.float32))
-    reach = omega * slow_ref[0]
+def prepare(
+    freq_ref, refslow_ref, lat_ref, last_ref, class_ref, coupling_ref,
+    blocks_any, slow_any, spread_any, pick_any, own_any, x_any, peers_any, twist_any,
+    phase_ref, lens_ref, row_ref, mx_ref, my_ref, own_ref, x_ref, peers_ref, twist_ref,
+    blocks_ref, slow_ref, spread_ref, pick_ref, wide_ref, sems,
+):
+    copies = fetch(
+        [blocks_any, spread_any, pick_any, own_any, slow_any, x_any, peers_any, twist_any],
+        [blocks_ref, spread_ref, pick_ref, own_ref, slow_ref, x_ref, peers_ref, twist_ref],
+        sems,
+    )
+    omega = 2.0 * math.pi * (LOW_HZ + STEP_HZ * freq_ref[0, 0].astype(jnp.float32))
+    base = refslow_ref[0]
+    phases(omega * base, lat_ref[0], phase_ref)
+    for copy in copies:
+        copy.wait()
+    for top in range(0, 32, 8):
+        rows = slice(top, top + 8)
+        cos, sin = sincos(omega * (slow_ref[rows] - base) * DEPTH_KM)
+        lens_ref[0, rows], lens_ref[1, rows] = cos * NORM, sin * NORM
+    row_ref[2:3] = jnp.full((1, N), omega)
+    row_ref[3:4] = jnp.full((1, N), base)
+    row_ref[4:5] = jnp.full((1, N), last_ref[0].astype(jnp.float32))
+    weights(class_ref, coupling_ref, blocks_ref, spread_ref, pick_ref, own_ref, row_ref, mx_ref, my_ref, wide_ref)
+
+
+def phases(reach, lat, out_ref):
     scale = 2.0 * math.pi / (N * SPACING_KM)
     for block in range(8):
         h, k2l = block // 4, block % 4
         q = lax.broadcasted_iota(jnp.int32, (32, 128), 0)
         lane = lax.broadcasted_iota(jnp.int32, (32, 128), 1)
         kx = q + 32 * (lane % 32)
-        ky = h * 4 + lane // 32 + 8 * (4 * lat_ref[0] + k2l)
+        ky = h * 4 + lane // 32 + 8 * (4 * lat + k2l)
         kx = jnp.where(kx < N // 2, kx, kx - N).astype(jnp.float32) * scale
         ky = jnp.where(ky < N // 2, ky, ky - N).astype(jnp.float32) * scale
         square = reach * reach - kx * kx - ky * ky
@@ -214,8 +239,6 @@
         cos, sin = sincos(angle)
         out_ref[0, block * 32 : block * 32 + 32] = amplitude * cos
         out_ref[1, block * 32 : block * 32 + 32] = amplitude * sin
-    for copy in copies:
-        copy.wait()
 
 
 def both_tiles(ref, rows):
@@ -279,30 +302,25 @@
     out_ref[pl.ds(17, LAT, stride=SECOND), :] = jnp.where(lane < 32, before, after)
 
 
-def weights(
-    freq_ref, refslow_ref, class_ref, coupling_ref, last_ref, slow_ref, blocks_ref, own_ref, spread_ref,
-    lens_ref, row_ref, mx_ref, my_ref, wide_ref,
-):
-    omega = 2.0 * math.pi * (LOW_HZ + STEP_HZ * freq_ref[0].astype(jnp.float32))
-    base = refslow_ref[0]
-    for top in range(0, 32, 8):
-        rows = slice(top, top + 8)
-        cos, sin = sincos(omega * (slow_ref[rows] - base) * DEPTH_KM)
-        lens_ref[0, rows], lens_ref[1, rows] = cos * NORM, sin * NORM
-    high, low = split(blocks_ref[...])
-    dot = lambda a: lax.dot_general(a, spread_ref[...], NN, preferred_element_type=jnp.float32)
-    wide_ref[0] = dot(high).astype(jnp.bfloat16).reshape(2, 16, 64, 128)
-    wide_ref[1] = dot(low).astype(jnp.bfloat16).reshape(2, 16, 64, 128)
-    row_ref[2:3] = jnp.full((1, N), omega)
-    row_ref[3:4] = jnp.full((1, N), base)
-    row_ref[4:5] = jnp.full((1, N), last_ref[0].astype(jnp.float32))
+def weights(class_ref, coupling_ref, blocks_ref, spread_ref, pick_ref, own_ref, row_ref, mx_ref, my_ref, wide_ref):
+    dot = lambda a, b, dims=NN: lax.dot_general(a, b, dims, preferred_element_type=jnp.float32).astype(jnp.bfloat16)
+    for part, values in enumerate(split(blocks_ref[...])):
+        wide_ref[part, 0] = dot(values, spread_ref[...]).reshape(16, 64, 128)
+        turned = dot(spread_ref[:, :32], values, NT)
+        turned = jnp.concatenate([turned[:, k * 128 : k * 128 + 128] for k in range(8)], axis=0)
+        turned = dot(turned, pick_ref[...])
+        for k in range(16):
+            for c in range(2):
+                m = k % 2 * 2 + c
+                piece = turned[k // 2 * 32 : k // 2 * 32 + 32, m * 128 : m * 128 + 128]
+                wide_ref[part, 1, k, c * 32 : c * 32 + 32] = piece
     lane = lax.broadcasted_iota(jnp.int32, (1, 128), 1) // 32
     for g in range(8):
-        classes = [class_ref[g * 4 + t] for t in range(4)]
+        classes = [class_ref[0, 0, g * 4 + t] for t in range(4)]
         for c in range(2):
-            beta = jnp.full((1, 128), coupling_ref[classes[0] * 2 + c])
+            beta = jnp.full((1, 128), coupling_ref[classes[0], c])
             for t in range(1, 4):
-                beta = jnp.where(lane == t, coupling_ref[classes[t] * 2 + c], beta)
+                beta = jnp.where(lane == t, coupling_ref[classes[t], c], beta)
             row_ref[c : c + 1, g * 128 : g * 128 + 128] = beta
         for part in range(2):
             total = []
@@ -431,30 +449,30 @@
     return call(forward_y, [shape(LAT * FIRST, 128)], scratch, args, large=(0, 1, 2, 3))[0]
 
 
-def phase_tables(freq, refslow, lat, t):
-    args = [freq, refslow, lat, t["x"], t["peers"], t["twist_x"]]
-    outs = [shape(2, 256, 128)] + [jax.ShapeDtypeStruct(a.shape, a.dtype) for a in args[3:]]
-    return call(phases, outs, [pltpu.SemaphoreType.DMA((3,))], args, scalars=(0, 1, 2), large=(3, 4, 5))
+def prepared(freq, refslow, lat, last, classes, coupling, blocks, slow, t):
+    half = jnp.bfloat16
+    tables = [t["spread"], t["pick"], t["own"], t["x"], t["peers"], t["twist_x"]]
+    args = [freq, refslow, lat, last, classes, coupling, blocks, slow, *tables]
+    outs = [shape(2, 256, 128), shape(2, 32, N), shape(8, N)] + [shape(2, 8, 64, 256, dtype=half)] * 2
+    outs += [jax.ShapeDtypeStruct(a.shape, a.dtype) for a in tables[2:]]
+    scratch = [pltpu.VMEM((1024, 32), jnp.float32), pltpu.VMEM((32, N), jnp.float32), pltpu.VMEM((32, 128), half)]
+    scratch += [pltpu.VMEM((128, 512), half), pltpu.VMEM((2, 2, 16, 64, 128), half), pltpu.SemaphoreType.DMA((8,))]
+    phase, lens, rows, mx, my, own, x, peers, twist = call(
+        prepare, outs, scratch, args, scalars=range(6), large=range(6, 14)
+    )
+    return [phase, x, peers, twist], [lens, rows, mx, my, own]
 
 
 def continue_x(block, tabs):
     scratch = [pltpu.VMEM((256, 256), jnp.bfloat16)] * 2 + [pltpu.VMEM((192, N), jnp.bfloat16)]
-    return call(along_x, [shape(LAT * SECOND, 128)], scratch, [block, *tabs])[0]
-
-
-def correction_tables(freq, refslow, classes, coupling, last, slow, blocks, t):
-    half = jnp.bfloat16
-    outs = [shape(2, 32, N), shape(8, N), shape(2, 8, 64, 256, dtype=half), shape(2, 8, 64, 256, dtype=half)]
-    scratch = [pltpu.VMEM((2, 2, 16, 64, 128), half)]
-    args = [freq, refslow, classes, coupling, last, slow, blocks, t["own"], t["spread"]]
-    return call(weights, outs, scratch, args, scalars=(0, 1, 2, 3, 4))
+    return call(along_x, [pltpu.VMEM((LAT * SECOND, 128), jnp.float32)], scratch, [block, *tabs])[0]
 
 
 def correct(block, tabs, fresh, t):
     plane = pltpu.VMEM((2, 32, N), jnp.float32)
     scratch = [pltpu.VMEM((320, 256), jnp.float32), pltpu.VMEM((2, 48, N), jnp.float32)]
     scratch += [plane, plane, plane, pltpu.SemaphoreType.DMA]
-    args = [block, t["w3"], t["twist_y"], *tabs, t["own"], t["fold"], fresh]
+    args = [block, t["w3"], t["twist_y"], *tabs, t["fold"], fresh]
     return call(finish, [shape(2, 32, N), shape(32, N)], scratch, args, large=(9,))
 
 
@@ -473,16 +491,14 @@
     t = tables()
     slow = slowness[0]
     block = spread_y(field.reshape(2, 32, N), slow, t)
-    block, (freq, refslow, blocks) = after(block, freq_index.reshape(1), ref_slowness, fd_blocks)
+    block, (blocks, slow) = after(block, fd_blocks.reshape(1024, 32), slow)
     received = exchange(block)
     lat = lax.axis_index("lat").reshape(1).astype(jnp.int32)
-    block = continue_x(received, phase_tables(freq, refslow, lat, t))
-    block, (freq, classes, slow) = after(block, freq, tile_classes.reshape(32), slow)
-    received = exchange(block)
     count = lax.axis_size("depth")
     last = (lax.axis_index("depth") == count - 1).reshape(1).astype(jnp.int32)
-    blocks = jnp.stack([blocks, jnp.swapaxes(blocks, 2, 3)]).reshape(2048, 32)
-    tabs = correction_tables(freq, refslow, classes, fd_coupling.reshape(32), last, slow, blocks, t)
+    phase, tabs = prepared(freq_index, ref_slowness, lat, last, tile_classes, fd_coupling, blocks, slow, t)
+    received, (phase, tabs) = after(received, phase, tabs)
+    received = exchange(continue_x(received, phase))
     result, real = correct(received, tabs, fresh[0], t)
     next_field = lax.ppermute(result, "depth", [(i, (i + 1) % count) for i in range(count)])
     return next_field[None, None], image + real[None]

time: 55.1 us -> 54.2 us (0.984)
  blocking collectives: 0 us -> 15.3 us
  waiting for transfers between devices: 19.2 us -> 8.86 us
  starting transfers between devices: 21.5 us -> 16.9 us
  local copies, waits for them, and re-layouts: 2.55 us -> 1.48 us
    all_to_all x0 -> x1, blocking collectives: none -> 15.3 us  [exchange(): lax.all_to_all(blocks, 'lat', split_axis=0, concat_axis=0, tiled=True)]
    all_to_all x2 -> x1, waiting for transfers between devices: 16.6 us -> 6.22 us  [exchange(): lax.all_to_all(blocks, 'lat', split_axis=0, concat_axis=0, tiled=True)]
    all_to_all x2 -> x1, starting transfers between devices: 16.5 us -> 11.9 us  [exchange(): lax.all_to_all(blocks, 'lat', split_axis=0, concat_axis=0, tiled=True)]
    unnamed x22 -> x14, local copies, waits for them, and re-layouts: 2.27 us -> 1.48 us
    pallas_call x5 -> x4, Pallas kernels: 8.65 us -> 8.59 us  [call(): pl.pallas_call(body, out_shape=outs, in_specs=[pl.BlockSpec(memory_space=...]
  transfers between devices with their start and end apart: 3 -> 2, of which waited for: 3 -> 2; matrix products, arithmetic and copies ran while one was open for 2% -> 1% of each run, Pallas kernels for 5% -> 7%
where the time goes in v5:
time: 54.2 us; the launch traced here: 53.9 us
  starting transfers between devices  16.9 us (31%)
  blocking collectives  15.3 us (28%)
  waiting for transfers between devices  8.86 us (16%)
  Pallas kernels  8.59 us (16%)
  between operations  2.03 us (4%)
  local copies, waits for them, and re-layouts  1.48 us (3%)
  other arithmetic  0.67 us (1%)
    all_to_all x1, blocking collectives, exchange(): lax.all_to_all(blocks, 'lat', split_axis=0, concat_axis=0, tiled=True)  15.3 us
    all_to_all x1, starting transfers between devices, exchange(): lax.all_to_all(blocks, 'lat', split_axis=0, concat_axis=0, tiled=True)  11.9 us
    pallas_call x4, Pallas kernels, call(): pl.pallas_call(body, out_shape=outs, in_specs=[pl.BlockSpec(memory_space=...  8.59 us
    all_to_all x1, waiting for transfers between devices, exchange(): lax.all_to_all(blocks, 'lat', split_axis=0, concat_axis=0, tiled=True)  6.22 us
    ppermute x1, starting transfers between devices, per_device(): lax.ppermute(result, 'depth', [(i, (i + 1) % count) for i in range(count)])  5.05 us
    ppermute x1, waiting for transfers between devices, per_device(): lax.ppermute(result, 'depth', [(i, (i + 1) % count) for i in range(count)])  2.64 us
    unnamed x14, local copies, waits for them, and re-layouts  1.48 us
  transfers between devices with their start and end apart: 2, of which 2 were waited for; matrix products, arithmetic and copies ran while one was open for 1% of the time, Pallas kernels for 7%

profile of v5, /device:TPU:1, one launch (start us, length us, event | category | flops | bytes accessed | tf_op | source)
XLA Modules:
  0.0 53.9 jit_solution(14344336301732018656)
XLA Ops:
  0.6 2.2 %shard_map.194 = f32[544,128]{1,0:T(8,128)} custom-call(f32[2,32,1024]{2,1,0:T(8,128)} %bitcast.19, f32[2,8,128]{2,1,0:T(8,128)} %constant.29.clone.twist_any.twist_ref, bf16[2,256,256]{2,1,0:T(8,128)(2,1)} %constant.30.clone.w1_any.w3_ref, f32[32,1024]{1,0:T(8,128)} %bitcast.17), custom_call_target="tpu_custom_call" | custom-call | bytes 942080 | tf_op jit(solution)/shard_map/pallas_call | solution.py:124
  2.9 11.9 %all-to-all-start = ((f32[32,1,2176]{2,1,0:T(1,128)}), f32[32,1,2176]{2,1,0:T(1,128)S(1)}, u32[]{:S(2)}, u32[]{:S(2)}) async-start(f32[32,1,2176]{2,1,0:T(1,128)} %bitcast.3), calls=%async_computation | async-start | bytes 557056 | tf_op jit(solution)/shard_map/all_to_all | solution.py:481
  15.4 0.0 copy-start.5
  16.1 0.0 copy-done.5
  16.1 0.1 copy.23.coupling_ref
  16.2 0.0 copy-start.3
  16.2 0.7 %copy-done.3 = s32[1,1,32]{2,1,0:T(1,128)S(1)} copy-done((s32[1,1,32]{2,1,0:T(1,128)S(1)}, s32[1,1,32]{2,1,0:T(1,128)}, u32[]{:S(2)}) %copy-start.3) | copy-done | bytes 152
  16.8 3.5 %shard_map.195 = (f32[2,256,128]{2,1,0:T(8,128)S(1)}, f32[2,32,1024]{2,1,0:T(8,128)S(1)}, f32[8,1024]{1,0:T(8,128)S(1)}, bf16[2,8,64,256]{3,2,1,0:T(8,128)(2,1)S...) custom-call(s32[1,1]{1,0:T(1,128)S(6)} %copy.26.freq_ref, ...), custom_call_target="tpu_custom_call" | custom-call | bytes 3350800 | tf_op jit(solution)/shard_map/pallas_call | solution.py:124
  20.4 6.2 %all-to-all-done = f32[32,1,2176]{2,1,0:T(1,128)S(1)} async-done(((f32[32,1,2176]{2,1,0:T(1,128)}), f32[32,1,2176]{2,1,0:T(1,128)S(1)}, u32[]{:S(2)}, u32[]{:S(2)}) %all-to-all-start) | async-done | bytes 278560 | tf_op jit(solution)/shard_map/all_to_all | solution.py:481
  26.6 1.1 %shard_map.196 = f32[576,128]{1,0:T(8,128)S(1)} custom-call(f32[544,128]{1,0:T(8,128)S(1)} %bitcast.15, f32[2,256,128]{2,1,0:T(8,128)S(1)} %get-tuple-element.39.phase_ref, bf16[2,2,256,256]{3,2,1,0:T(8,128)(2,1)S(1)} %get-tuple-element.40.x_ref, bf16[2,64,192]{2,1,0:T(8,128)(2,1)S(1)} %get-tuple-element.41.peers_ref, ...), custom_call_target="tpu_custom_call" | custom-call | bytes 1441792 | tf_op jit(solution)/shard_map/pallas_call | solution.py:124
  27.7 0.0 copy-start
  27.7 0.0 copy-start.1
  27.7 0.0 copy-start.2
  27.7 15.3 %all_to_all.10 = f32[32,1,2304]{2,1,0:T(1,128)S(1)} all-to-all(f32[32,1,2304]{2,1,0:T(1,128)S(1)} %bitcast.14), channel_id=1, replica_groups=mesh['depth'=8,'lat'=32] {'lat'}, dimensions={0} | all-to-all | bytes 589824 | tf_op jit(solution)/shard_map/all_to_all | solution.py:481
  43.1 0.0 copy-done
  43.1 0.0 copy-done.1
  43.1 0.0 copy-done.2
  43.1 0.0 copy-start.4
  43.1 1.7 %shard_map.197 = (f32[2,32,1024]{2,1,0:T(8,128)S(1)}, f32[32,1024]{1,0:T(8,128)S(1)}) custom-call(f32[576,128]{1,0:T(8,128)S(1)} %bitcast.13, bf16[2,256,256]{2,1,0:T(8,128)(2,1)S(1)} %copy-done, f32[2,8,128]{2,1,0:T(8,128)S(1)} %copy-done.2, f32[2,32,1024]{2,1,0:T(8,128)S(1)} %get-tuple-element.43.lens_ref, f32[8,1024]{1,0:T(8,128)S(1)} %get-tuple-element.44.row_ref, ...), custom_call_target="tpu_custom_call" | custom-call | bytes 2662400 | tf_op jit(solution)/shard_map/pallas_call | solution.py:124
  44.8 5.1 %collective-permute-start = (f32[2,32,1024]{2,1,0:T(8,128)S(1)}, f32[2,32,1024]{2,1,0:T(8,128)S(1)}, u32[]{:S(2)}, u32[]{:S(2)}) collective-permute-start(f32[2,32,1024]{2,1,0:T(8,128)S(1)} %get-tuple-element.48), channel_id=1, source_target_pairs={{0,32},{32,64},{64,96},{96,128},{128,160},{160,192},{192,224},{224... | collective-permute-start | bytes 786440 | tf_op jit(solution)/shard_map/ppermute | solution.py:503
  49.9 0.0 copy-done.4
  49.9 0.7 %bitcast_add_fusion = f32[1,32,1024]{2,1,0:T(8,128)} fusion(f32[1,32,1024]{2,1,0:T(8,128)S(1)} %copy-done.4, f32[32,1024]{1,0:T(8,128)S(1)} %get-tuple-element.49), kind=kLoop, calls=%fused_computation | loop fusion | flops 32768 | bytes 393216 | tf_op jit(solution)/shard_map/add | solution.py:504
  50.6 2.6 %collective-permute-done = f32[2,32,1024]{2,1,0:T(8,128)S(1)} collective-permute-done((f32[2,32,1024]{2,1,0:T(8,128)S(1)}, f32[2,32,1024]{2,1,0:T(8,128)S(1)}, u32[]{:S(2)}, u32[]{:S(2)}) %collective-permute-start) | collective-permute-done | bytes 262176 | tf_op jit(solution)/shard_map/ppermute | solution.py:503
  53.2 0.7 %copy.28 = f32[1,1,2,32,1024]{4,3,2,1,0:T(8,128)} copy(f32[1,1,2,32,1024]{4,3,2,1,0:T(8,128)S(1)} %bitcast.21) | data formatting | bytes 524288
Async XLA Ops:
  2.9 23.7 %all-to-all-start = ((f32[32,1,2176]{2,1,0:T(1,128)}), f32[32,1,2176]{2,1,0:T(1,128)S(1)}, u32[]{:S(2)}, u32[]{:S(2)}) async-start(f32[32,1,2176]{2,1,0:T(1,128)} %bitcast.3), calls=%async_computation | async-start | bytes 557056 | tf_op jit(solution)/shard_map/all_to_all | solution.py:481
  15.4 0.7 %copy-start.5 = (f32[16,2]{0,1:T(2,128)S(1)}, f32[16,2]{0,1:T(2,128)}, u32[]{:S(2)}) copy-start(f32[16,2]{0,1:T(2,128)} %param.26) | copy-start | bytes 388
  16.2 0.7 %copy-start.3 = (s32[1,1,32]{2,1,0:T(1,128)S(1)}, s32[1,1,32]{2,1,0:T(1,128)}, u32[]{:S(2)}) copy-start(s32[1,1,32]{2,1,0:T(1,128)} %class_ref.1) | copy-start | bytes 388
  27.7 15.4 %copy-start = (bf16[2,256,256]{2,1,0:T(8,128)(2,1)S(1)}, bf16[2,256,256]{2,1,0:T(8,128)(2,1)}, u32[]{:S(2)}) copy-start(bf16[2,256,256]{2,1,0:T(8,128)(2,1)} %constant.30.clone.w1_any.w3_ref) | copy-start | bytes 786436
  27.7 15.4 %copy-start.1 = (bf16[128,128]{1,0:T(8,128)(2,1)S(1)}, bf16[128,128]{1,0:T(8,128)(2,1)}, u32[]{:S(2)}) copy-start(bf16[128,128]{1,0:T(8,128)(2,1)} %constant.37.clone.fold_ref) | copy-start | bytes 98308
  27.7 15.4 %copy-start.2 = (f32[2,8,128]{2,1,0:T(8,128)S(1)}, f32[2,8,128]{2,1,0:T(8,128)}, u32[]{:S(2)}) copy-start(f32[2,8,128]{2,1,0:T(8,128)} %constant.29.clone.twist_any.twist_ref) | copy-start | bytes 24580
  43.1 6.8 %copy-start.4 = (f32[1,32,1024]{2,1,0:T(8,128)S(1)}, f32[1,32,1024]{2,1,0:T(8,128)}, u32[]{:S(2)}) copy-start(f32[1,32,1024]{2,1,0:T(8,128)} %param.27) | copy-start | bytes 393220
  44.8 8.4 %collective-permute-start = (f32[2,32,1024]{2,1,0:T(8,128)S(1)}, f32[2,32,1024]{2,1,0:T(8,128)S(1)}, u32[]{:S(2)}, u32[]{:S(2)}) collective-permute-start(f32[2,32,1024]{2,1,0:T(8,128)S(1)} %get-tuple-element.48), channel_id=1, source_target_pairs={{0,32},{32,64},{64,96},{96,128},{128,160},{160,192},{192,224},{224... | collective-permute-start | bytes 786440 | tf_op jit(solution)/shard_map/ppermute | solution.py:503

commit v6 on v5

--- a/solution.py
+++ b/solution.py
@@ -50,11 +50,6 @@
     tx = np.tile(2 * np.pi * small[:, None] * small / N, (1, 4))
     twist_y = np.stack([np.cos(ty), np.sin(ty)]).astype(np.float32)
     twist_x = np.stack([np.cos(tx), np.sin(tx)]).astype(np.float32)
-    fold = np.zeros((4, 8, 2, 2, 16, 8))
-    for k1 in range(8):
-        for side in range(2):
-            fold[k1 % 4, :, k1 // 4, side, k1, side] = 1
-    fold = fold.reshape(128, 128).astype(ml_dtypes.bfloat16)
     own = (np.arange(128)[None, :] // 32 == np.arange(4)[:, None]).astype(np.float32)
     own = np.broadcast_to(np.tile(own, (1, 2))[:, None, :], (4, 32, 256)).astype(ml_dtypes.bfloat16)
     spread = np.tile(np.eye(32), (1, 4)).astype(ml_dtypes.bfloat16)
@@ -66,7 +61,6 @@
         "peers": np.stack(peers),
         "twist_y": twist_y,
         "twist_x": twist_x,
-        "fold": fold,
         "own": own,
         "spread": spread,
         "pick": pick.astype(ml_dtypes.bfloat16),
@@ -185,11 +179,13 @@
         last = pltpu.roll(ends_ref[1], (32 - 32 * m) % 128, 1)
         out_ref[pl.ds(FIRST * m + 16, 8, stride=4 * FIRST), :] = jnp.where(lane < 32, first, last)
     copies[4].wait()
-    out = product((w1_ref[0], w1_ref[1]), (high_ref[...], low_ref[...]), NT)
-    for j in range(LAT):
-        for half in range(2):
-            top = FIRST * j + half * 8
-            out_ref[top : top + 8] = out[j * 8 : j * 8 + 8, half * 128 : half * 128 + 128]
+    for first in range(0, LAT, 16):
+        rows = slice(first * 8, first * 8 + 128)
+        out = product((w1_ref[0, rows], w1_ref[1, rows]), (high_ref[...], low_ref[...]), NT)
+        for j in range(16):
+            for half in range(2):
+                top = FIRST * (first + j) + half * 8
+                out_ref[top : top + 8] = out[j * 8 : j * 8 + 8, half * 128 : half * 128 + 128]
 
 
 def sincos(angle):
@@ -267,22 +263,25 @@
             high_ref[at, c * 128 : c * 128 + 128] = high
             low_ref[at, c * 128 : c * 128 + 128] = low
 
-    for block in range(8):
-        lanes = slice(block * 128, block * 128 + 128)
-        put(slice(block * 32, block * 32 + 32), cmul((mixed[:32, lanes], mixed[32:, lanes]), (cos, -sin)))
-    spectrum = product((high_ref[...], low_ref[...]), (x_ref[0, 0], x_ref[0, 1]))
-    for block in range(8):
-        rows = slice(block * 32, block * 32 + 32)
-        value = (spectrum[rows, :128], spectrum[rows, 128:])
-        put(rows, cmul(value, (phase_ref[0, rows], phase_ref[1, rows])))
-    mixed = product((high_ref[...], low_ref[...]), (x_ref[1, 0], x_ref[1, 1]))
-    for block in range(8):
-        rows, lanes = slice(block * 32, block * 32 + 32), slice(block * 128, block * 128 + 128)
-        value = cmul((mixed[rows, :128], mixed[rows, 128:]), (cos, sin))
-        for c in range(2):
-            high, low = split(value[c])
-            for at, piece in enumerate((high, low, high)):
-                back_ref[at * 64 + c * 32 : at * 64 + c * 32 + 32, lanes] = piece
+    for half in range(2):
+        some = range(half * 4, half * 4 + 4)
+        whole = slice(half * 128, half * 128 + 128)
+        for block in some:
+            lanes = slice(block * 128, block * 128 + 128)
+            put(slice(block * 32, block * 32 + 32), cmul((mixed[:32, lanes], mixed[32:, lanes]), (cos, -sin)))
+        spectrum = product((high_ref[whole], low_ref[whole]), (x_ref[0, 0], x_ref[0, 1]))
+        for block in some:
+            rows, at = slice(block * 32, block * 32 + 32), block % 4 * 32
+            value = (spectrum[at : at + 32, :128], spectrum[at : at + 32, 128:])
+            put(rows, cmul(value, (phase_ref[0, rows], phase_ref[1, rows])))
+        back = product((high_ref[whole], low_ref[whole]), (x_ref[1, 0], x_ref[1, 1]))
+        for block in some:
+            at, lanes = block % 4 * 32, slice(block * 128, block * 128 + 128)
+            value = cmul((back[at : at + 32, :128], back[at : at + 32, 128:]), (cos, sin))
+            for c in range(2):
+                high, low = split(value[c])
+                for part, piece in enumerate((high, low, high)):
+                    back_ref[part * 64 + c * 32 : part * 64 + c * 32 + 32, lanes] = piece
     out = dot(peers_ref[1], back_ref[...])
     lane, row = lane_of((LAT, 128)), lax.broadcasted_iota(jnp.int32, (LAT, 128), 0)
     edge = jnp.zeros((LAT, 128), jnp.float32)
@@ -341,7 +340,7 @@
 
 
 def finish(
-    in_ref, w3_ref, twist_ref, lens_ref, row_ref, mx_ref, my_ref, own_ref, fold_ref, fresh_any,
+    in_ref, w3_ref, twist_ref, lens_ref, row_ref, mx_ref, my_ref, own_ref, fresh_any,
     out_ref, real_ref, mixed_ref, lensed_ref, rhs_ref, across_ref, fresh_ref, sem,
 ):
     copy = pltpu.make_async_copy(fresh_any, fresh_ref, sem)
@@ -361,16 +360,26 @@
         [jnp.broadcast_to(in_ref[SECOND * j + 16 : SECOND * j + 17], (8, 128)) for j in range(LAT)], axis=0
     )
     own = lane_of((256, 128)) % 32 // 4 == lax.broadcasted_iota(jnp.int32, (256, 128), 0) % 8
-    high, low = split(jnp.where(own, beside, 0.0))
-    dot = lambda a: lax.dot_general(a, fold_ref[...], NN, preferred_element_type=jnp.float32)
-    lines = [*both_tiles(in_ref, SECOND), dot(high) + dot(low)]
-    turned = jnp.concatenate([line.T for line in lines], axis=0)[:320]
-    mixed_ref[...] = product(split(turned), (w3_ref[0], w3_ref[1]))
+    turned = jnp.concatenate([line.T for line in both_tiles(in_ref, SECOND)], axis=0)
+    mixed_ref[:256] = product(split(turned), (w3_ref[0], w3_ref[1]))
+    mixed_ref[256:384] = product(split(jnp.where(own, beside, 0.0).T), (w3_ref[0], w3_ref[1]))
+    halos = []
+    for k1l in range(4):
+        top = 256 + k1l * 32
+        total = [
+            (mixed_ref[top : top + 8, c] + mixed_ref[top + 8 : top + 16, c])
+            + (mixed_ref[top + 16 : top + 24, c] + mixed_ref[top + 24 : top + 32, c])
+            for c in (slice(0, 128), slice(128, 256))
+        ]
+        halos.append([part + pltpu.roll(part, 4, 0) for part in total])
     for block in range(5):
         values = []
         for k1 in range(8):
-            top = k1 * 32 + block * 8 if block < 4 else 256 + k1 * 8
-            value = (mixed_ref[top : top + 8, :128], mixed_ref[top : top + 8, 128:])
+            top = k1 * 32 + block * 8
+            if block < 4:
+                value = (mixed_ref[top : top + 8, :128], mixed_ref[top : top + 8, 128:])
+            else:
+                value = halos[k1 % 4] if k1 < 4 else [pltpu.roll(part, 6, 0) for part in halos[k1 % 4]]
             if k1:
                 value = cmul(value, (twist_ref[0, k1 : k1 + 1], twist_ref[1, k1 : k1 + 1]))
             values.append(value)
@@ -470,10 +479,10 @@
 
 def correct(block, tabs, fresh, t):
     plane = pltpu.VMEM((2, 32, N), jnp.float32)
-    scratch = [pltpu.VMEM((320, 256), jnp.float32), pltpu.VMEM((2, 48, N), jnp.float32)]
+    scratch = [pltpu.VMEM((384, 256), jnp.float32), pltpu.VMEM((2, 48, N), jnp.float32)]
     scratch += [plane, plane, plane, pltpu.SemaphoreType.DMA]
-    args = [block, t["w3"], t["twist_y"], *tabs, t["fold"], fresh]
-    return call(finish, [shape(2, 32, N), shape(32, N)], scratch, args, large=(9,))
+    args = [block, t["w3"], t["twist_y"], *tabs, fresh]
+    return call(finish, [shape(2, 32, N), shape(32, N)], scratch, args, large=(8,))
 
 
 def exchange(block):

time: 54.2 us -> 53.8 us (level)
    unnamed x14 -> x12, local copies, waits for them, and re-layouts: 1.48 us -> 1.47 us
where the time goes in v6:
time: 53.8 us; the launch traced here: 53.5 us
  starting transfers between devices  16.9 us (31%)
  blocking collectives  15.3 us (28%)
  waiting for transfers between devices  8.87 us (16%)
  Pallas kernels  8.24 us (15%)
  between operations  2.01 us (4%)
  local copies, waits for them, and re-layouts  1.47 us (3%)
  other arithmetic  0.67 us (1%)
    all_to_all x1, blocking collectives, exchange(): lax.all_to_all(blocks, 'lat', split_axis=0, concat_axis=0, tiled=True)  15.3 us
    all_to_all x1, starting transfers between devices, exchange(): lax.all_to_all(blocks, 'lat', split_axis=0, concat_axis=0, tiled=True)  11.9 us
    pallas_call x4, Pallas kernels, call(): pl.pallas_call(body, out_shape=outs, in_specs=[pl.BlockSpec(memory_space=...  8.24 us
    all_to_all x1, waiting for transfers between devices, exchange(): lax.all_to_all(blocks, 'lat', split_axis=0, concat_axis=0, tiled=True)  6.23 us
    ppermute x1, starting transfers between devices, per_device(): lax.ppermute(result, 'depth', [(i, (i + 1) % count) for i in range(count)])  5.05 us
    ppermute x1, waiting for transfers between devices, per_device(): lax.ppermute(result, 'depth', [(i, (i + 1) % count) for i in range(count)])  2.64 us
    unnamed x12, local copies, waits for them, and re-layouts  1.47 us
  transfers between devices with their start and end apart: 2, of which 2 were waited for; matrix products, arithmetic and copies ran while one was open for 1% of the time, Pallas kernels for 7%

profile of v6, /device:TPU:1, one launch (start us, length us, event | category | flops | bytes accessed | tf_op | source)
XLA Modules:
  0.0 53.5 jit_solution(17405370512695600302)
XLA Ops:
  0.6 2.2 %shard_map.185 = f32[544,128]{1,0:T(8,128)} custom-call(f32[2,32,1024]{2,1,0:T(8,128)} %bitcast.19, f32[2,8,128]{2,1,0:T(8,128)} %constant.27.clone.twist_any.twist_ref, bf16[2,256,256]{2,1,0:T(8,128)(2,1)} %constant.28.clone.w1_any.w3_ref, f32[32,1024]{1,0:T(8,128)} %bitcast.17), custom_call_target="tpu_custom_call" | custom-call | bytes 942080 | tf_op jit(solution)/shard_map/pallas_call | solution.py:118
  2.8 11.9 %all-to-all-start = ((f32[32,1,2176]{2,1,0:T(1,128)}), f32[32,1,2176]{2,1,0:T(1,128)S(1)}, u32[]{:S(2)}, u32[]{:S(2)}) async-start(f32[32,1,2176]{2,1,0:T(1,128)} %bitcast.3), calls=%async_computation | async-start | bytes 557056 | tf_op jit(solution)/shard_map/all_to_all | solution.py:490
  15.4 0.0 copy-start.4
  16.1 0.0 copy-done.4
  16.1 0.1 copy.22.coupling_ref
  16.1 0.0 copy-start.2
  16.1 0.7 %copy-done.2 = s32[1,1,32]{2,1,0:T(1,128)S(1)} copy-done((s32[1,1,32]{2,1,0:T(1,128)S(1)}, s32[1,1,32]{2,1,0:T(1,128)}, u32[]{:S(2)}) %copy-start.2) | copy-done | bytes 152
  16.8 3.5 %shard_map.186 = (f32[2,256,128]{2,1,0:T(8,128)S(1)}, f32[2,32,1024]{2,1,0:T(8,128)S(1)}, f32[8,1024]{1,0:T(8,128)S(1)}, bf16[2,8,64,256]{3,2,1,0:T(8,128)(2,1)S...) custom-call(s32[1,1]{1,0:T(1,128)S(6)} %copy.25.freq_ref, ...), custom_call_target="tpu_custom_call" | custom-call | bytes 3350800 | tf_op jit(solution)/shard_map/pallas_call | solution.py:118
  20.3 6.2 %all-to-all-done = f32[32,1,2176]{2,1,0:T(1,128)S(1)} async-done(((f32[32,1,2176]{2,1,0:T(1,128)}), f32[32,1,2176]{2,1,0:T(1,128)S(1)}, u32[]{:S(2)}, u32[]{:S(2)}) %all-to-all-start) | async-done | bytes 278560 | tf_op jit(solution)/shard_map/all_to_all | solution.py:490
  26.6 1.0 %shard_map.187 = f32[576,128]{1,0:T(8,128)S(1)} custom-call(f32[544,128]{1,0:T(8,128)S(1)} %bitcast.15, f32[2,256,128]{2,1,0:T(8,128)S(1)} %get-tuple-element.39.phase_ref, bf16[2,2,256,256]{3,2,1,0:T(8,128)(2,1)S(1)} %get-tuple-element.40.x_ref, bf16[2,64,192]{2,1,0:T(8,128)(2,1)S(1)} %get-tuple-element.41.peers_ref, ...), custom_call_target="tpu_custom_call" | custom-call | bytes 1441792 | tf_op jit(solution)/shard_map/pallas_call | solution.py:118
  27.6 0.0 copy-start
  27.6 0.0 copy-start.1
  27.6 15.3 %all_to_all.10 = f32[32,1,2304]{2,1,0:T(1,128)S(1)} all-to-all(f32[32,1,2304]{2,1,0:T(1,128)S(1)} %bitcast.14), channel_id=1, replica_groups=mesh['depth'=8,'lat'=32] {'lat'}, dimensions={0} | all-to-all | bytes 589824 | tf_op jit(solution)/shard_map/all_to_all | solution.py:490
  42.9 0.0 copy-done
  42.9 0.0 copy-done.1
  42.9 0.0 copy-start.3
  42.9 1.5 %shard_map.188 = (f32[2,32,1024]{2,1,0:T(8,128)S(1)}, f32[32,1024]{1,0:T(8,128)S(1)}) custom-call(f32[576,128]{1,0:T(8,128)S(1)} %bitcast.13, bf16[2,256,256]{2,1,0:T(8,128)(2,1)S(1)} %copy-done, f32[2,8,128]{2,1,0:T(8,128)S(1)} %copy-done.1, f32[2,32,1024]{2,1,0:T(8,128)S(1)} %get-tuple-element.43.lens_ref, f32[8,1024]{1,0:T(8,128)S(1)} %get-tuple-element.44.row_ref, ...), custom_call_target="tpu_custom_call" | custom-call | bytes 2629632 | tf_op jit(solution)/shard_map/pallas_call | solution.py:118
  44.4 5.1 %collective-permute-start = (f32[2,32,1024]{2,1,0:T(8,128)S(1)}, f32[2,32,1024]{2,1,0:T(8,128)S(1)}, u32[]{:S(2)}, u32[]{:S(2)}) collective-permute-start(f32[2,32,1024]{2,1,0:T(8,128)S(1)} %get-tuple-element.48), channel_id=1, source_target_pairs={{0,32},{32,64},{64,96},{96,128},{128,160},{160,192},{192,224},{224... | collective-permute-start | bytes 786440 | tf_op jit(solution)/shard_map/ppermute | solution.py:512
  49.5 0.0 copy-done.3
  49.5 0.7 %bitcast_add_fusion = f32[1,32,1024]{2,1,0:T(8,128)} fusion(f32[1,32,1024]{2,1,0:T(8,128)S(1)} %copy-done.3, f32[32,1024]{1,0:T(8,128)S(1)} %get-tuple-element.49), kind=kLoop, calls=%fused_computation | loop fusion | flops 32768 | bytes 393216 | tf_op jit(solution)/shard_map/add | solution.py:513
  50.2 2.6 %collective-permute-done = f32[2,32,1024]{2,1,0:T(8,128)S(1)} collective-permute-done((f32[2,32,1024]{2,1,0:T(8,128)S(1)}, f32[2,32,1024]{2,1,0:T(8,128)S(1)}, u32[]{:S(2)}, u32[]{:S(2)}) %collective-permute-start) | collective-permute-done | bytes 262176 | tf_op jit(solution)/shard_map/ppermute | solution.py:512
  52.8 0.7 %copy.27 = f32[1,1,2,32,1024]{4,3,2,1,0:T(8,128)} copy(f32[1,1,2,32,1024]{4,3,2,1,0:T(8,128)S(1)} %bitcast.21) | data formatting | bytes 524288
Async XLA Ops:
  2.8 23.7 %all-to-all-start = ((f32[32,1,2176]{2,1,0:T(1,128)}), f32[32,1,2176]{2,1,0:T(1,128)S(1)}, u32[]{:S(2)}, u32[]{:S(2)}) async-start(f32[32,1,2176]{2,1,0:T(1,128)} %bitcast.3), calls=%async_computation | async-start | bytes 557056 | tf_op jit(solution)/shard_map/all_to_all | solution.py:490
  15.4 0.7 %copy-start.4 = (f32[16,2]{0,1:T(2,128)S(1)}, f32[16,2]{0,1:T(2,128)}, u32[]{:S(2)}) copy-start(f32[16,2]{0,1:T(2,128)} %param.25) | copy-start | bytes 388
  16.1 0.7 %copy-start.2 = (s32[1,1,32]{2,1,0:T(1,128)S(1)}, s32[1,1,32]{2,1,0:T(1,128)}, u32[]{:S(2)}) copy-start(s32[1,1,32]{2,1,0:T(1,128)} %class_ref.1) | copy-start | bytes 388
  27.6 15.4 %copy-start = (bf16[2,256,256]{2,1,0:T(8,128)(2,1)S(1)}, bf16[2,256,256]{2,1,0:T(8,128)(2,1)}, u32[]{:S(2)}) copy-start(bf16[2,256,256]{2,1,0:T(8,128)(2,1)} %constant.28.clone.w1_any.w3_ref) | copy-start | bytes 786436
  27.6 15.3 %copy-start.1 = (f32[2,8,128]{2,1,0:T(8,128)S(1)}, f32[2,8,128]{2,1,0:T(8,128)}, u32[]{:S(2)}) copy-start(f32[2,8,128]{2,1,0:T(8,128)} %constant.27.clone.twist_any.twist_ref) | copy-start | bytes 24580
  42.9 6.6 %copy-start.3 = (f32[1,32,1024]{2,1,0:T(8,128)S(1)}, f32[1,32,1024]{2,1,0:T(8,128)}, u32[]{:S(2)}) copy-start(f32[1,32,1024]{2,1,0:T(8,128)} %param.26) | copy-start | bytes 393220
  44.4 8.4 %collective-permute-start = (f32[2,32,1024]{2,1,0:T(8,128)S(1)}, f32[2,32,1024]{2,1,0:T(8,128)S(1)}, u32[]{:S(2)}, u32[]{:S(2)}) collective-permute-start(f32[2,32,1024]{2,1,0:T(8,128)S(1)} %get-tuple-element.48), channel_id=1, source_target_pairs={{0,32},{32,64},{64,96},{96,128},{128,160},{160,192},{192,224},{224... | collective-permute-start | bytes 786440 | tf_op jit(solution)/shard_map/ppermute | solution.py:512
